TPU v7x, 32 devices: a whole 2x2x4 slice. The times are simulated.
32 devices in a mesh: wide: 4 (over y, x), narrow: 8 (over z, core).
Axes of the slice: x: 2, y: 2, z: 4, core: 2. Of those that a mesh axis runs over, the one named last changes fastest.
Arguments:
- images: bfloat16 [64, 256, 1024], P('wide', 'narrow'), may hold values from -6 to 6
- cotangent: bfloat16 [64, 256, 1024], P('wide', 'narrow'), may hold values from -12 to 12
- test_images: bfloat16 [4, 256, 1024], P('wide', 'narrow'), may hold values from -6 to 6
- test_cotangent: bfloat16 [4, 256, 1024], P('wide', 'narrow'), may hold values from -6 to 6
- pair_index: int32 [32, 2], P('wide'), may hold values from 0 to 63, as said below
- example_count: int32 [4], P('wide'), may hold values from 1 to 16, as said below
- aug_count: int32 [64], P('wide'), may hold values from 8 to 16, as said below
- conv_weight: float32 [2, 3, 3, 256, 256], P(None, None, None, None, 'narrow'), may hold values from -0.125 to 0.125
- gn_params: float32 [4, 256], P(None, 'narrow'), may hold values from -0.5 to 1.4, as said below
- conv_moment1: float32 [2, 3, 3, 256, 256], P(None, None, None, None, 'narrow'), may hold values from -2.5 to 2.5
- conv_moment2: float32 [2, 3, 3, 256, 256], P(None, None, None, None, 'narrow'), may hold values from 0.0265625 to 0.10625
- gn_moment1: float32 [4, 256], P(None, 'narrow'), may hold values from -3.5 to 3.5
- gn_moment2: float32 [4, 256], P(None, 'narrow'), may hold values from 0.05625 to 0.225
- noise_conv: float32 [2, 3, 3, 256, 256], P(None, None, None, None, 'narrow'), may hold values from -6 to 6
- noise_gn: float32 [4, 256], P(None, 'narrow'), may hold values from -6 to 6
- step_count: int32 [1], replicated, may hold values from 2 to 20
Outputs:
- block_out: bfloat16 [64, 256, 1024], P('wide', 'narrow')
- input_grad: float32 [64, 256, 1024], P('wide', 'narrow')
- example_norm: float32 [64], P('wide')
- influence: float32 [64], P('wide')
- conv_new: float32 [2, 3, 3, 256, 256], P(None, None, None, None, 'narrow')
- conv_low: bfloat16 [2, 3, 3, 256, 256], P(None, None, None, None, 'narrow')
- conv_first: float32 [2, 3, 3, 256, 256], P(None, None, None, None, 'narrow')
- conv_second: float32 [2, 3, 3, 256, 256], P(None, None, None, None, 'narrow')
- gn_new: float32 [4, 256], P(None, 'narrow')
- gn_first: float32 [4, 256], P(None, 'narrow')
- gn_second: float32 [4, 256], P(None, 'narrow')
Inputs may be any that keep to these rules, and one draw needn't show every extreme that they name: `pair_index`: pair p uses two different test images of the block of 16 test images 16 * (p div (8)) and on; every test image is in exactly one pair. `example_count`: some index of wide has all 16 examples live and some has one. `aug_count`: some example has all 16 augmentations live and some has 8. `gn_params`: rows 0 and 2 are gains, rows 1 and 3 biases.
All inputs are finite; a program needn't handle non-finite values.
Results may differ from a plain program's by a relative error of at most 0.0068.
Values may be sent and summed in bfloat16 or wider, within the bound.
A program may use at most 320 MiB of HBM per device.

v0:
```python
import math

import jax
import jax.numpy as jnp
from jax import lax
from jax.sharding import PartitionSpec as P

C = 256
MAP = 8
GROUPS = 16
AUG = 16


def standardize(weight):
    fan_in = weight.shape[-4] * weight.shape[-3] * weight.shape[-2]
    centre = weight - jnp.mean(weight, axis=(-4, -3, -2), keepdims=True)
    spread = jnp.mean(centre * centre, axis=(-4, -3, -2), keepdims=True)
    return centre * lax.rsqrt(fan_in * spread + 1e-06)


def norm_act(values, gains, biases, group_size):
    count, height, width, chans = values.shape
    grouped = values.reshape(count, height * width, chans // group_size, group_size)
    centre = grouped - jnp.mean(grouped, axis=(1, 3), keepdims=True)
    spread = jnp.mean(centre * centre, axis=(1, 3), keepdims=True)
    normed = (centre * lax.rsqrt(spread + 1e-05)).reshape(values.shape)
    scaled = normed * gains[:, None, None, :] + biases[:, None, None, :]
    return scaled * jax.nn.sigmoid(scaled)


def to_pixels(values):
    lead = values.shape[0]
    chans = values.shape[1]
    return (
        values.reshape(lead, chans, AUG, MAP, MAP)
        .transpose(0, 2, 3, 4, 1)
        .reshape(lead * AUG, MAP, MAP, chans)
    )


def from_pixels(values):
    lead = values.shape[0] // AUG
    chans = values.shape[3]
    return (
        values.reshape(lead, AUG, MAP, MAP, chans)
        .transpose(0, 4, 1, 2, 3)
        .reshape(lead, chans, AUG * MAP * MAP)
    )


def pad_map(values):
    return jnp.pad(values, ((0, 0), (1, 1), (1, 1), (0, 0)))


def taps_product(padded, kernel, side):
    count = padded.shape[0]
    total = jnp.zeros((count * side * side, kernel.shape[3]), jnp.float32)
    for row in range(3):
        for col in range(3):
            window = padded[:, row : row + side, col : col + side, :].reshape(
                count * side * side, padded.shape[3]
            )
            total = total + jnp.dot(window, kernel[row, col], preferred_element_type=jnp.float32)
    return total.reshape(count, side, side, kernel.shape[3])


def transposed_product(grad_low, kernel, side):
    count = grad_low.shape[0]
    padded = pad_map(grad_low)
    total = jnp.zeros((count * side * side, kernel.shape[2]), jnp.float32)
    for row in range(3):
        for col in range(3):
            window = padded[:, 2 - row : 2 - row + side, 2 - col : 2 - col + side, :].reshape(
                count * side * side, grad_low.shape[3]
            )
            total = total + lax.dot_general(
                window,
                kernel[row, col],
                (((1,), (1,)), ((), ())),
                preferred_element_type=jnp.float32,
            )
    return total.reshape(count, side, side, kernel.shape[2])


def kernel_rows(hidden_piece, grad_low, groups, side):
    count = hidden_piece.shape[0]
    width = hidden_piece.shape[3]
    per_group = count // groups * side * side
    padded = pad_map(hidden_piece)
    grad_groups = grad_low.reshape(groups, per_group, grad_low.shape[3])
    taps = []
    for row in range(3):
        for col in range(3):
            window = padded[:, row : row + side, col : col + side, :].reshape(
                groups, per_group, width
            )
            taps.append(
                jnp.einsum("gnk,gnd->gkd", window, grad_groups, preferred_element_type=jnp.float32)
            )
    return jnp.stack(taps, 1).reshape(groups, 3, 3, width, grad_low.shape[3])


def conv_forward(hidden, kernel, side):
    whole = lax.all_gather(hidden, "narrow", axis=3, tiled=True)
    result = taps_product(pad_map(whole), kernel, side)
    return (result, whole)


def kernel_grad(source, grad_low, groups, side):
    result = kernel_rows(source, grad_low, groups, side)
    return result


def input_grad_share(grad_low, kernel, side):
    partial_sum = transposed_product(grad_low, kernel, side)
    return lax.psum_scatter(partial_sum, "narrow", scatter_dimension=3, tiled=True)


def adamw(weight, first, second, grad, correction, rate, decay):
    first_new = 0.5 * first + 0.5 * grad
    second_new = 0.5 * second + 0.5 * grad * grad
    update = first_new / correction / (jnp.sqrt(second_new / correction) + 1e-08)
    return (weight - rate * (update + decay * weight), first_new, second_new)


def clipped(norm_sq, train_conv, train_norm, clip):
    lengths = jnp.sqrt(norm_sq)
    factors = clip / jnp.maximum(lengths, clip)
    clip_conv = jnp.sum(factors[:, None, None, None, None, None] * train_conv, 0)
    clip_norm = jnp.sum(factors[:, None, None] * train_norm, 0)
    return (lengths, factors, clip_conv, clip_norm)


def inner_part(train_conv, train_norm, dir_conv, dir_norm):
    inner_local = jnp.sum(train_conv * dir_conv[None], axis=(1, 2, 3, 4, 5)) + jnp.sum(
        train_norm * dir_norm[None], axis=(1, 2)
    )
    dir_local = jnp.sum(dir_conv * dir_conv) + jnp.sum(dir_norm * dir_norm)
    return (inner_local, dir_local)


def influence_of(factors, inner, dir_sq, clip):
    params_count = 18 * C * C + 4 * C
    return factors * inner * math.sqrt(params_count) / (clip * jnp.sqrt(dir_sq + 1e-06))


def local(
    images,
    cotangent,
    test_images,
    test_cotangent,
    pair_index,
    example_count,
    aug_count,
    conv_weight,
    gn_params,
    conv_moment1,
    conv_moment2,
    gn_moment1,
    gn_moment2,
    noise_conv,
    noise_gn,
    step_count,
):
    local_examples = images.shape[0]
    augments = AUG
    side = MAP
    channels = images.shape[1]
    group_size = C // GROUPS
    clip = 6.0 * C
    slots = jnp.arange(augments, dtype=jnp.int32)
    live = jnp.arange(local_examples, dtype=jnp.int32) < example_count[0]
    train_weight = jnp.where(
        live[:, None] & (slots[None, :] < aug_count[:, None]),
        1.0 / aug_count.astype(jnp.float32)[:, None],
        jnp.float32(0.0),
    )
    local_pairs = pair_index % augments
    signs = jnp.sum((local_pairs[:, 0:1] == slots[None, :]).astype(jnp.float32), 0) - jnp.sum(
        (local_pairs[:, 1:2] == slots[None, :]).astype(jnp.float32), 0
    )

    def activate(inputs, gains, biases):
        return norm_act(inputs, gains, biases, group_size)

    groups = local_examples + 1
    train_rows = local_examples * augments
    pictures = jnp.concatenate([to_pixels(images), to_pixels(test_images)], 0)
    targets = jnp.concatenate([to_pixels(cotangent), to_pixels(test_cotangent)], 0)
    row_weight = jnp.concatenate([train_weight.reshape(train_rows), signs], 0)
    values = pictures.astype(jnp.float32)
    count = values.shape[0]

    def tiled(index):
        return jnp.broadcast_to(gn_params[index][None, :], (count, channels))

    first_act, first_back = jax.vjp(activate, values, tiled(0), tiled(1))
    hidden_one = first_act.astype(jnp.bfloat16)
    kernels, kernel_back = jax.vjp(standardize, conv_weight)
    kernels_low = kernels.astype(jnp.bfloat16)
    middle, source_one = conv_forward(hidden_one, kernels_low[0], side)
    second_act, second_back = jax.vjp(activate, middle, tiled(2), tiled(3))
    hidden_two = second_act.astype(jnp.bfloat16)
    branch, source_two = conv_forward(hidden_two, kernels_low[1], side)
    block_out = from_pixels((values + branch)[:train_rows].astype(jnp.bfloat16))
    weighted = targets.astype(jnp.float32) * row_weight[:, None, None, None]
    branch_grad = weighted.astype(jnp.bfloat16)
    hidden_two_grad = input_grad_share(branch_grad, kernels_low[1], side)
    kernel_two_grad = kernel_grad(source_two, branch_grad, groups, side)
    middle_grad, gain_two, bias_two = second_back(hidden_two_grad)
    middle_low = middle_grad.astype(jnp.bfloat16)
    hidden_one_grad = input_grad_share(middle_low, kernels_low[0], side)
    kernel_one_grad = kernel_grad(source_one, middle_low, groups, side)
    input_part, gain_one, bias_one = first_back(hidden_one_grad)
    input_grad = from_pixels((weighted + input_part)[:train_rows])

    def raw_grad(standard):
        return kernel_back(standard)[0]

    conv_grads = jax.vmap(raw_grad)(jnp.stack([kernel_one_grad, kernel_two_grad], 1))
    norm_grads = (
        jnp.stack([gain_one, bias_one, gain_two, bias_two], 1)
        .reshape(groups, augments, 4, channels)
        .sum(1)
    )
    train_conv = conv_grads[:local_examples]
    train_norm = norm_grads[:local_examples]
    test_conv = conv_grads[local_examples]
    test_norm = norm_grads[local_examples]
    square_part = jnp.sum(train_conv * train_conv, axis=(1, 2, 3, 4, 5)) + jnp.sum(
        train_norm * train_norm, axis=(1, 2)
    )
    norm_sq = lax.psum(square_part, "narrow")
    lengths, factors, clip_conv, clip_norm = clipped(norm_sq, train_conv, train_norm, clip)
    sum_conv, sum_norm, dir_conv, dir_norm = (
        lax.psum(clip_conv.astype(jnp.bfloat16), "wide").astype(jnp.float32),
        lax.psum(clip_norm.astype(jnp.bfloat16), "wide").astype(jnp.float32),
        lax.psum(test_conv.astype(jnp.bfloat16), "wide").astype(jnp.float32),
        lax.psum(test_norm.astype(jnp.bfloat16), "wide").astype(jnp.float32),
    )
    inner_local, dir_local = inner_part(train_conv, train_norm, dir_conv, dir_norm)
    inner, dir_sq = lax.psum((inner_local, dir_local), "narrow")
    influence = influence_of(factors, inner, dir_sq, clip)
    total = local_examples * lax.axis_size("wide")
    noisy_conv = (sum_conv + math.sqrt(total) * noise_conv) / total
    noisy_norm = (sum_norm + math.sqrt(total) * noise_gn) / total
    correction = 1.0 - jnp.power(jnp.float32(0.5), step_count[0].astype(jnp.float32))
    conv_new, conv_first, conv_second = adamw(
        conv_weight, conv_moment1, conv_moment2, noisy_conv, correction, 1.0 / math.sqrt(9 * C), 0.1
    )
    gn_new, gn_first, gn_second = adamw(
        gn_params, gn_moment1, gn_moment2, noisy_norm, correction, 0.1, 0.0
    )
    return (
        block_out,
        input_grad,
        lengths,
        influence,
        conv_new,
        conv_new.astype(jnp.bfloat16),
        conv_first,
        conv_second,
        gn_new,
        gn_first,
        gn_second,
    )


def solution(mesh):
    in_specs = (
        P("wide", "narrow", None),
        P("wide", "narrow", None),
        P("wide", "narrow", None),
        P("wide", "narrow", None),
        P("wide", None),
        P("wide"),
        P("wide"),
        P(None, None, None, None, "narrow"),
        P(None, "narrow"),
        P(None, None, None, None, "narrow"),
        P(None, None, None, None, "narrow"),
        P(None, "narrow"),
        P(None, "narrow"),
        P(None, None, None, None, "narrow"),
        P(None, "narrow"),
        P(),
    )
    out_specs = (
        P("wide", "narrow", None),
        P("wide", "narrow", None),
        P("wide"),
        P("wide"),
        P(None, None, None, None, "narrow"),
        P(None, None, None, None, "narrow"),
        P(None, None, None, None, "narrow"),
        P(None, None, None, None, "narrow"),
        P(None, "narrow"),
        P(None, "narrow"),
        P(None, "narrow"),
    )
    return jax.shard_map(local, mesh=mesh, in_specs=in_specs, out_specs=out_specs, check_vma=False)
```

profile of v0, /device:TPU:0, one launch (start us, length us, event | category | flops | bytes accessed | tf_op | source)
XLA Modules:
  0.0 1277.8 jit_solution(1179548556138636593)
XLA Ops:
  14.5 14.7 %reshape.532 = bf16[256,64,2,16]{3,2,1,0:T(2,128)(2,1)} reshape(bf16[16,16,8,8,32]{4,3,2,1,0:T(8,128)(2,1)} %bitcast.375) | data formatting | bytes 2097152 | tf_op jit(solution)/shard_map/concatenate | solution.py:188
  29.2 15.9 %copy.348 = bf16[256,64,2,16]{0,3,2,1:T(8,128)(2,1)S(1)} copy(bf16[256,64,2,16]{3,2,1,0:T(2,128)(2,1)} %reshape.532) | data formatting | bytes 2097152 | tf_op jit(solution)/shard_map/concatenate | solution.py:188
  46.9 10.9 multiply_convert_fusion.1
  57.8 7.3 copy.299
  71.6 7.5 fusion.38
  79.1 10.6 pad_slice_fusion.24
  89.7 10.9 fusion.31
  100.6 16.1 %convolution_add_fusion.15 = f32[17408,256]{1,0:T(8,128)} fusion(f32[17408,256]{1,0:T(8,128)} %fusion.31, bf16[17408,32]{1,0:T(8,128)(2,1)} %bitcast.486, bf16[3,3,256,32]{2,3,1,0:T(8,128)(2,1)S(1)} %get-tuple-element.140), kind=kOutput, calls=%fused_computation.47 | convolution fusion | flops 289669120 | bytes 36782080 | tf_op jit(solution)/shard_map/dot_general | solution.py:76
  116.8 16.2 %convolution_add_fusion.14 = f32[17408,256]{1,0:T(8,128)} fusion(f32[17408,256]{1,0:T(8,128)} %convolution_add_fusion.15, bf16[17408,32]{1,0:T(8,128)(2,1)} %bitcast.485, bf16[3,3,256,32]{2,3,1,0:T(8,128)(2,1)S(1)} %get-tuple-element.140), kind=kOutput, calls=%fused_computation.46 | convolution fusion | flops 289669120 | bytes 36782080 | tf_op jit(solution)/shard_map/dot_general | solution.py:76
  133.0 16.2 %convolution_add_fusion.13 = f32[17408,256]{1,0:T(8,128)} fusion(f32[17408,256]{1,0:T(8,128)} %convolution_add_fusion.14, bf16[17408,32]{1,0:T(8,128)(2,1)} %bitcast.484, bf16[3,3,256,32]{2,3,1,0:T(8,128)(2,1)S(1)} %get-tuple-element.140), kind=kOutput, calls=%fused_computation.45 | convolution fusion | flops 289669120 | bytes 36782080 | tf_op jit(solution)/shard_map/dot_general | solution.py:76
  149.2 14.9 %convolution_add_fusion.12 = f32[17408,256]{1,0:T(8,128)} fusion(f32[17408,256]{1,0:T(8,128)} %convolution_add_fusion.13, bf16[17408,32]{1,0:T(8,128)(2,1)S(1)} %bitcast.455, bf16[3,3,256,32]{2,3,1,0:T(8,128)(2,1)S(1)} %get-tuple-element.140), kind=kOutput, calls=%fused_computation.44 | convolution fusion | flops 289669120 | bytes 40124416 | tf_op jit(solution)/shard_map/dot_general | solution.py:76
  164.1 16.6 %convolution_add_fusion.11 = f32[17408,256]{1,0:T(8,128)} fusion(f32[17408,256]{1,0:T(8,128)} %convolution_add_fusion.12, bf16[17408,32]{1,0:T(8,128)(2,1)} %bitcast.483, bf16[3,3,256,32]{2,3,1,0:T(8,128)(2,1)S(1)} %get-tuple-element.140), kind=kOutput, calls=%fused_computation.43 | convolution fusion | flops 289669120 | bytes 36782080 | tf_op jit(solution)/shard_map/dot_general | solution.py:76
  180.7 16.1 %convolution_add_fusion.10 = f32[17408,256]{1,0:T(8,128)} fusion(f32[17408,256]{1,0:T(8,128)} %convolution_add_fusion.11, bf16[17408,32]{1,0:T(8,128)(2,1)} %bitcast.482, bf16[3,3,256,32]{2,3,1,0:T(8,128)(2,1)S(1)} %get-tuple-element.140), kind=kOutput, calls=%fused_computation.42 | convolution fusion | flops 289669120 | bytes 36782080 | tf_op jit(solution)/shard_map/dot_general | solution.py:76
  196.8 14.7 %convolution_add_fusion.9 = f32[17408,256]{1,0:T(8,128)} fusion(f32[17408,256]{1,0:T(8,128)} %convolution_add_fusion.10, bf16[17408,32]{1,0:T(8,128)(2,1)S(1)} %bitcast.481, bf16[3,3,256,32]{2,3,1,0:T(8,128)(2,1)S(1)} %get-tuple-element.140), kind=kOutput, calls=%fused_computation.41 | convolution fusion | flops 289669120 | bytes 40124416 | tf_op jit(solution)/shard_map/dot_general | solution.py:76
  211.5 14.8 %convolution_add_fusion.8 = f32[17408,256]{1,0:T(8,128)} fusion(f32[17408,256]{1,0:T(8,128)} %convolution_add_fusion.9, bf16[17408,32]{1,0:T(8,128)(2,1)S(1)} %bitcast.480, bf16[3,3,256,32]{2,3,1,0:T(8,128)(2,1)S(1)} %get-tuple-element.140), kind=kOutput, calls=%fused_computation.40 | convolution fusion | flops 289669120 | bytes 40124416 | tf_op jit(solution)/shard_map/dot_general | solution.py:76
  226.3 21.9 %copy.311 = f32[272,8,8,256]{0,2,1,3:T(8,128)} copy(f32[272,8,8,256]{3,2,1,0:T(8,128)} %bitcast.390) | data formatting | bytes 35651584 | tf_op jit(solution)/shard_map/reshape | solution.py:82
  249.8 6.7 maximum_convert_fusion
  263.9 17.3 %copy.300 = bf16[272,8,8,256]{3,2,1,0:T(8,128)(2,1)} copy(bf16[272,8,8,256]{0,2,1,3:T(8,128)(2,1)} %all-gather.3.cloned.1.call-done) | data formatting | bytes 17825792 | tf_op jit(solution)/shard_map/all_gather | solution.py:104
  281.3 47.9 %pad_slice_fusion.8 = (bf16[272,8,8,256]{3,2,1,0:T(8,128)(2,1)}, bf16[272,8,8,256]{3,2,1,0:T(8,128)(2,1)}, bf16[272,8,8,256]{3,2,1,0:T(8,128)(2,1)}, bf16[272,8,...) fusion(bf16[272,8,8,256]{3,2,1,0:T(8,128)(2,1)} %copy.300), kind=kLoop, calls=%fused_computation.8 | loop fusion | bytes 80216064 | tf_op jit(solution)/shard_map/slice | solution.py:60
  329.3 6.4 fusion.30
  338.4 6.4 convolution_add_fusion.30
  375.2 122.8 %reduce-scatter.3.cloned.1.call-done = f32[272,8,8,32]{0,2,1,3:T(8,128)} async-done(((f32[272,8,8,256]{0,2,1,3:T(8,128)}), f32[272,8,8,32]{0,2,1,3:T(8,128)}) %reduce-scatter.3.cloned.1.call-update) | async-done | bytes 2228240 | tf_op jit(solution)/shard_map/reduce_scatter | solution.py:116
  498.0 8.4 copy.312
  506.5 16.1 %multiply_reduce_fusion.7 = (f32[272,32]{1,0:T(8,128)S(1)}, f32[272,8,8,32]{3,2,1,0:T(8,128)}, bf16[272,8,8,32]{3,2,1,0:T(8,128)(2,1)}) fusion(f32[272,8,8,32]{3,2,1,0:T(8,128)} %bitcast.384, f32[32]{0:T(128)S(1)} %copy-done.31, f32[272,32]{1,0:T(8,128)S(1)} %copy.303, f32[272,8,8,32]{3,2,1,0:T(8,128)} %copy.312, f32[32]{0:T(128)S(1)} %copy-done.38, ...), kind=kLoop, calls=%fused_computation.82 | loop fusion | flops 10018304 | bytes 7903488 | tf_op jit(solution)/shard_map/transpose(jvp())/reduce_sum | solution.py:26
  522.8 10.2 multiply_reduce_fusion.4
  533.3 9.4 add_convert_fusion
  542.7 7.3 copy.305
  550.0 24.4 %pad_slice_fusion.16 = (bf16[272,8,8,32]{3,2,1,0:T(8,128)(2,1)}, bf16[272,8,8,32]{3,2,1,0:T(8,128)(2,1)}, bf16[272,8,8,32]{3,2,1,0:T(8,128)(2,1)}, bf16[272,8,8,...) fusion(bf16[272,8,8,32]{3,2,1,0:T(8,128)(2,1)} %add_convert_fusion), kind=kLoop, calls=%fused_computation.16 | loop fusion | bytes 10027008 | tf_op jit(solution)/shard_map/slice | solution.py:73
  574.4 8.6 fusion.29
  583.0 7.3 fusion.17
  590.3 6.2 fusion.16
  596.5 6.3 fusion.15
  602.8 6.2 fusion.14
  609.0 6.1 fusion.13
  615.1 6.2 fusion.12
  621.3 6.2 fusion.11
  627.5 16.5 %convolution_add_fusion.7 = f32[17408,256]{1,0:T(8,128)} fusion(f32[17408,256]{1,0:T(8,128)} %fusion.29, bf16[17408,32]{1,0:T(8,128)(2,1)} %bitcast.479, bf16[3,3,256,32]{2,3,1,0:T(8,128)(2,1)S(1)} %copy-done.17), kind=kOutput, calls=%fused_computation.39 | convolution fusion | flops 289669120 | bytes 36782080 | tf_op jit(solution)/shard_map/dot_general | solution.py:76
  656.1 16.1 %convolution_add_fusion.6 = f32[17408,256]{1,0:T(8,128)} fusion(f32[17408,256]{1,0:T(8,128)} %convolution_add_fusion.7, bf16[17408,32]{1,0:T(8,128)(2,1)} %bitcast.478, bf16[3,3,256,32]{2,3,1,0:T(8,128)(2,1)S(1)} %copy-done.17), kind=kOutput, calls=%fused_computation.38 | convolution fusion | flops 289669120 | bytes 36782080 | tf_op jit(solution)/shard_map/dot_general | solution.py:76
  672.2 16.1 %convolution_add_fusion.5 = f32[17408,256]{1,0:T(8,128)} fusion(f32[17408,256]{1,0:T(8,128)} %convolution_add_fusion.6, bf16[17408,32]{1,0:T(8,128)(2,1)} %bitcast.477, bf16[3,3,256,32]{2,3,1,0:T(8,128)(2,1)S(1)} %copy-done.17), kind=kOutput, calls=%fused_computation.37 | convolution fusion | flops 289669120 | bytes 36782080 | tf_op jit(solution)/shard_map/dot_general | solution.py:76
  688.3 15.0 %convolution_add_fusion.4 = f32[17408,256]{1,0:T(8,128)} fusion(f32[17408,256]{1,0:T(8,128)} %convolution_add_fusion.5, bf16[17408,32]{1,0:T(8,128)(2,1)S(1)} %bitcast.368, bf16[3,3,256,32]{2,3,1,0:T(8,128)(2,1)S(1)} %copy-done.17), kind=kOutput, calls=%fused_computation.36 | convolution fusion | flops 289669120 | bytes 40124416 | tf_op jit(solution)/shard_map/dot_general | solution.py:76
  703.3 16.6 %convolution_add_fusion.3 = f32[17408,256]{1,0:T(8,128)} fusion(f32[17408,256]{1,0:T(8,128)} %convolution_add_fusion.4, bf16[17408,32]{1,0:T(8,128)(2,1)} %bitcast.476, bf16[3,3,256,32]{2,3,1,0:T(8,128)(2,1)S(1)} %copy-done.17), kind=kOutput, calls=%fused_computation.35 | convolution fusion | flops 289669120 | bytes 36782080 | tf_op jit(solution)/shard_map/dot_general | solution.py:76
  719.9 14.8 %convolution_add_fusion.2 = f32[17408,256]{1,0:T(8,128)} fusion(f32[17408,256]{1,0:T(8,128)} %convolution_add_fusion.3, bf16[17408,32]{1,0:T(8,128)(2,1)S(1)} %bitcast.475, bf16[3,3,256,32]{2,3,1,0:T(8,128)(2,1)S(1)} %copy-done.17), kind=kOutput, calls=%fused_computation.34 | convolution fusion | flops 289669120 | bytes 40124416 | tf_op jit(solution)/shard_map/dot_general | solution.py:76
  734.7 14.8 %convolution_add_fusion.1 = f32[17408,256]{1,0:T(8,128)} fusion(f32[17408,256]{1,0:T(8,128)} %convolution_add_fusion.2, bf16[17408,32]{1,0:T(8,128)(2,1)S(1)} %bitcast.472, bf16[3,3,256,32]{2,3,1,0:T(8,128)(2,1)S(1)} %copy-done.17), kind=kOutput, calls=%fused_computation.33 | convolution fusion | flops 289669120 | bytes 40124416 | tf_op jit(solution)/shard_map/dot_general | solution.py:76
  749.5 17.3 %copy.306 = bf16[272,8,8,256]{3,2,1,0:T(8,128)(2,1)} copy(bf16[272,8,8,256]{0,2,1,3:T(8,128)(2,1)} %all-gather.5.cloned.1.call-done) | data formatting | bytes 17825792 | tf_op jit(solution)/shard_map/all_gather | solution.py:104
  766.8 48.1 %pad_slice_fusion = (bf16[272,8,8,256]{3,2,1,0:T(8,128)(2,1)}, bf16[272,8,8,256]{3,2,1,0:T(8,128)(2,1)}, bf16[272,8,8,256]{3,2,1,0:T(8,128)(2,1)}, bf16[272,8,8,...) fusion(bf16[272,8,8,256]{3,2,1,0:T(8,128)(2,1)} %copy.306), kind=kLoop, calls=%fused_computation | loop fusion | bytes 80216064 | tf_op jit(solution)/shard_map/slice | solution.py:60
  852.0 16.1 %convolution_add_fusion = f32[17408,256]{1,0:T(8,128)} fusion(f32[17408,256]{1,0:T(8,128)} %convolution_add_fusion.1, bf16[17408,32]{1,0:T(8,128)(2,1)} %bitcast.469, bf16[3,3,256,32]{2,3,1,0:T(8,128)(2,1)S(1)} %copy-done.17), kind=kOutput, calls=%fused_computation.32 | convolution fusion | flops 289669120 | bytes 36782080 | tf_op jit(solution)/shard_map/dot_general | solution.py:76
  868.1 22.0 %copy.318 = f32[272,8,8,256]{0,2,1,3:T(8,128)} copy(f32[272,8,8,256]{3,2,1,0:T(8,128)} %bitcast.389) | data formatting | bytes 35651584 | tf_op jit(solution)/shard_map/reshape | solution.py:82
  891.3 6.7 fusion.39
  898.0 6.4 fusion.32
  904.4 6.4 convolution_add_fusion.23
  910.8 6.4 convolution_add_fusion.22
  938.9 9.1 fusion.4
  960.1 183.1 %reduce-scatter.5.cloned.1.call-done = f32[272,8,8,32]{0,2,1,3:T(8,128)} async-done(((f32[272,8,8,256]{0,2,1,3:T(8,128)}), f32[272,8,8,32]{0,2,1,3:T(8,128)}) %reduce-scatter.5.cloned.1.call-update) | async-done | bytes 2228240 | tf_op jit(solution)/shard_map/reduce_scatter | solution.py:116
  1143.2 8.4 copy.319
  1151.6 15.6 %multiply_reduce_fusion.5 = (f32[272,32]{1,0:T(8,128)S(1)}, f32[272,32]{1,0:T(8,128)S(1)}, f32[272,32]{1,0:T(8,128)S(1)}, f32[272,8,8,32]{3,2,1,0:T(8,128)}) fusion(f32[272,32]{1,0:T(8,128)S(1)} %copy-done.14, f32[272,32]{1,0:T(8,128)S(1)} %copy-done.12, bf16[16,8,8,32]{3,2,1,0:T(8,128)(2,1)S(1)} %bitcast.493, bf16[256,8,8,32]{3,2,1,0:T(8,128)(2,1)} %bitcast.378, ...), kind=kLoop, calls=%fused_computation.79 | loop fusion | flops 11672064 | bytes 5744896 | tf_op jit(solution)/shard_map/transpose(jvp())/reduce_sum | solution.py:27
  1167.5 9.8 psum.51
  1178.2 12.1 fusion.41
  1190.5 13.8 %psum.49 = f32[16]{0:T(128)S(1)} all-reduce(f32[16]{0:T(128)S(1)} %add.276), channel_id=1, replica_groups=mesh['wide'=4,'narrow'=8] {'narrow'}, use_global_device_ids=true, to_apply=%region_27.28 | all-reduce | flops 16 | bytes 128 | tf_op jit(solution)/shard_map/psum | solution.py:233
  1205.0 7.2 multiply_reduce_fusion.1
  1213.5 14.1 %all-reduce.4 = (f32[16]{0:T(128)S(1)}, f32[]{:T(128)}) all-reduce(f32[16]{0:T(128)S(1)} %add.277, f32[]{:T(128)S(6)} %add.278), channel_id=1, replica_groups=mesh['wide'=4,'narrow'=8] {'narrow'}, use_global_device_ids=true, to_apply=%region_32.33 | all-reduce | flops 17 | bytes 136 | tf_op jit(solution)/shard_map/psum | solution.py:242
  1228.3 9.4 slice_add_fusion
  1238.3 6.4 copy.338
  1244.8 8.0 psum.55
  1253.4 14.7 %all-reduce.10.cloned.1.call-done = bf16[2,3,3,256,32]{3,4,2,1,0:T(8,128)(2,1)} async-done(((bf16[2,3,3,256,32]{3,4,2,1,0:T(8,128)(2,1)}), bf16[2,3,3,256,32]{3,4,2,1,0:T(8,128)(2,1)}) %all-reduce.10.cloned.1.call-update) | async-done | bytes 294928 | tf_op jit(solution)/shard_map/psum | solution.py:236
  (375 shorter events, 145.9 us)
Async XLA Ops:
  7.2 256.7 %all-gather.3.cloned.1.call-start = ((), (), s32[]{:S(2)}) async-start(), calls=%async_computation.2 | async-start | bytes 14155776 | tf_op jit(solution)/shard_map/all_gather | solution.py:104
  8.6 38.3 %copy-start.32 = (f32[32]{0:T(128)}, f32[32]{0:T(128)S(1)}, u32[]{:S(2)}) copy-start(f32[32]{0:T(128)S(1)} %get-tuple-element.144) | copy-start | bytes 388
  8.6 38.3 %copy-start.35 = (f32[32]{0:T(128)}, f32[32]{0:T(128)S(1)}, u32[]{:S(2)}) copy-start(f32[32]{0:T(128)S(1)} %get-tuple-element.143) | copy-start | bytes 388
  9.6 37.3 %copy-start.5 = (bf16[1,32,1024]{1,2,0:T(8,128)(2,1)}, bf16[1,32,1024]{1,2,0:T(8,128)(2,1)S(1)}, u32[]{:S(2)}) copy-start(bf16[1,32,1024]{1,2,0:T(8,128)(2,1)S(1)} %copy.294) | copy-start | bytes 196612
  46.1 19.9 %copy-start.43 = (s32[16]{0:T(128)S(1)}, s32[16]{0:T(128)}, u32[]{:S(2)}) copy-start(s32[16]{0:T(128)} %param.22) | copy-start | bytes 196
  46.1 19.9 %copy-start.42 = (s32[8,2]{0,1:T(2,128)S(1)}, s32[8,2]{0,1:T(2,128)}, u32[]{:S(2)}) copy-start(s32[8,2]{0,1:T(2,128)} %param.20) | copy-start | bytes 196
  46.1 20.0 %copy-start.7 = (f32[2,3,3,256,32]{3,4,2,1,0:T(8,128)S(1)}, f32[2,3,3,256,32]{3,4,2,1,0:T(8,128)}, u32[]{:S(2)}) copy-start(f32[2,3,3,256,32]{3,4,2,1,0:T(8,128)} %param.23) | copy-start | bytes 1769476
  46.7 19.7 %copy-start.24 = (bf16[1,32,1024]{2,1,0:T(8,128)(2,1)S(1)}, bf16[1,32,1024]{2,1,0:T(8,128)(2,1)}, u32[]{:S(2)}) copy-start(bf16[1,32,1024]{2,1,0:T(8,128)(2,1)} %param.19) | copy-start | bytes 196612
  46.8 19.8 %copy-start.11 = (f32[272,32]{1,0:T(8,128)}, f32[272,32]{1,0:T(8,128)S(1)}, u32[]{:S(2)}) copy-start(f32[272,32]{1,0:T(8,128)S(1)} %copy.297) | copy-start | bytes 104452
  46.9 19.9 %copy-start.13 = (f32[272,32]{1,0:T(8,128)}, f32[272,32]{1,0:T(8,128)S(1)}, u32[]{:S(2)}) copy-start(f32[272,32]{1,0:T(8,128)S(1)} %copy.298) | copy-start | bytes 104452
  46.9 21.5 %copy-start.18 = (bf16[16,32,1024]{2,1,0:T(8,128)(2,1)S(1)}, bf16[16,32,1024]{2,1,0:T(8,128)(2,1)}, u32[]{:S(2)}) copy-start(bf16[16,32,1024]{2,1,0:T(8,128)(2,1)} %param.17) | copy-start | bytes 3145732
  65.1 432.9 %reduce-scatter.3.cloned.1.call-start = ((), (), s32[]{:S(2)}) async-start(), calls=%async_computation.4 | async-start | bytes 28311552 | tf_op jit(solution)/shard_map/reduce_scatter | solution.py:116
  66.5 12.6 copy-start.9
  67.4 11.7 copy-start.29
  68.4 143.1 %copy-start.15 = (bf16[3,3,256,32]{2,3,1,0:T(8,128)(2,1)}, bf16[3,3,256,32]{2,3,1,0:T(8,128)(2,1)S(1)}, u32[]{:S(2)}) copy-start(bf16[3,3,256,32]{2,3,1,0:T(8,128)(2,1)S(1)} %get-tuple-element.140) | copy-start | bytes 442372
  71.6 7.5 copy-start.27
  248.2 501.3 %all-gather.5.cloned.1.call-start = ((), (), s32[]{:S(2)}) async-start(), calls=%async_computation.3 | async-start | bytes 14155776 | tf_op jit(solution)/shard_map/all_gather | solution.py:104
  281.3 48.0 %copy-start.17 = (bf16[3,3,256,32]{2,3,1,0:T(8,128)(2,1)S(1)}, bf16[3,3,256,32]{2,3,1,0:T(8,128)(2,1)}, u32[]{:S(2)}) copy-start(bf16[3,3,256,32]{2,3,1,0:T(8,128)(2,1)} %get-tuple-element.141) | copy-start | bytes 442372
  329.2 15.5 %slice-start.59 = ((s8[8912896]{0:T(1024)(128)(4,1)}), s8[4194304]{0:T(1024)(128)(4,1)S(1)}, s32[]{:S(2)}) async-start(s8[8912896]{0:T(1024)(128)(4,1)} %bitcast.448), calls=%async_computation.67 | async-start | bytes 8388608
  329.2 15.5 %slice-start.60 = ((s8[8912896]{0:T(1024)(128)(4,1)}), s8[4194304]{0:T(1024)(128)(4,1)S(1)}, s32[]{:S(2)}) async-start(s8[8912896]{0:T(1024)(128)(4,1)} %bitcast.448), calls=%async_computation.68 | async-start | bytes 8388608
  335.6 9.1 slice-start.61
  335.6 14.6 %slice-start.56 = ((s8[8912896]{0:T(1024)(128)(4,1)}), s8[4194304]{0:T(1024)(128)(4,1)S(1)}, s32[]{:S(2)}) async-start(s8[8912896]{0:T(1024)(128)(4,1)} %bitcast.444), calls=%async_computation.64 | async-start | bytes 8388608
  338.3 9.2 slice-start.8
  338.4 9.2 slice-start.9
  338.4 11.9 slice-start.57
  344.8 11.0 slice-start.50
  347.6 8.2 slice-start.51
  371.9 134.5 %copy-start.31 = (f32[32]{0:T(128)S(1)}, f32[32]{0:T(128)}, u32[]{:S(2)}) copy-start(f32[32]{0:T(128)} %get-tuple-element.142) | copy-start | bytes 388
  371.9 134.5 %copy-start.38 = (f32[32]{0:T(128)S(1)}, f32[32]{0:T(128)}, u32[]{:S(2)}) copy-start(f32[32]{0:T(128)} %get-tuple-element.145) | copy-start | bytes 388
  550.0 407.3 %all-reduce.8.cloned.1.call-start = ((), (), s32[]{:S(2)}) async-start(), calls=%async_computation.6 | async-start | bytes 589824 | tf_op jit(solution)/shard_map/psum | solution.py:238
  583.0 7.3 slice-start
  583.0 7.3 slice-start.1
  688.3 31.6 %slice-start.66 = ((s8[4456448]{0:T(1024)(128)(4,1)}), s8[4194304]{0:T(1024)(128)(4,1)S(1)}, s32[]{:S(2)}) async-start(s8[4456448]{0:T(1024)(128)(4,1)} %bitcast.473), calls=%async_computation.74 | async-start | bytes 8388608
  703.3 16.6 %slice-start.67 = ((s8[4456448]{0:T(1024)(128)(4,1)}), s8[262144]{0:T(1024)(128)(4,1)S(1)}, s32[]{:S(2)}) async-start(s8[4456448]{0:T(1024)(128)(4,1)} %bitcast.473), calls=%async_computation.75 | async-start | bytes 524288
  703.3 31.4 %slice-start.64 = ((s8[4456448]{0:T(1024)(128)(4,1)}), s8[4194304]{0:T(1024)(128)(4,1)S(1)}, s32[]{:S(2)}) async-start(s8[4456448]{0:T(1024)(128)(4,1)} %bitcast.470), calls=%async_computation.72 | async-start | bytes 8388608
  719.9 14.8 %slice-start.65 = ((s8[4456448]{0:T(1024)(128)(4,1)}), s8[262144]{0:T(1024)(128)(4,1)S(1)}, s32[]{:S(2)}) async-start(s8[4456448]{0:T(1024)(128)(4,1)} %bitcast.470), calls=%async_computation.73 | async-start | bytes 524288
  766.8 48.1 %copy-start = (bf16[17,1024,32]{1,2,0:T(8,128)(2,1)S(1)}, bf16[17,1024,32]{1,2,0:T(8,128)(2,1)}, u32[]{:S(2)}) copy-start(bf16[17,1024,32]{1,2,0:T(8,128)(2,1)} %multiply_convert_fusion.2) | copy-start | bytes 3342340
  851.9 291.3 %reduce-scatter.5.cloned.1.call-start = ((), (), s32[]{:S(2)}) async-start(), calls=%async_computation.5 | async-start | bytes 28311552 | tf_op jit(solution)/shard_map/reduce_scatter | solution.py:116
  890.1 7.9 copy-start.16
  890.1 378.0 %all-reduce.10.cloned.1.call-start = ((), (), s32[]{:S(2)}) async-start(), calls=%async_computation.7 | async-start | bytes 589824 | tf_op jit(solution)/shard_map/psum | solution.py:236
  898.0 19.2 %slice-start.38 = ((s8[8912896]{0:T(1024)(128)(4,1)}), s8[4194304]{0:T(1024)(128)(4,1)S(1)}, s32[]{:S(2)}) async-start(s8[8912896]{0:T(1024)(128)(4,1)} %bitcast.418), calls=%async_computation.46 | async-start | bytes 8388608
  898.0 19.2 %slice-start.39 = ((s8[8912896]{0:T(1024)(128)(4,1)}), s8[4194304]{0:T(1024)(128)(4,1)S(1)}, s32[]{:S(2)}) async-start(s8[8912896]{0:T(1024)(128)(4,1)} %bitcast.418), calls=%async_computation.47 | async-start | bytes 8388608
  904.4 12.9 %slice-start.40 = ((s8[8912896]{0:T(1024)(128)(4,1)}), s8[524288]{0:T(1024)(128)(4,1)S(1)}, s32[]{:S(2)}) async-start(s8[8912896]{0:T(1024)(128)(4,1)} %bitcast.418), calls=%async_computation.48 | async-start | bytes 1048576
  904.4 18.4 %slice-start.32 = ((s8[8912896]{0:T(1024)(128)(4,1)}), s8[4194304]{0:T(1024)(128)(4,1)S(1)}, s32[]{:S(2)}) async-start(s8[8912896]{0:T(1024)(128)(4,1)} %bitcast.412), calls=%async_computation.40 | async-start | bytes 8388608
  910.8 9.2 slice-start.5
  910.8 9.2 slice-start.6
  910.8 12.0 slice-start.33
  917.3 11.0 slice-start.20
  920.1 8.3 slice-start.21
  957.2 194.4 %copy-start.12 = (f32[272,32]{1,0:T(8,128)S(1)}, f32[272,32]{1,0:T(8,128)}, u32[]{:S(2)}) copy-start(f32[272,32]{1,0:T(8,128)} %copy-done.11) | copy-start | bytes 104452
  957.2 194.4 %copy-start.14 = (f32[272,32]{1,0:T(8,128)S(1)}, f32[272,32]{1,0:T(8,128)}, u32[]{:S(2)}) copy-start(f32[272,32]{1,0:T(8,128)} %copy-done.13) | copy-start | bytes 104452
  957.2 194.4 %copy-start.33 = (f32[32]{0:T(128)S(1)}, f32[32]{0:T(128)}, u32[]{:S(2)}) copy-start(f32[32]{0:T(128)} %copy-done.32) | copy-start | bytes 388
  957.2 194.4 %copy-start.36 = (f32[32]{0:T(128)S(1)}, f32[32]{0:T(128)}, u32[]{:S(2)}) copy-start(f32[32]{0:T(128)} %copy-done.35) | copy-start | bytes 388
  1151.6 15.7 %copy-start.22 = (f32[272,32]{1,0:T(8,128)S(1)}, f32[272,32]{1,0:T(8,128)}, u32[]{:S(2)}) copy-start(f32[272,32]{1,0:T(8,128)} %get-tuple-element.77) | copy-start | bytes 104452
  1151.6 15.7 %copy-start.23 = (f32[272,32]{1,0:T(8,128)S(1)}, f32[272,32]{1,0:T(8,128)}, u32[]{:S(2)}) copy-start(f32[272,32]{1,0:T(8,128)} %get-tuple-element.84) | copy-start | bytes 104452
  1151.6 26.4 %copy-start.26 = (f32[272,2]{0,1:T(2,128)S(1)}, f32[272,2]{0,1:T(2,128)}, u32[]{:S(2)}) copy-start(f32[272,2]{0,1:T(2,128)} %copy-done.25) | copy-start | bytes 6532
  1237.7 15.0 %copy-start.34 = (f32[4,32]{1,0:T(4,128)S(1)}, f32[4,32]{1,0:T(4,128)}, u32[]{:S(2)}) copy-start(f32[4,32]{1,0:T(4,128)} %param.24) | copy-start | bytes 1540
  1237.7 15.0 %copy-start.39 = (f32[4,32]{1,0:T(4,128)S(1)}, f32[4,32]{1,0:T(4,128)}, u32[]{:S(2)}) copy-start(f32[4,32]{1,0:T(4,128)} %param.30) | copy-start | bytes 1540
  1237.8 15.0 %copy-start.40 = (f32[4,32]{1,0:T(4,128)S(1)}, f32[4,32]{1,0:T(4,128)}, u32[]{:S(2)}) copy-start(f32[4,32]{1,0:T(4,128)} %param.28) | copy-start | bytes 1540
  1237.8 15.0 %copy-start.41 = (f32[4,32]{1,0:T(4,128)S(1)}, f32[4,32]{1,0:T(4,128)}, u32[]{:S(2)}) copy-start(f32[4,32]{1,0:T(4,128)} %param.27) | copy-start | bytes 1540
  1237.8 30.3 %copy-start.8 = (f32[2,3,3,256,32]{3,4,2,1,0:T(8,128)S(1)}, f32[2,3,3,256,32]{3,4,2,1,0:T(8,128)}, u32[]{:S(2)}) copy-start(f32[2,3,3,256,32]{3,4,2,1,0:T(8,128)} %param.23) | copy-start | bytes 1769476
  1237.8 30.3 %copy-start.19 = (f32[2,3,3,256,32]{3,4,2,1,0:T(8,128)S(1)}, f32[2,3,3,256,32]{3,4,2,1,0:T(8,128)}, u32[]{:S(2)}) copy-start(f32[2,3,3,256,32]{3,4,2,1,0:T(8,128)} %param.29) | copy-start | bytes 1769476
  1237.8 30.3 %copy-start.20 = (f32[2,3,3,256,32]{3,4,2,1,0:T(8,128)S(1)}, f32[2,3,3,256,32]{3,4,2,1,0:T(8,128)}, u32[]{:S(2)}) copy-start(f32[2,3,3,256,32]{3,4,2,1,0:T(8,128)} %param.26) | copy-start | bytes 1769476
  1237.8 30.3 %copy-start.21 = (f32[2,3,3,256,32]{3,4,2,1,0:T(8,128)S(1)}, f32[2,3,3,256,32]{3,4,2,1,0:T(8,128)}, u32[]{:S(2)}) copy-start(f32[2,3,3,256,32]{3,4,2,1,0:T(8,128)} %param.25) | copy-start | bytes 1769476
  (54 other events, 178.7 us)
Sparse Core Ops, SparseCore 0:
  65.2 119.4 all-gather.2
  248.3 249.6 reduce-scatter.2
  550.1 115.0 all-gather.4
  852.1 41.4 all-reduce.7
  895.9 247.2 reduce-scatter.4
  1228.4 39.6 all-reduce.9
where the time goes:
time: 1290 us; the launch traced here: 1280 us
  matrix products  412 us (32%)
  local copies, waits for them, and re-layouts  329 us (26%)
  waiting for transfers between devices  321 us (25%)
  other arithmetic  149 us (12%)
  blocking collectives  45.7 us (4%)
  between operations  19.2 us (1%)
    reduce_scatter x2, waiting for transfers between devices, input_grad_share(): lax.psum_scatter(partial_sum, 'narrow', scatter_dimension=3, tiled=True)  306 us
    dot_general x18, matrix products, transposed_product(): lax.dot_general(window, kernel[row, col], (((1,), (1,)), ((), ())), prefe...  271 us
    slice x2, local copies, waits for them, and re-layouts, taps_product(): padded[:, row:row + side, col:col + side, :]  96 us
    dot_general x18, matrix products, kernel_rows(): jnp.einsum('gnk,gnd->gkd', window, grad_groups, preferred_element_type=jn...  74.5 us
    dot_general x18, matrix products, taps_product(): jnp.dot(window, kernel[row, col], preferred_element_type=jnp.float32)  66.9 us
    reshape x2, local copies, waits for them, and re-layouts, transposed_product(): return total.reshape(count, side, side, kernel.shape[2])  43.9 us
    slice x2, local copies, waits for them, and re-layouts, transposed_product(): padded[:, 2 - row:2 - row + side, 2 - col:2 - col + side, :]  35 us
    all_gather x2, local copies, waits for them, and re-layouts, conv_forward(): whole = lax.all_gather(hidden, 'narrow', axis=3, tiled=True)  34.6 us
  transfers between devices with their start and end apart: 6, of which 3 were waited for; matrix products, arithmetic and copies ran while one was open for 49% of the time, Pallas kernels for 0%

commit v1 on v0

v1 whole, which is shorter than its diff:
```python
import functools
import math

import jax
import jax.numpy as jnp
from jax import lax
from jax.experimental import pallas as pl
from jax.experimental.pallas import tpu as pltpu
from jax.sharding import PartitionSpec as P

C = 256
MAP = 8
GROUPS = 16
AUG = 16
PIX = MAP * MAP
FAN = 9 * C
LANES = 128
CLIP = 6.0 * C
MESH = pl.DeviceIdType.MESH
f32 = jnp.float32
bf16 = jnp.bfloat16
KCOLS = 2 * FAN


def lane_tile(index):
    return pl.ds(pl.multiple_of(index * LANES, LANES), LANES)


def group_sum(tile):
    return tile.reshape(GROUPS, C // GROUPS, LANES).sum(1)


def spread_group(rows):
    return jnp.broadcast_to(rows[:, None, :], (GROUPS, C // GROUPS, LANES)).reshape(C, LANES)


def image_sum(rows, ones):
    return lax.dot_general(
        rows,
        ones,
        (((1,), (0,)), ((), ())),
        precision=lax.Precision.HIGHEST,
        preferred_element_type=f32,
    )


def sigmoid(z):
    return 0.5 * jnp.tanh(0.5 * z) + 0.5


def tap_masks():
    lane = lax.broadcasted_iota(jnp.int32, (1, LANES), 1)
    row = (lane // MAP) % MAP
    col = lane % MAP
    masks = []
    for r in (-1, 0, 1):
        for c in (-1, 0, 1):
            ok = (row + r >= 0) & (row + r < MAP) & (col + c >= 0) & (col + c < MAP)
            masks.append(jnp.where(ok, 1.0, 0.0).astype(f32).astype(bf16))
    return masks


def store_taps(value, col_ref, t, masks, flip):
    for tap in range(9):
        shift = (tap // 3 - 1) * MAP + (tap % 3 - 1)
        if shift == 0:
            moved = value
        else:
            moved = pltpu.roll(value, (-shift) % LANES, 1) * masks[tap]
        place = 8 - tap if flip else tap
        col_ref[place * C : (place + 1) * C, lane_tile(t)] = moved


def product(a, b):
    return jnp.dot(a, b, preferred_element_type=f32)


def product_nt(a, b):
    return lax.dot_general(a, b, (((1,), (1,)), ((), ())), preferred_element_type=f32)


class Work:
    pass


def norm_forward(wk, load, tiles, which, hat, rstd, hidden, col):
    stat = wk.stat

    @pl.loop(0, tiles)
    def _(t):
        stat[pl.ds(pl.multiple_of(t * GROUPS, GROUPS), GROUPS), :] = group_sum(load(t))

    rows = tiles * GROUPS
    stat[:rows, :] = image_sum(stat[:rows, :], wk.ones[...]) * (1.0 / (PIX * C // GROUPS))

    @pl.loop(0, tiles)
    def _(t):
        at = pl.ds(pl.multiple_of(t * GROUPS, GROUPS), GROUPS)
        centre = load(t) - spread_group(stat[at, :])
        hat[:, lane_tile(t)] = centre
        stat[at, :] = group_sum(centre * centre)

    spread = image_sum(stat[:rows, :], wk.ones[...]) * (1.0 / (PIX * C // GROUPS))
    rstd[:rows, :] = lax.rsqrt(spread + 1e-05)

    @pl.loop(0, tiles)
    def _(t):
        at = pl.ds(pl.multiple_of(t * GROUPS, GROUPS), GROUPS)
        normed = hat[:, lane_tile(t)] * spread_group(rstd[at, :])
        hat[:, lane_tile(t)] = normed
        scaled = normed * wk.gn[2 * which] + wk.gn[2 * which + 1]
        act = (scaled * sigmoid(scaled)).astype(bf16)
        hidden[:, lane_tile(t)] = act
        if col is not None:
            store_taps(act, col, t, wk.masks, False)


def norm_backward(wk, grad, tiles, which, hat, rstd, emit, acc):
    stat, stat2 = wk.stat, wk.stat2
    acc[0] = jnp.zeros((C, LANES), f32)
    acc[1] = jnp.zeros((C, LANES), f32)

    @pl.loop(0, tiles)
    def _(t):
        at = pl.ds(pl.multiple_of(t * GROUPS, GROUPS), GROUPS)
        normed = hat[:, lane_tile(t)]
        scaled = normed * wk.gn[2 * which] + wk.gn[2 * which + 1]
        gate = sigmoid(scaled)
        inner = grad[:, lane_tile(t)] * gate * (1.0 + scaled * (1.0 - gate))
        acc[0] += inner * normed
        acc[1] += inner
        inner = inner * wk.gn[2 * which]
        grad[:, lane_tile(t)] = inner
        stat[at, :] = group_sum(inner)
        stat2[at, :] = group_sum(inner * normed)

    if emit is not None:
        rows = tiles * GROUPS
        scale = 1.0 / (PIX * C // GROUPS)
        stat[:rows, :] = image_sum(stat[:rows, :], wk.ones[...]) * scale
        stat2[:rows, :] = image_sum(stat2[:rows, :], wk.ones[...]) * scale

        @pl.loop(0, tiles)
        def _(t):
            at = pl.ds(pl.multiple_of(t * GROUPS, GROUPS), GROUPS)
            value = grad[:, lane_tile(t)] - spread_group(stat[at, :])
            value = value - hat[:, lane_tile(t)] * spread_group(stat2[at, :])
            emit(t, value * spread_group(rstd[at, :]))


def matmul_cols(out, left, right, width):
    step = min(width, 256)
    for j in range(0, width, step):
        out[:, j : j + step] = product(left, right[:, j : j + step])


def fill_work(wk):
    half_a = lax.broadcasted_iota(jnp.int32, (LANES, LANES), 0) // PIX
    half_b = lax.broadcasted_iota(jnp.int32, (LANES, LANES), 1) // PIX
    wk.ones[...] = jnp.where(half_a == half_b, 1.0, 0.0).astype(f32)
    wk.masks = tap_masks()


def unpack_params(wk):
    tail = wk.ktp[:, KCOLS : KCOLS + LANES].astype(f32)
    for k in range(6):
        value = tail[:, k : k + 1] + tail[:, 8 + k : 9 + k] + tail[:, 16 + k : 17 + k]
        value = jnp.broadcast_to(value, (C, LANES))
        if k < 4:
            wk.gn[k] = value
        else:
            wk.rs[k - 4] = value


def turn_kernels(wk):
    for k in range(18):
        at = (k // 9) * FAN + (k % 9) * C
        wk.kb[k // 9, :, (k % 9) * C : (k % 9 + 1) * C] = wk.ktp[:, at : at + C].T


def unit(wk, x_load, cot_load, weight_load, tiles, grads, gn_out, block_store, part_store):
    width = tiles * LANES
    col = wk.col

    def cols(ref):
        return ref if width == ref.shape[1] else ref.at[:, :width]

    norm_forward(wk, x_load, tiles, 0, wk.hat1, wk.rstd1, wk.hid1, col)
    matmul_cols(wk.mid, wk.ktp[:, :FAN], cols(col), width)
    norm_forward(
        wk,
        lambda t: wk.mid[:, lane_tile(t)],
        tiles,
        1,
        wk.hat2,
        wk.rstd2,
        wk.hid2,
        col if block_store is not None else None,
    )
    if block_store is not None:
        matmul_cols(wk.mid, wk.ktp[:, FAN : 2 * FAN], cols(col), width)

    @pl.loop(0, tiles)
    def _(t):
        if block_store is not None:
            block_store(t, x_load(t) + wk.mid[:, lane_tile(t)])
        store_taps((cot_load(t) * weight_load(t)).astype(bf16), col, t, wk.masks, True)

    matmul_cols(wk.mid, wk.kb[1], cols(col), width)
    for tap in range(9):
        grads[9 + tap] = product_nt(col[tap * C : (tap + 1) * C, :width], wk.hid2[:, :width])

    def emit_middle(t, value):
        store_taps(value.astype(bf16), col, t, wk.masks, True)

    norm_backward(wk, wk.mid, tiles, 1, wk.hat2, wk.rstd2, emit_middle, wk.acc.at[1])
    matmul_cols(wk.mid, wk.kb[0], cols(col), width)
    for tap in range(9):
        grads[tap] = product_nt(col[tap * C : (tap + 1) * C, :width], wk.hid1[:, :width])
    norm_backward(wk, wk.mid, tiles, 0, wk.hat1, wk.rstd1, part_store, wk.acc.at[0])

    lane = lax.broadcasted_iota(jnp.int32, (1, LANES), 1)
    total = jnp.zeros((C, LANES), f32)
    for k in range(4):
        one = jnp.sum(wk.acc[k // 2, k % 2], axis=1, keepdims=True)
        total = total + jnp.where(lane == k, one, 0.0)
    gn_out[...] = total


def raw_gradient(wk, grads, sq):
    rows = 32

    @pl.loop(0, C // rows)
    def _(j):
        at = pl.ds(pl.multiple_of(j * rows, rows), rows)
        for conv in range(2):
            first = jnp.zeros((rows, C), f32)
            second = jnp.zeros((rows, C), f32)
            for tap in range(9):
                g = grads[conv * 9 + tap, at, :]
                k = wk.ktp[at, conv * FAN + tap * C : conv * FAN + (tap + 1) * C].astype(f32)
                first = first + g
                second = second + g * k
            first = jnp.sum(first, axis=1, keepdims=True) * (1.0 / FAN)
            second = jnp.sum(second, axis=1, keepdims=True)
            rs = wk.rs[conv, at, 0:1]
            squares = jnp.zeros((rows, C), f32)
            for tap in range(9):
                g = grads[conv * 9 + tap, at, :]
                k = wk.ktp[at, conv * FAN + tap * C : conv * FAN + (tap + 1) * C].astype(f32)
                value = (g - first - k * second) * rs
                grads[conv * 9 + tap, at, :] = value
                squares = squares + value * value
            fold = squares[:, :LANES] + squares[:, LANES:]
            sq[...] += fold.reshape(rows // 8, 8, LANES).sum(0)


def whole_sum(tile):
    return jnp.sum(jnp.sum(tile, axis=1, keepdims=True), axis=0, keepdims=True)


WORK_SCRATCH = [
    pltpu.VMEM((2, C, FAN), bf16),
    pltpu.VMEM((FAN, AUG * PIX), bf16),
    pltpu.VMEM((C, AUG * PIX), f32),
    pltpu.VMEM((C, AUG * PIX), f32),
    pltpu.VMEM((C, AUG * PIX), f32),
    pltpu.VMEM((C, AUG * PIX), bf16),
    pltpu.VMEM((C, AUG * PIX), bf16),
    pltpu.VMEM((LANES, LANES), f32),
    pltpu.VMEM((LANES, LANES), f32),
    pltpu.VMEM((LANES, LANES), f32),
    pltpu.VMEM((LANES, LANES), f32),
    pltpu.VMEM((LANES, LANES), f32),
    pltpu.VMEM((4, C, LANES), f32),
    pltpu.VMEM((2, C, LANES), f32),
    pltpu.VMEM((2, 2, C, LANES), f32),
]
WORK_NAMES = (
    "kb",
    "col",
    "mid",
    "hat1",
    "hat2",
    "hid1",
    "hid2",
    "stat",
    "stat2",
    "rstd1",
    "rstd2",
    "ones",
    "gn",
    "rs",
    "acc",
)


def make_work(ktp, refs):
    wk = Work()
    wk.ktp = ktp
    for name, ref in zip(WORK_NAMES, refs):
        setattr(wk, name, ref)
    return wk


def compute_kernel(
    x, cot, xt, ct, ktp, wl, sg, block, part, clipped, test, clipped_gn, test_gn, raw, raw_gn, length, *scratch
):
    examples = x.shape[0]
    wk = make_work(ktp, scratch[:-2])
    tgrad, sq = scratch[-2:]
    fill_work(wk)
    unpack_params(wk)
    turn_kernels(wk)
    gn_tmp = test_gn
    unit(
        wk,
        lambda t: xt[...].astype(f32),
        lambda t: ct[...].astype(f32),
        lambda t: sg[...],
        1,
        tgrad,
        gn_tmp,
        None,
        None,
    )
    raw_gradient(wk, tgrad, sq)

    @pl.loop(0, 18)
    def _(k):
        test[k] = tgrad[k].astype(bf16)

    sq[...] = jnp.zeros_like(sq)

    @pl.loop(0, examples)
    def _(e):
        def block_store(t, value):
            block[e, :, lane_tile(t)] = value.astype(bf16)

        def part_store(t, value):
            part[e, :, lane_tile(t)] = value.astype(bf16)

        unit(
            wk,
            lambda t: x[e, :, lane_tile(t)].astype(f32),
            lambda t: cot[e, :, lane_tile(t)].astype(f32),
            lambda t: wl[e, :, lane_tile(t)],
            8,
            raw.at[e],
            raw_gn.at[e],
            block_store,
            part_store,
        )
        sq[...] = jnp.zeros_like(sq)
        raw_gradient(wk, raw.at[e], sq)
        gn = raw_gn[e]
        square = whole_sum(sq[...]) + whole_sum(gn * gn)
        length[e] = jnp.broadcast_to(jnp.sqrt(square), (8, LANES))

    factors = [CLIP / jnp.maximum(length[e][0:1, 0:1], CLIP) for e in range(examples)]
    total = factors[0] * raw_gn[0]
    for e in range(1, examples):
        total = total + factors[e] * raw_gn[e]
    clipped_gn[...] = total

    @pl.loop(0, 18)
    def _(k):
        total = factors[0] * raw[0, k]
        for e in range(1, examples):
            total = total + factors[e] * raw[e, k]
        clipped[k] = total.astype(bf16)


def compute(x, cot, xt, ct, ktp, wl, sg):
    examples = x.shape[0]
    out = jax.ShapeDtypeStruct
    shapes = (
        out(x.shape, bf16),
        out(x.shape, bf16),
        out((18, C, C), bf16),
        out((18, C, C), bf16),
        out((C, LANES), f32),
        out((C, LANES), f32),
        out((examples, 18, C, C), f32),
        out((examples, C, LANES), f32),
        out((examples, 8, LANES), f32),
    )
    spec = pl.BlockSpec(memory_space=pltpu.VMEM)
    return pl.pallas_call(
        compute_kernel,
        out_shape=shapes,
        in_specs=[spec] * 7,
        out_specs=(spec,) * 9,
        scratch_shapes=WORK_SCRATCH + [pltpu.VMEM((18, C, C), f32), pltpu.VMEM((8, LANES), f32)],
        compiler_params=pltpu.CompilerParams(vmem_limit_bytes=58 << 20),
    )(x, cot, xt, ct, ktp, wl, sg)


def peer_copy(src, dst, send, recv, **where):
    return pltpu.make_async_remote_copy(
        src_ref=src, dst_ref=dst, send_sem=send, recv_sem=recv, device_id=where, device_id_type=MESH
    )


def greet(peers):
    barrier = pltpu.get_barrier_semaphore()
    for where in peers:
        pl.semaphore_signal(barrier, inc=1, device_id=where, device_id_type=MESH)
    pl.semaphore_wait(barrier, len(peers))


def gather_kernel(
    images, cots, timg, tcot, kshard, x, cot, xt, ct, ktp, s_a2a, r_a2a, s_own, r_up, r_dn, s_up, s_dn, s_core, r_core, s_loc
):
    n = 8
    me = lax.axis_index("narrow")
    z, c = me // 2, me % 2
    examples = x.shape[0]
    chans = images.shape[1]
    mine = pl.ds(pl.multiple_of(me * chans, chans), chans)
    greet([{"narrow": lax.rem(me + k, n)} for k in range(1, n)])

    def rows(zz):
        return pl.ds(pl.multiple_of((zz * 2 + c) * chans, chans), chans)

    sibling = me + 1 - 2 * c

    def up(step):
        src = kshard if step == 0 else ktp.at[rows(z - step)]
        return peer_copy(src, ktp.at[rows(z - step)], s_up.at[step], r_up.at[step], narrow=me + 2)

    def down(step):
        src = kshard if step == 0 else ktp.at[rows(z + step)]
        return peer_copy(src, ktp.at[rows(z + step)], s_dn.at[step], r_dn.at[step], narrow=me - 2)

    def across(slot, zz):
        src = kshard if slot == 0 else ktp.at[rows(zz)]
        return peer_copy(src, ktp.at[rows(zz)], s_core.at[slot], r_core.at[slot], narrow=sibling)

    @pl.when(z < 3)
    def _():
        up(0).start()

    @pl.when(z > 0)
    def _():
        down(0).start()

    across(0, z).start()
    pairs = ((timg, xt), (tcot, ct), (images, x), (cots, cot))
    local = [pltpu.make_async_copy(kshard, ktp.at[mine], s_loc.at[4])]
    sends = []
    for a, (src, dst) in enumerate(pairs):
        for k in range(n):
            to = lax.rem(me + k, n)
            if a < 2:
                piece = src.at[:, pl.ds(pl.multiple_of(to * LANES, LANES), LANES)]
                place = dst.at[mine]
            else:
                piece = src.at[pl.ds(to * examples, examples)]
                place = dst.at[:, mine]
            if k == 0:
                local.append(pltpu.make_async_copy(piece, place, s_loc.at[a]))
            else:
                sends.append(peer_copy(piece, place, s_a2a.at[a, k - 1], r_a2a.at[a, k - 1], narrow=to))
    for copy in local + sends:
        copy.start()
    for step in range(1, 4):

        @pl.when(z - step >= 0)
        def _():
            up(step - 1).wait_recv()
            across(step, z - step).start()
            if step < 3:

                @pl.when(z < 3)
                def _():
                    up(step).start()

        @pl.when(z + step <= 3)
        def _():
            down(step - 1).wait_recv()
            across(3 + step, z + step).start()
            if step < 3:

                @pl.when(z > 0)
                def _():
                    down(step).start()

    for step in range(3):

        @pl.when((z < 3) & (z - step >= 0))
        def _():
            up(step).wait_send()

        @pl.when((z > 0) & (z + step <= 3))
        def _():
            down(step).wait_send()

    across(0, z).wait()
    for step in range(1, 4):

        @pl.when(z - step >= 0)
        def _():
            across(step, z - step).wait()

        @pl.when(z + step <= 3)
        def _():
            across(3 + step, z + step).wait()

    for copy in local + sends:
        copy.wait()


def gather(images, cots, timg, tcot, kshard, examples):
    out = jax.ShapeDtypeStruct
    anyspace = pl.BlockSpec(memory_space=pl.ANY)
    dma = pltpu.SemaphoreType.DMA
    return pl.pallas_call(
        gather_kernel,
        out_shape=(
            out((examples, C, AUG * PIX), bf16),
            out((examples, C, AUG * PIX), bf16),
            out((C, LANES), bf16),
            out((C, LANES), bf16),
            out((C, KCOLS + LANES), bf16),
        ),
        in_specs=[anyspace] * 5,
        out_specs=(anyspace,) * 5,
        scratch_shapes=[
            dma((4, 7)),
            dma((4, 7)),
            dma,
            dma((3,)),
            dma((3,)),
            dma((3,)),
            dma((3,)),
            dma((7,)),
            dma((7,)),
            dma((5,)),
        ],
        compiler_params=pltpu.CompilerParams(collective_id=0, has_side_effects=True),
    )(images, cots, timg, tcot, kshard)


def reduce_kernel(
    block,
    part,
    clip_conv,
    test_conv,
    clip_gn,
    test_gn,
    raw,
    raw_gn,
    length,
    ob,
    op,
    red,
    figures,
    cb,
    cg,
    half,
    wb,
    quarter,
    zb,
    dt,
    s_back,
    r_back,
    s_core,
    r_core,
    s_wide,
    r_wide,
    s_z,
    r_z,
    s_f,
    r_f,
    s_fin,
    r_fin,
    s_fig,
    r_fig,
    s_loc,
):
    n = 8
    me = lax.axis_index("narrow")
    w = lax.axis_index("wide")
    z, c = me // 2, me % 2
    sibling = me + 1 - 2 * c
    examples = block.shape[0]
    chans = ob.shape[1]
    greet(
        [{"narrow": lax.rem(me + k, n)} for k in range(1, n)]
        + [{"wide": lax.rem(w + k, 4)} for k in range(1, 4)]
    )
    core = []
    for a, (conv, gn) in enumerate(((clip_conv, clip_gn), (test_conv, test_gn))):
        core.append(peer_copy(conv.at[:, :, 1 - c], cb.at[a], s_core.at[a, 0], r_core.at[a, 0], narrow=sibling))
        core.append(peer_copy(gn.at[:, 1 - c], cg.at[a], s_core.at[a, 1], r_core.at[a, 1], narrow=sibling))
    for copy in core:
        copy.start()
    back = []
    for a, (src, dst) in enumerate(((block, ob), (part, op))):
        for k in range(n):
            to = lax.rem(me + k, n)
            piece = src.at[:, pl.ds(pl.multiple_of(to * chans, chans), chans)]
            place = dst.at[pl.ds(me * examples, examples)]
            if k == 0:
                back.append(pltpu.make_async_copy(piece, place, s_loc.at[a]))
            else:
                back.append(peer_copy(piece, place, s_back.at[a, k - 1], r_back.at[a, k - 1], narrow=to))
    for copy in back:
        copy.start()
    for copy in core:
        copy.wait()
    for a, (conv, gn) in enumerate(((clip_conv, clip_gn), (test_conv, test_gn))):
        for k in range(2):

            @pl.loop(0, 9)
            def _(tap):
                total = conv[k * 9 + tap, :, c].astype(f32) + cb[a, k * 9 + tap].astype(f32)
                half[a, k * 2, tap] = total[:, :, :LANES].astype(bf16)
                half[a, k * 2 + 1, tap] = total[:, :, LANES:].astype(bf16)

        half[a, 0, 9] = (gn[:, c].astype(f32) + cg[a].astype(f32)).astype(bf16)
        for q in range(1, 4):
            half[a, q, 9] = jnp.zeros_like(half[a, q, 9])
    wide = []
    for k in range(1, 4):
        to = lax.rem(w + k, 4)
        wide.append(peer_copy(half.at[:, to], wb.at[k - 1], s_wide.at[k - 1], r_wide.at[k - 1], wide=to))
    for copy in wide:
        copy.start()
    for copy in wide:
        copy.wait()
    for a in range(2):

        @pl.loop(0, 10)
        def _(tap):
            total = half[a, w, tap].astype(f32)
            for k in range(3):
                total = total + wb[k, a, tap].astype(f32)
            quarter[a, tap] = total.astype(bf16)

    line = []
    for k in range(1, 4):
        to = lax.rem(z + k, 4)
        line.append(
            peer_copy(quarter.at[:, :, to], zb.at[k - 1], s_z.at[k - 1], r_z.at[k - 1], narrow=to * 2 + c)
        )
    for copy in line:
        copy.start()
    for copy in line:
        copy.wait()

    def final(a, tap):
        total = quarter[a, tap, z].astype(f32)
        for k in range(3):
            total = total + zb[k, a, tap].astype(f32)
        return total.astype(bf16)

    @pl.loop(0, 10)
    def _(tap):
        red[w, tap] = final(0, tap)
        dt[c, w, z, tap] = final(1, tap)

    finals = []
    for k in range(1, 4):
        to = lax.rem(w + k, 4)
        finals.append(peer_copy(red.at[w], red.at[w], s_f.at[0, k - 1], r_f.at[0, k - 1], wide=to))
    spread = []
    for k in range(1, 4):
        to = lax.rem(z + k, 4)
        own = dt.at[c, w, z]
        spread.append(peer_copy(own, own, s_f.at[1, k - 1], r_f.at[1, k - 1], narrow=to * 2 + c))
    for copy in spread + finals:
        copy.start()
    for copy in spread:
        copy.wait()
    fin = []
    for k in range(1, 4):
        to = lax.rem(w + k, 4)
        fin.append(peer_copy(dt.at[c, w], dt.at[c, w], s_fin.at[k - 1], r_fin.at[k - 1], wide=to))
    for copy in fin:
        copy.start()
    for copy in fin:
        copy.wait()
    last = peer_copy(dt.at[c], dt.at[c], s_fin.at[3], r_fin.at[3], narrow=sibling)
    last.start()
    last.wait()

    own_rows = lax.broadcasted_iota(jnp.int32, (8, LANES), 0)
    zero = jnp.zeros((chans, LANES), f32)

    def visit(index, carry):
        q, rest = index // 8, index % 8
        zz, cc = rest // 2, rest % 2
        at = pl.ds(pl.multiple_of(rest * chans, chans), chans)
        square = carry[0]
        sums = list(carry[1:])
        for tap in range(9):
            d = dt[cc, q, zz, tap].astype(f32)
            square = square + d * d
            for e in range(examples):
                sums[e] = sums[e] + d * raw[e, (q // 2) * 9 + tap, at, pl.ds(pl.multiple_of((q % 2) * LANES, LANES), LANES)]
        return (square, *sums)

    totals = lax.fori_loop(0, 32, visit, (zero,) * (examples + 1))

    def visit_gn(rest, carry):
        at = pl.ds(pl.multiple_of(rest * chans, chans), chans)
        d = dt[rest % 2, 0, rest // 2, 9].astype(f32)
        return (carry[0] + d * d,) + tuple(carry[1 + e] + d * raw_gn[e, at, :] for e in range(examples))

    totals = lax.fori_loop(0, 8, visit_gn, totals)
    dir_sq = whole_sum(totals[0])
    params = 18 * C * C + 4 * C
    for e in range(examples):
        size = length[e]
        factor = CLIP / jnp.maximum(size, CLIP)
        influence = factor * whole_sum(totals[1 + e]) * math.sqrt(params) / (CLIP * jnp.sqrt(dir_sq + 1e-06))
        figures[me, e] = jnp.where(own_rows == 0, size, influence)
    figs = []
    for k in range(1, n):
        figs.append(
            peer_copy(figures.at[me], figures.at[me], s_fig.at[k - 1], r_fig.at[k - 1], narrow=lax.rem(me + k, n))
        )
    for copy in figs:
        copy.start()
    for copy in figs + finals + back:
        copy.wait()


def reduce_all(block, part, clip_conv, test_conv, clip_gn, test_gn, raw, raw_gn, length, chans):
    examples = block.shape[0]
    out = jax.ShapeDtypeStruct
    anyspace = pl.BlockSpec(memory_space=pl.ANY)
    vmem = pl.BlockSpec(memory_space=pltpu.VMEM)
    dma = pltpu.SemaphoreType.DMA
    whole = (18, 4, 2, chans, C)
    return pl.pallas_call(
        reduce_kernel,
        out_shape=(
            out((8 * examples, chans, AUG * PIX), bf16),
            out((8 * examples, chans, AUG * PIX), bf16),
            out((4, 10, chans, LANES), bf16),
            out((8, examples, 8, LANES), f32),
        ),
        in_specs=[anyspace, anyspace] + [vmem] * 7,
        out_specs=(anyspace, anyspace, vmem, vmem),
        scratch_shapes=[
            pltpu.VMEM((2, 18, 4, chans, C), bf16),
            pltpu.VMEM((2, 4, chans, LANES), bf16),
            pltpu.VMEM((2, 4, 10, 4, chans, LANES), bf16),
            pltpu.VMEM((3, 2, 10, 4, chans, LANES), bf16),
            pltpu.VMEM((2, 10, 4, chans, LANES), bf16),
            pltpu.VMEM((3, 2, 10, chans, LANES), bf16),
            pltpu.VMEM((2, 4, 4, 10, chans, LANES), bf16),
            dma((2, 7)),
            dma((2, 7)),
            dma((2, 2)),
            dma((2, 2)),
            dma((3,)),
            dma((3,)),
            dma((3,)),
            dma((3,)),
            dma((2, 3)),
            dma((2, 3)),
            dma((4,)),
            dma((4,)),
            dma((7,)),
            dma((7,)),
            dma((2,)),
        ],
        compiler_params=pltpu.CompilerParams(collective_id=1, has_side_effects=True, vmem_limit_bytes=58 << 20),
    )(
        block,
        part,
        clip_conv.reshape(whole),
        test_conv.reshape(whole),
        clip_gn.astype(bf16).reshape(4, 2, chans, LANES),
        test_gn.astype(bf16).reshape(4, 2, chans, LANES),
        raw,
        raw_gn,
        length,
    )


def pieces(v):
    high = lax.reduce_precision(v, 8, 7)
    rest = v - high
    mid = lax.reduce_precision(rest, 8, 7)
    low = rest - mid
    return high.astype(bf16), mid.astype(bf16), low.astype(bf16)


def kernel_rows(conv_weight, gn_params):
    chans = conv_weight.shape[4]
    centre = conv_weight - jnp.mean(conv_weight, axis=(1, 2, 3), keepdims=True)
    spread = jnp.mean(centre * centre, axis=(1, 2, 3), keepdims=True)
    scale = lax.rsqrt(FAN * spread + 1e-06)
    kernels = (centre * scale).astype(bf16).reshape(2, FAN, chans)
    rows = kernels.transpose(2, 0, 1).reshape(chans, KCOLS)
    small = jnp.concatenate([gn_params.T, scale.reshape(2, chans).T, jnp.zeros((chans, 2), f32)], 1)
    tail = jnp.concatenate(list(pieces(small)) + [jnp.zeros((chans, LANES - 24), bf16)], 1)
    return jnp.concatenate([rows, tail], 1)


def adamw(weight, first, second, grad, correction, rate, decay):
    first_new = 0.5 * first + 0.5 * grad
    second_new = 0.5 * second + 0.5 * grad * grad
    update = first_new / correction / (jnp.sqrt(second_new / correction) + 1e-08)
    return (weight - rate * (update + decay * weight), first_new, second_new)


def plain_gather(images, cots, timg, tcot, kshard, narrow):
    share = narrow // 8
    x = lax.all_to_all(images, "narrow", 0, 1, tiled=True)
    cot = lax.all_to_all(cots, "narrow", 0, 1, tiled=True)
    ktp = lax.all_gather(kshard, "narrow", axis=0, tiled=True)
    own = (lax.axis_index("narrow") // share) * LANES

    def pick(v):
        return lax.dynamic_slice_in_dim(lax.all_gather(v, "narrow", axis=0, tiled=True), own, LANES, 1)

    return x, cot, pick(timg), pick(tcot), ktp


def plain_reduce(block, part, clip_conv, test_conv, clip_gn, test_gn, raw, raw_gn, length, chans):
    examples = block.shape[0]
    ob = lax.all_to_all(block, "narrow", 1, 0, tiled=True)
    op = lax.all_to_all(part, "narrow", 1, 0, tiled=True)
    own = lax.axis_index("narrow") * chans
    rows = lax.psum(clip_conv, ("wide", "narrow"))
    rows = lax.dynamic_slice_in_dim(rows, own, chans, 1)
    gn_rows = lax.dynamic_slice_in_dim(lax.psum(clip_gn.astype(bf16), ("wide", "narrow")), own, chans, 0)
    red = rows.reshape(2, 9, chans, 2, LANES).transpose(0, 3, 1, 2, 4).reshape(4, 9, chans, LANES)
    red = jnp.concatenate([red, jnp.broadcast_to(gn_rows, (4, 1, chans, LANES))], 1)
    d = lax.psum(test_conv, ("wide", "narrow")).astype(f32)
    d_gn = lax.psum(test_gn.astype(bf16), ("wide", "narrow")).astype(f32)
    dir_sq = jnp.sum(d * d) + jnp.sum(d_gn * d_gn)
    inner = jnp.sum(raw * d, axis=(1, 2, 3)) + jnp.sum(raw_gn * d_gn, axis=(1, 2))
    size = length[:, 0, 0]
    factor = CLIP / jnp.maximum(size, CLIP)
    influence = factor * inner * math.sqrt(18 * C * C + 4 * C) / (CLIP * jnp.sqrt(dir_sq + 1e-06))
    figures = lax.all_gather(jnp.stack([size, influence], 1), "narrow", axis=0)
    return ob, op, red, figures[:, :, :, None]


def local(
    images,
    cotangent,
    test_images,
    test_cotangent,
    pair_index,
    example_count,
    aug_count,
    conv_weight,
    gn_params,
    conv_moment1,
    conv_moment2,
    gn_moment1,
    gn_moment2,
    noise_conv,
    noise_gn,
    step_count,
):
    n_wide, narrow = lax.axis_size("wide"), lax.axis_size("narrow")
    held, chans = images.shape[0], images.shape[1]
    examples = held // narrow
    share = narrow // 8
    me = lax.axis_index("narrow")
    slots = jnp.arange(AUG, dtype=jnp.int32)
    live = jnp.arange(held, dtype=jnp.int32) < example_count[0]
    weights = jnp.where(
        live[:, None] & (slots[None, :] < aug_count[:, None]),
        1.0 / aug_count.astype(f32)[:, None],
        f32(0.0),
    )
    pixels = jnp.repeat(weights, PIX, axis=1)
    pairs = pair_index % AUG
    signs = jnp.sum((pairs[:, 0:1] == slots[None, :]).astype(f32), 0) - jnp.sum(
        (pairs[:, 1:2] == slots[None, :]).astype(f32), 0
    )
    sign_pixels = jnp.repeat(signs, PIX).reshape(8, LANES) * (1.0 / share)
    wl = lax.dynamic_slice_in_dim(pixels, me * examples, examples, 0)[:, None, :]
    sg = lax.dynamic_slice_in_dim(sign_pixels, me // share, 1, 0)
    kshard = kernel_rows(conv_weight, gn_params)
    timg, tcot = test_images[0], test_cotangent[0]
    direct = n_wide == 4 and narrow == 8
    if direct:
        x, cot, xt, ct, ktp = gather(images, cotangent, timg, tcot, kshard, examples)
    else:
        x, cot, xt, ct, ktp = plain_gather(images, cotangent, timg, tcot, kshard, narrow)
    block, part, clip_conv, test_conv, clip_gn, test_gn, raw, raw_gn, length = compute(x, cot, xt, ct, ktp, wl, sg)
    send = reduce_all if direct else plain_reduce
    block_out, op, red, figures = send(
        block, part, clip_conv, test_conv, clip_gn, test_gn, raw, raw_gn, length, chans
    )
    input_grad = cotangent.astype(f32) * pixels[:, None, :] + op.astype(f32)
    lengths = figures[:, :, 0, 0].reshape(held)
    influence = figures[:, :, 1, 0].reshape(held)
    sum_conv = red[:, :9].reshape(2, 2, 9, chans, LANES).transpose(0, 2, 1, 4, 3)
    sum_conv = sum_conv.reshape(2, 3, 3, C, chans).astype(f32)
    sum_norm = red[0, 9, :, :4].T.astype(f32)
    total = held * n_wide
    noisy_conv = (sum_conv + math.sqrt(total) * noise_conv) / total
    noisy_norm = (sum_norm + math.sqrt(total) * noise_gn) / total
    correction = 1.0 - jnp.power(f32(0.5), step_count[0].astype(f32))
    conv_new, conv_first, conv_second = adamw(
        conv_weight, conv_moment1, conv_moment2, noisy_conv, correction, 1.0 / math.sqrt(9 * C), 0.1
    )
    gn_new, gn_first, gn_second = adamw(
        gn_params, gn_moment1, gn_moment2, noisy_norm, correction, 0.1, 0.0
    )
    return (
        block_out,
        input_grad,
        lengths,
        influence,
        conv_new,
        conv_new.astype(bf16),
        conv_first,
        conv_second,
        gn_new,
        gn_first,
        gn_second,
    )


def solution(mesh):
    in_specs = (
        P("wide", "narrow", None),
        P("wide", "narrow", None),
        P("wide", "narrow", None),
        P("wide", "narrow", None),
        P("wide", None),
        P("wide"),
        P("wide"),
        P(None, None, None, None, "narrow"),
        P(None, "narrow"),
        P(None, None, None, None, "narrow"),
        P(None, None, None, None, "narrow"),
        P(None, "narrow"),
        P(None, "narrow"),
        P(None, None, None, None, "narrow"),
        P(None, "narrow"),
        P(),
    )
    out_specs = (
        P("wide", "narrow", None),
        P("wide", "narrow", None),
        P("wide"),
        P("wide"),
        P(None, None, None, None, "narrow"),
        P(None, None, None, None, "narrow"),
        P(None, None, None, None, "narrow"),
        P(None, None, None, None, "narrow"),
        P(None, "narrow"),
        P(None, "narrow"),
        P(None, "narrow"),
    )
    return jax.shard_map(local, mesh=mesh, in_specs=in_specs, out_specs=out_specs, check_vma=False)
```

time: 1290 us -> 269 us (0.21)
  matrix products: 412 us -> 0 us
  waiting for transfers between devices: 321 us -> 0 us
  local copies, waits for them, and re-layouts: 329 us -> 9.23 us
  Pallas kernels: 0 us -> 245 us
  other arithmetic: 149 us -> 12.5 us
  blocking collectives: 45.7 us -> 0 us
  between operations: 19.2 us -> 2.28 us
    dot_general x54 -> x0, matrix products: 412 us -> none  [the longest x18 271 us: transposed_product(): lax.dot_general(window, kernel[row, col], (((1,), (1,)), ((), ())), prefe...]
    reduce_scatter x2 -> x0, waiting for transfers between devices: 306 us -> none  [input_grad_share(): lax.psum_scatter(partial_sum, 'narrow', scatter_dimension=3, tiled=True)]
    pallas_call x0 -> x3, Pallas kernels: none -> 245 us  [the longest x1 102 us: reduce_all(): pl.pallas_call(reduce_kernel, out_shape=(out((8 * examples, chans, AUG *...]
    slice x7 -> x2, local copies, waits for them, and re-layouts: 132 us -> 2.18 us  [the longest x1 1.14 us: local(): red[:, :9].reshape(2, 2, 9, chans, LANES).transpose(0, 2, 1, 4, 3)]
    reduce_sum x24 -> x3, other arithmetic: 79 us -> 2.54 us  [the longest x1 1.27 us: kernel_rows(): spread = jnp.mean(centre * centre, axis=(1, 2, 3), keepdims=True)]
    psum x4 -> x0, blocking collectives: 45.7 us -> none  [the longest x1 14.1 us: local(): inner, dir_sq = lax.psum((inner_local, dir_local), 'narrow')]
    reshape x2 -> x3, local copies, waits for them, and re-layouts: 43.9 us -> 0.46 us  [the longest x1 0.34 us: kernel_rows(): kernels = (centre * scale).astype(bf16).reshape(2, FAN, chans)]
    convert_element_type x10 -> x7, other arithmetic: 46.3 us -> 6.72 us  [the longest x1 1.68 us: local(): conv_new.astype(bf16)]
  transfers between devices with their start and end apart: 6 -> 0, of which waited for: 3 -> 0; matrix products, arithmetic and copies ran while one was open for 49% -> 0% of each run, Pallas kernels for 0% -> 0%
where the time goes in v1:
time: 269 us
  Pallas kernels  245 us (91%)
  other arithmetic  12.5 us (5%)
  local copies, waits for them, and re-layouts  9.23 us (3%)
    pallas_call x1, Pallas kernels, reduce_all(): pl.pallas_call(reduce_kernel, out_shape=(out((8 * examples, chans, AUG *...  102 us
    pallas_call x1, Pallas kernels, gather(): pl.pallas_call(gather_kernel, out_shape=(out((examples, C, AUG * PIX), bf...  78.1 us
    pallas_call x1, Pallas kernels, compute(): pl.pallas_call(compute_kernel, out_shape=shapes, in_specs=[spec] * 7, out...  64.8 us

profile of v1, /device:TPU:0, one launch (start us, length us, event | category | flops | bytes accessed | tf_op | source)
XLA Modules:
  0.0 268.8 jit_solution(783953691603545447)
XLA Ops:
  0.6 1.2 reduce_sum.36
  1.8 1.3 multiply_reduce_fusion
  3.1 0.1 pad.2.clone
  3.2 0.8 maximum_maximum_fusion
  4.0 0.1 copy.51
  4.0 0.1 copy.52
  4.1 1.2 multiply_convert_fusion
  5.3 0.3 copy.49
  5.6 0.0 copy-start.14
  5.6 0.3 reshape.81
  5.9 0.0 copy-start.13
  6.0 0.8 concatenate.7.kshard
  6.8 78.1 %shard_map.239 = (bf16[2,256,1024]{2,1,0:T(8,128)(2,1)}, bf16[2,256,1024]{2,1,0:T(8,128)(2,1)}, bf16[256,128]{1,0:T(8,128)(2,1)}, bf16[256,128]{1,0:T(8,128)(2,1)}, bf16[256,4736]{1,0:T(8,128)(2,1)}) custom-call(bf16[16,32,1024]{2,1,0:T(8,128)(2,1)} %images.1, bf16[16,32,1024]{2,1,0:T(8,128)(2,1)} %cots.1, bf16[32,1024]{1,0:T(8,128)(2,1)} %bitcast.44, ...), custom_call_target="tpu_custom_call" | custom-call | tf_op jit(solution)/shard_map/pallas_call | solution.py:518
  85.5 0.0 copy-done.14
  85.6 0.1 fusion.2
  85.6 0.1 broadcast_in_dim.41
  85.7 0.1 reshape.83
  85.8 0.0 copy-start.7
  85.9 0.6 broadcast_in_dim.42.wl
  86.5 0.0 copy-done.13
  86.5 0.1 convert_reduce_fusion
  86.6 0.1 sub.40
  86.7 0.1 broadcast_in_dim.43
  86.7 0.1 broadcast_in_dim.44
  86.8 0.5 constant_dynamic-slice_fusion.sg
  87.3 64.8 %shard_map.240 = (bf16[2,256,1024]{2,1,0:T(8,128)(2,1)}, bf16[2,256,1024]{2,1,0:T(8,128)(2,1)}, bf16[18,256,256]{2,1,0:T(8,128)(2,1)}, bf16[18,256,256]{2,1,0:T(...) custom-call(bf16[2,256,1024]{2,1,0:T(8,128)(2,1)} %get-tuple-element, ...), custom_call_target="tpu_custom_call" | custom-call | tf_op jit(solution)/shard_map/pallas_call | solution.py:389
  152.1 0.0 copy-done.7
  152.1 1.5 convert_element_type.68
  153.7 1.5 convert_element_type.69
  155.2 101.9 %shard_map.241 = (bf16[16,32,1024]{2,1,0:T(8,128)(2,1)}, bf16[16,32,1024]{2,1,0:T(8,128)(2,1)}, bf16[4,10,32,128]{3,2,1,0:T(8,128)(2,1)}, f32[8,2,8,128]{3,2,1,0:T(8,128)}) custom-call(bf16[2,256,1024]{2,1,0:T(8,128)(2,1)} %get-tuple-element.34.block, bf16[2,256,1024]{2,1,0:T(8,128)(2,1)} %get-tuple-element.35.part, bf16[18,4,2,32,256]{4,3,2,1,0:T(8,128)(2,1)} %bitcast.37, ...), custom_call_target="tpu_custom_call" | custom-call | tf_op jit(solution)/shard_map/pallas_call | solution.py:738
  257.2 0.0 copy-start
  257.2 0.0 copy-start.4
  257.2 0.0 copy-start.5
  257.2 0.0 copy-start.6
  257.2 1.1 slice.22
  258.3 0.1 convert_bitcast_fusion
  258.4 0.5 copy.54
  258.9 0.5 reshape.88
  260.0 0.0 copy-done
  260.1 0.0 copy-done.4
  260.1 0.0 copy-done.5
  260.1 0.0 copy-done.6
  260.1 0.0 copy-start.1
  260.1 0.0 copy-start.3
  260.1 0.0 copy-start.8
  260.1 1.7 fusion.6
  261.8 0.0 copy-done.1
  261.8 0.6 copy-done.3
  262.4 0.0 copy-done.8
  262.4 0.0 copy-start.12
  262.4 0.0 copy-start.2
  262.4 1.8 convert_add_fusion
  264.2 0.7 slice_convert_fusion
  264.9 0.1 copy.55
  264.9 0.0 copy-done.9
  264.9 0.0 copy-done.10
  264.9 0.0 copy-done.11
  264.9 0.0 copy-done.12
  265.0 0.6 multiply_subtract_fusion.1
  265.6 1.0 slice_reduce_fusion
  266.6 0.6 reshape_squeeze.6
  267.2 0.6 reshape_squeeze.7
  267.8 0.0 copy-done.2
  267.8 1.0 copy.60
  (15 shorter events, 0.1 us)
Async XLA Ops:
  5.6 79.9 %copy-start.14 = (s32[16]{0:T(128)S(1)}, s32[16]{0:T(128)}, u32[]{:S(2)}) copy-start(s32[16]{0:T(128)} %param.22) | copy-start | bytes 196
  5.9 80.5 %copy-start.13 = (s32[8,2]{0,1:T(2,128)S(1)}, s32[8,2]{0,1:T(2,128)}, u32[]{:S(2)}) copy-start(s32[8,2]{0,1:T(2,128)} %param.20) | copy-start | bytes 196
  85.8 66.3 %copy-start.7 = (f32[16,1024]{1,0:T(8,128)}, f32[16,1024]{1,0:T(8,128)S(1)}, u32[]{:S(2)}) copy-start(f32[16,1024]{1,0:T(8,128)S(1)} %reshape.83) | copy-start | bytes 196612
  257.2 2.9 %copy-start = (f32[2,3,3,256,32]{3,4,2,1,0:T(8,128)S(1)}, f32[2,3,3,256,32]{3,4,2,1,0:T(8,128)}, u32[]{:S(2)}) copy-start(f32[2,3,3,256,32]{3,4,2,1,0:T(8,128)} %param.23) | copy-start | bytes 1769476
  257.2 2.9 %copy-start.4 = (f32[2,3,3,256,32]{3,4,2,1,0:T(8,128)S(1)}, f32[2,3,3,256,32]{3,4,2,1,0:T(8,128)}, u32[]{:S(2)}) copy-start(f32[2,3,3,256,32]{3,4,2,1,0:T(8,128)} %param.29) | copy-start | bytes 1769476
  257.2 2.9 %copy-start.5 = (f32[2,3,3,256,32]{3,4,2,1,0:T(8,128)S(1)}, f32[2,3,3,256,32]{3,4,2,1,0:T(8,128)}, u32[]{:S(2)}) copy-start(f32[2,3,3,256,32]{3,4,2,1,0:T(8,128)} %param.26) | copy-start | bytes 1769476
  257.2 2.9 %copy-start.6 = (f32[2,3,3,256,32]{3,4,2,1,0:T(8,128)S(1)}, f32[2,3,3,256,32]{3,4,2,1,0:T(8,128)}, u32[]{:S(2)}) copy-start(f32[2,3,3,256,32]{3,4,2,1,0:T(8,128)} %param.25) | copy-start | bytes 1769476
  260.1 1.7 copy-start.1
  260.1 2.3 copy-start.3
  260.1 2.3 copy-start.8
  262.4 2.6 copy-start.9
  262.4 2.6 copy-start.10
  262.4 2.6 copy-start.11
  262.4 2.6 copy-start.12
  262.4 5.4 %copy-start.2 = (bf16[16,32,1024]{2,1,0:T(8,128)(2,1)S(1)}, bf16[16,32,1024]{2,1,0:T(8,128)(2,1)}, u32[]{:S(2)}) copy-start(bf16[16,32,1024]{2,1,0:T(8,128)(2,1)} %get-tuple-element.78) | copy-start | bytes 3145732

commit v2 on v1

--- a/solution.py
+++ b/solution.py
@@ -178,15 +178,14 @@
         wk.kb[k // 9, :, (k % 9) * C : (k % 9 + 1) * C] = wk.ktp[:, at : at + C].T
 
 
-def unit(wk, x_load, cot_load, weight_load, tiles, grads, gn_out, block_store, part_store):
+def cols(ref, width):
+    return ref if width == ref.shape[1] else ref.at[:, :width]
+
+
+def forward(wk, x_load, tiles, block_store):
     width = tiles * LANES
-    col = wk.col
-
-    def cols(ref):
-        return ref if width == ref.shape[1] else ref.at[:, :width]
-
-    norm_forward(wk, x_load, tiles, 0, wk.hat1, wk.rstd1, wk.hid1, col)
-    matmul_cols(wk.mid, wk.ktp[:, :FAN], cols(col), width)
+    norm_forward(wk, x_load, tiles, 0, wk.hat1, wk.rstd1, wk.hid1, wk.col)
+    matmul_cols(wk.mid, wk.ktp[:, :FAN], cols(wk.col, width), width)
     norm_forward(
         wk,
         lambda t: wk.mid[:, lane_tile(t)],
@@ -195,28 +194,38 @@
         wk.hat2,
         wk.rstd2,
         wk.hid2,
-        col if block_store is not None else None,
+        wk.col if block_store is not None else None,
     )
     if block_store is not None:
-        matmul_cols(wk.mid, wk.ktp[:, FAN : 2 * FAN], cols(col), width)
+        matmul_cols(wk.mid, wk.ktp[:, FAN : 2 * FAN], cols(wk.col, width), width)
+
+        @pl.loop(0, tiles)
+        def _(t):
+            block_store(t, x_load(t) + wk.mid[:, lane_tile(t)])
+
+
+def backward_two(wk, cot_load, weight_load, tiles, grads):
+    width = tiles * LANES
 
     @pl.loop(0, tiles)
     def _(t):
-        if block_store is not None:
-            block_store(t, x_load(t) + wk.mid[:, lane_tile(t)])
-        store_taps((cot_load(t) * weight_load(t)).astype(bf16), col, t, wk.masks, True)
-
-    matmul_cols(wk.mid, wk.kb[1], cols(col), width)
+        store_taps((cot_load(t) * weight_load(t)).astype(bf16), wk.col, t, wk.masks, True)
+
+    matmul_cols(wk.mid, wk.kb[1], cols(wk.col, width), width)
     for tap in range(9):
-        grads[9 + tap] = product_nt(col[tap * C : (tap + 1) * C, :width], wk.hid2[:, :width])
+        grads[9 + tap] = product_nt(wk.col[tap * C : (tap + 1) * C, :width], wk.hid2[:, :width])
+
+
+def backward_one(wk, tiles, grads, gn_out, part_store):
+    width = tiles * LANES
 
     def emit_middle(t, value):
-        store_taps(value.astype(bf16), col, t, wk.masks, True)
+        store_taps(value.astype(bf16), wk.col, t, wk.masks, True)
 
     norm_backward(wk, wk.mid, tiles, 1, wk.hat2, wk.rstd2, emit_middle, wk.acc.at[1])
-    matmul_cols(wk.mid, wk.kb[0], cols(col), width)
+    matmul_cols(wk.mid, wk.kb[0], cols(wk.col, width), width)
     for tap in range(9):
-        grads[tap] = product_nt(col[tap * C : (tap + 1) * C, :width], wk.hid1[:, :width])
+        grads[tap] = product_nt(wk.col[tap * C : (tap + 1) * C, :width], wk.hid1[:, :width])
     norm_backward(wk, wk.mid, tiles, 0, wk.hat1, wk.rstd1, part_store, wk.acc.at[0])
 
     lane = lax.broadcasted_iota(jnp.int32, (1, LANES), 1)
@@ -312,18 +321,9 @@
     fill_work(wk)
     unpack_params(wk)
     turn_kernels(wk)
-    gn_tmp = test_gn
-    unit(
-        wk,
-        lambda t: xt[...].astype(f32),
-        lambda t: ct[...].astype(f32),
-        lambda t: sg[...],
-        1,
-        tgrad,
-        gn_tmp,
-        None,
-        None,
-    )
+    forward(wk, lambda t: xt[...].astype(f32), 1, None)
+    backward_two(wk, lambda t: ct[...].astype(f32), lambda t: sg[...], 1, tgrad)
+    backward_one(wk, 1, tgrad, test_gn, None)
     raw_gradient(wk, tgrad, sq)
 
     @pl.loop(0, 18)
@@ -340,17 +340,15 @@
         def part_store(t, value):
             part[e, :, lane_tile(t)] = value.astype(bf16)
 
-        unit(
+        forward(wk, lambda t: x[e, :, lane_tile(t)].astype(f32), 8, block_store)
+        backward_two(
             wk,
-            lambda t: x[e, :, lane_tile(t)].astype(f32),
             lambda t: cot[e, :, lane_tile(t)].astype(f32),
             lambda t: wl[e, :, lane_tile(t)],
             8,
             raw.at[e],
-            raw_gn.at[e],
-            block_store,
-            part_store,
         )
+        backward_one(wk, 8, raw.at[e], raw_gn.at[e], part_store)
         sq[...] = jnp.zeros_like(sq)
         raw_gradient(wk, raw.at[e], sq)
         gn = raw_gn[e]
@@ -409,21 +407,113 @@
     pl.semaphore_wait(barrier, len(peers))
 
 
-def gather_kernel(
-    images, cots, timg, tcot, kshard, x, cot, xt, ct, ktp, s_a2a, r_a2a, s_own, r_up, r_dn, s_up, s_dn, s_core, r_core, s_loc
-):
+class Exchange:
+    def __init__(self, place, conv, gn, refs, sems):
+        self.w, self.z, self.c, self.me = place
+        self.conv, self.gn = conv, gn
+        self.cb, self.cg, self.half, self.wb, self.quarter, self.zb = refs
+        s_core, r_core, s_wide, r_wide, s_z, r_z = sems
+        w, z, c = self.w, self.z, self.c
+        sibling = self.me + 1 - 2 * c
+        self.core = [
+            peer_copy(conv.at[:, :, 1 - c], self.cb, s_core.at[0], r_core.at[0], narrow=sibling),
+            peer_copy(gn.at[:, 1 - c], self.cg, s_core.at[1], r_core.at[1], narrow=sibling),
+        ]
+        self.wide, self.line = [], []
+        for k in range(1, 4):
+            to = lax.rem(w + k, 4)
+            self.wide.append(
+                peer_copy(self.half.at[to], self.wb.at[k - 1], s_wide.at[k - 1], r_wide.at[k - 1], wide=to)
+            )
+        for k in range(1, 4):
+            to = lax.rem(z + k, 4)
+            self.line.append(
+                peer_copy(
+                    self.quarter.at[:, to], self.zb.at[k - 1], s_z.at[k - 1], r_z.at[k - 1], narrow=to * 2 + c
+                )
+            )
+
+    def start_core(self):
+        for copy in self.core:
+            copy.start()
+
+    def start_wide(self):
+        for copy in self.core:
+            copy.wait()
+        half, c = self.half, self.c
+        for k in range(2):
+
+            @pl.loop(0, 9)
+            def _(tap):
+                total = self.conv[k * 9 + tap, :, c].astype(f32) + self.cb[k * 9 + tap].astype(f32)
+                half[k * 2, tap] = total[:, :, :LANES].astype(bf16)
+                half[k * 2 + 1, tap] = total[:, :, LANES:].astype(bf16)
+
+        half[0, 9] = (self.gn[:, c].astype(f32) + self.cg[...].astype(f32)).astype(bf16)
+        for q in range(1, 4):
+            half[q, 9] = jnp.zeros_like(half[q, 9])
+        for copy in self.wide:
+            copy.start()
+
+    def start_line(self):
+        for copy in self.wide:
+            copy.wait()
+
+        @pl.loop(0, 10)
+        def _(tap):
+            total = self.half[self.w, tap].astype(f32)
+            for k in range(3):
+                total = total + self.wb[k, tap].astype(f32)
+            self.quarter[tap] = total.astype(bf16)
+
+        for copy in self.line:
+            copy.start()
+
+    def finish(self, out):
+        for copy in self.line:
+            copy.wait()
+
+        @pl.loop(0, 10)
+        def _(tap):
+            total = self.quarter[tap, self.z].astype(f32)
+            for k in range(3):
+                total = total + self.zb[k, tap].astype(f32)
+            out[tap] = total.astype(bf16)
+
+
+def start_all(copies):
+    for copy in copies:
+        copy.start()
+
+
+def wait_all(copies):
+    for copy in copies:
+        copy.wait()
+
+
+def mega_kernel(images, cots, timg, tcot, kshard, wl, sg, ob, op, red, figures, *scratch):
     n = 8
     me = lax.axis_index("narrow")
+    w = lax.axis_index("wide")
     z, c = me // 2, me % 2
-    examples = x.shape[0]
+    sibling = me + 1 - 2 * c
+    examples = images.shape[0] // n
     chans = images.shape[1]
     mine = pl.ds(pl.multiple_of(me * chans, chans), chans)
-    greet([{"narrow": lax.rem(me + k, n)} for k in range(1, n)])
+    work, rest = scratch[: len(WORK_SCRATCH)], scratch[len(WORK_SCRATCH) :]
+    x, cot, xt, ct, ktp, block, part, raw, raw_gn, length, tgrad, tgn, sq = rest[:13]
+    s_conv, s_gn, t_conv, t_gn, dt = rest[13:18]
+    s_refs, t_refs = rest[18:24], rest[24:30]
+    s_sems, t_sems = rest[30:36], rest[36:42]
+    s_in, r_in, s_up, r_up, s_dn, r_dn, s_core, r_core, s_loc = rest[42:51]
+    s_out, r_out, s_fin, r_fin, s_fig, r_fig = rest[51:57]
+    greet(
+        [{"narrow": lax.rem(me + k, n)} for k in range(1, n)]
+        + [{"wide": lax.rem(w + k, 4)} for k in range(1, 4)]
+    )
 
     def rows(zz):
         return pl.ds(pl.multiple_of((zz * 2 + c) * chans, chans), chans)
-
-    sibling = me + 1 - 2 * c
 
     def up(step):
         src = kshard if step == 0 else ktp.at[rows(z - step)]
@@ -437,6 +527,42 @@
         src = kshard if slot == 0 else ktp.at[rows(zz)]
         return peer_copy(src, ktp.at[rows(zz)], s_core.at[slot], r_core.at[slot], narrow=sibling)
 
+    def spread(a, src, dst, cut):
+        copies = []
+        for k in range(n):
+            to = lax.rem(me + k, n)
+            if k == 0:
+                copies.append(pltpu.make_async_copy(cut(src, to), dst, s_loc.at[a]))
+            else:
+                copies.append(peer_copy(cut(src, to), dst, s_in.at[a, k - 1], r_in.at[a, k - 1], narrow=to))
+        return copies
+
+    def test_cut(src, to):
+        return src.at[:, pl.ds(pl.multiple_of(to * LANES, LANES), LANES)]
+
+    def example_cut(e):
+        return lambda src, to: src.at[to * examples + e]
+
+    def give_back(a, e, src, dst):
+        copies = []
+        for k in range(n):
+            to = lax.rem(me + k, n)
+            piece = src.at[e, pl.ds(pl.multiple_of(to * chans, chans), chans)]
+            place = dst.at[me * examples + e]
+            slot = a * examples + e
+            if k == 0:
+                copies.append(pltpu.make_async_copy(piece, place, s_loc.at[6 + slot]))
+            else:
+                copies.append(peer_copy(piece, place, s_out.at[slot, k - 1], r_out.at[slot, k - 1], narrow=to))
+        return copies
+
+    own_k = pltpu.make_async_copy(kshard, ktp.at[mine], s_loc.at[10])
+    in_test = spread(0, timg, xt.at[mine], test_cut) + spread(1, tcot, ct.at[mine], test_cut)
+    in_x = [spread(2 + 2 * e, images, x.at[e, mine], example_cut(e)) for e in range(examples)]
+    in_cot = [spread(3 + 2 * e, cots, cot.at[e, mine], example_cut(e)) for e in range(examples)]
+    out_block = [give_back(0, e, block, ob) for e in range(examples)]
+    out_part = [give_back(1, e, part, op) for e in range(examples)]
+
     @pl.when(z < 3)
     def _():
         up(0).start()
@@ -446,24 +572,11 @@
         down(0).start()
 
     across(0, z).start()
-    pairs = ((timg, xt), (tcot, ct), (images, x), (cots, cot))
-    local = [pltpu.make_async_copy(kshard, ktp.at[mine], s_loc.at[4])]
-    sends = []
-    for a, (src, dst) in enumerate(pairs):
-        for k in range(n):
-            to = lax.rem(me + k, n)
-            if a < 2:
-                piece = src.at[:, pl.ds(pl.multiple_of(to * LANES, LANES), LANES)]
-                place = dst.at[mine]
-            else:
-                piece = src.at[pl.ds(to * examples, examples)]
-                place = dst.at[:, mine]
-            if k == 0:
-                local.append(pltpu.make_async_copy(piece, place, s_loc.at[a]))
-            else:
-                sends.append(peer_copy(piece, place, s_a2a.at[a, k - 1], r_a2a.at[a, k - 1], narrow=to))
-    for copy in local + sends:
-        copy.start()
+    own_k.start()
+    start_all(in_test)
+    start_all(in_x[0])
+    wk = make_work(ktp, work)
+    fill_work(wk)
     for step in range(1, 4):
 
         @pl.when(z - step >= 0)
@@ -507,199 +620,143 @@
         def _():
             across(3 + step, z + step).wait()
 
-    for copy in local + sends:
-        copy.wait()
-
-
-def gather(images, cots, timg, tcot, kshard, examples):
-    out = jax.ShapeDtypeStruct
-    anyspace = pl.BlockSpec(memory_space=pl.ANY)
-    dma = pltpu.SemaphoreType.DMA
-    return pl.pallas_call(
-        gather_kernel,
-        out_shape=(
-            out((examples, C, AUG * PIX), bf16),
-            out((examples, C, AUG * PIX), bf16),
-            out((C, LANES), bf16),
-            out((C, LANES), bf16),
-            out((C, KCOLS + LANES), bf16),
-        ),
-        in_specs=[anyspace] * 5,
-        out_specs=(anyspace,) * 5,
-        scratch_shapes=[
-            dma((4, 7)),
-            dma((4, 7)),
-            dma,
-            dma((3,)),
-            dma((3,)),
-            dma((3,)),
-            dma((3,)),
-            dma((7,)),
-            dma((7,)),
-            dma((5,)),
-        ],
-        compiler_params=pltpu.CompilerParams(collective_id=0, has_side_effects=True),
-    )(images, cots, timg, tcot, kshard)
-
-
-def reduce_kernel(
-    block,
-    part,
-    clip_conv,
-    test_conv,
-    clip_gn,
-    test_gn,
-    raw,
-    raw_gn,
-    length,
-    ob,
-    op,
-    red,
-    figures,
-    cb,
-    cg,
-    half,
-    wb,
-    quarter,
-    zb,
-    dt,
-    s_back,
-    r_back,
-    s_core,
-    r_core,
-    s_wide,
-    r_wide,
-    s_z,
-    r_z,
-    s_f,
-    r_f,
-    s_fin,
-    r_fin,
-    s_fig,
-    r_fig,
-    s_loc,
-):
-    n = 8
-    me = lax.axis_index("narrow")
-    w = lax.axis_index("wide")
-    z, c = me // 2, me % 2
-    sibling = me + 1 - 2 * c
-    examples = block.shape[0]
-    chans = ob.shape[1]
-    greet(
-        [{"narrow": lax.rem(me + k, n)} for k in range(1, n)]
-        + [{"wide": lax.rem(w + k, 4)} for k in range(1, 4)]
-    )
-    core = []
-    for a, (conv, gn) in enumerate(((clip_conv, clip_gn), (test_conv, test_gn))):
-        core.append(peer_copy(conv.at[:, :, 1 - c], cb.at[a], s_core.at[a, 0], r_core.at[a, 0], narrow=sibling))
-        core.append(peer_copy(gn.at[:, 1 - c], cg.at[a], s_core.at[a, 1], r_core.at[a, 1], narrow=sibling))
-    for copy in core:
-        copy.start()
-    back = []
-    for a, (src, dst) in enumerate(((block, ob), (part, op))):
-        for k in range(n):
-            to = lax.rem(me + k, n)
-            piece = src.at[:, pl.ds(pl.multiple_of(to * chans, chans), chans)]
-            place = dst.at[pl.ds(me * examples, examples)]
-            if k == 0:
-                back.append(pltpu.make_async_copy(piece, place, s_loc.at[a]))
-            else:
-                back.append(peer_copy(piece, place, s_back.at[a, k - 1], r_back.at[a, k - 1], narrow=to))
-    for copy in back:
-        copy.start()
-    for copy in core:
-        copy.wait()
-    for a, (conv, gn) in enumerate(((clip_conv, clip_gn), (test_conv, test_gn))):
-        for k in range(2):
-
-            @pl.loop(0, 9)
-            def _(tap):
-                total = conv[k * 9 + tap, :, c].astype(f32) + cb[a, k * 9 + tap].astype(f32)
-                half[a, k * 2, tap] = total[:, :, :LANES].astype(bf16)
-                half[a, k * 2 + 1, tap] = total[:, :, LANES:].astype(bf16)
-
-        half[a, 0, 9] = (gn[:, c].astype(f32) + cg[a].astype(f32)).astype(bf16)
-        for q in range(1, 4):
-            half[a, q, 9] = jnp.zeros_like(half[a, q, 9])
-    wide = []
+    own_k.wait()
+    start_all(in_cot[0])
+    unpack_params(wk)
+    turn_kernels(wk)
+    wait_all(in_test)
+
+    place = (w, z, c, me)
+    direction = Exchange(place, t_conv, t_gn, t_refs, t_sems)
+    clipped = Exchange(place, s_conv, s_gn, s_refs, s_sems)
+    forward(wk, lambda t: xt[...].astype(f32), 1, None)
+    backward_two(wk, lambda t: ct[...].astype(f32), lambda t: sg[me], 1, tgrad)
+    backward_one(wk, 1, tgrad, tgn, None)
+    raw_gradient(wk, tgrad, sq)
+
+    @pl.loop(0, 18)
+    def _(k):
+        t_conv[k] = tgrad[k].astype(bf16).reshape(4, 2, chans, C)
+
+    t_gn[...] = tgn[...].astype(bf16).reshape(4, 2, chans, LANES)
+    direction.start_core()
+
+    own = dt.at[c, w, z]
+    line_ag, wide_ag = [], []
+    for k in range(1, 4):
+        to = lax.rem(z + k, 4)
+        line_ag.append(peer_copy(own, own, s_fin.at[0, k - 1], r_fin.at[0, k - 1], narrow=to * 2 + c))
     for k in range(1, 4):
         to = lax.rem(w + k, 4)
-        wide.append(peer_copy(half.at[:, to], wb.at[k - 1], s_wide.at[k - 1], r_wide.at[k - 1], wide=to))
-    for copy in wide:
-        copy.start()
-    for copy in wide:
-        copy.wait()
-    for a in range(2):
-
-        @pl.loop(0, 10)
-        def _(tap):
-            total = half[a, w, tap].astype(f32)
-            for k in range(3):
-                total = total + wb[k, a, tap].astype(f32)
-            quarter[a, tap] = total.astype(bf16)
-
-    line = []
-    for k in range(1, 4):
-        to = lax.rem(z + k, 4)
-        line.append(
-            peer_copy(quarter.at[:, :, to], zb.at[k - 1], s_z.at[k - 1], r_z.at[k - 1], narrow=to * 2 + c)
+        wide_ag.append(
+            peer_copy(dt.at[c, w], dt.at[c, w], s_fin.at[1, k - 1], r_fin.at[1, k - 1], wide=to)
         )
-    for copy in line:
-        copy.start()
-    for copy in line:
-        copy.wait()
-
-    def final(a, tap):
-        total = quarter[a, tap, z].astype(f32)
-        for k in range(3):
-            total = total + zb[k, a, tap].astype(f32)
-        return total.astype(bf16)
-
-    @pl.loop(0, 10)
-    def _(tap):
-        red[w, tap] = final(0, tap)
-        dt[c, w, z, tap] = final(1, tap)
-
+    core_ag = peer_copy(dt.at[c], dt.at[c], s_fin.at[2, 0], r_fin.at[2, 0], narrow=sibling)
+
+    def after_forward(e):
+        if e == 0:
+            direction.start_wide()
+        else:
+            wait_all(line_ag)
+            start_all(wide_ag)
+
+    def between(e):
+        if e == 0:
+            direction.start_line()
+        else:
+            wait_all(wide_ag)
+            core_ag.start()
+
+    def after_backward(e):
+        if e == 0:
+            direction.finish(own)
+            start_all(line_ag)
+
+    for e in range(examples):
+        wait_all(in_x[e])
+        if e + 1 < examples:
+            start_all(in_x[e + 1])
+
+        def block_store(t, value):
+            block[e, :, lane_tile(t)] = value.astype(bf16)
+
+        def part_store(t, value):
+            part[e, :, lane_tile(t)] = value.astype(bf16)
+
+        forward(wk, lambda t: x[e, :, lane_tile(t)].astype(f32), 8, block_store)
+        start_all(out_block[e])
+        after_forward(e)
+        wait_all(in_cot[e])
+        if e + 1 < examples:
+            start_all(in_cot[e + 1])
+        backward_two(
+            wk,
+            lambda t: cot[e, :, lane_tile(t)].astype(f32),
+            lambda t: wl[me * examples + e, :, lane_tile(t)],
+            8,
+            raw.at[e],
+        )
+        between(e)
+        backward_one(wk, 8, raw.at[e], raw_gn.at[e], part_store)
+        start_all(out_part[e])
+        after_backward(e)
+        sq[...] = jnp.zeros_like(sq)
+        raw_gradient(wk, raw.at[e], sq)
+        gn = raw_gn[e]
+        square = whole_sum(sq[...]) + whole_sum(gn * gn)
+        length[e] = jnp.broadcast_to(jnp.sqrt(square), (8, LANES))
+
+    factors = [CLIP / jnp.maximum(length[e][0:1, 0:1], CLIP) for e in range(examples)]
+    total = factors[0] * raw_gn[0]
+    for e in range(1, examples):
+        total = total + factors[e] * raw_gn[e]
+    s_gn[...] = total.astype(bf16).reshape(4, 2, chans, LANES)
+
+    @pl.loop(0, 18)
+    def _(k):
+        total = factors[0] * raw[0, k]
+        for e in range(1, examples):
+            total = total + factors[e] * raw[e, k]
+        s_conv[k] = total.astype(bf16).reshape(4, 2, chans, C)
+
+    clipped.start_core()
+    core_ag.wait()
+    clipped.start_wide()
+    inner_products(dt, raw, raw_gn, length, figures, me, chans)
+    figs = []
+    for k in range(1, n):
+        to = lax.rem(me + k, n)
+        figs.append(peer_copy(figures.at[me], figures.at[me], s_fig.at[k - 1], r_fig.at[k - 1], narrow=to))
+    start_all(figs)
+    clipped.start_line()
+    clipped.finish(red.at[w])
     finals = []
     for k in range(1, 4):
         to = lax.rem(w + k, 4)
-        finals.append(peer_copy(red.at[w], red.at[w], s_f.at[0, k - 1], r_f.at[0, k - 1], wide=to))
-    spread = []
-    for k in range(1, 4):
-        to = lax.rem(z + k, 4)
-        own = dt.at[c, w, z]
-        spread.append(peer_copy(own, own, s_f.at[1, k - 1], r_f.at[1, k - 1], narrow=to * 2 + c))
-    for copy in spread + finals:
-        copy.start()
-    for copy in spread:
-        copy.wait()
-    fin = []
-    for k in range(1, 4):
-        to = lax.rem(w + k, 4)
-        fin.append(peer_copy(dt.at[c, w], dt.at[c, w], s_fin.at[k - 1], r_fin.at[k - 1], wide=to))
-    for copy in fin:
-        copy.start()
-    for copy in fin:
-        copy.wait()
-    last = peer_copy(dt.at[c], dt.at[c], s_fin.at[3], r_fin.at[3], narrow=sibling)
-    last.start()
-    last.wait()
-
-    own_rows = lax.broadcasted_iota(jnp.int32, (8, LANES), 0)
+        finals.append(peer_copy(red.at[w], red.at[w], s_fin.at[3, k - 1], r_fin.at[3, k - 1], wide=to))
+    start_all(finals)
+    for e in range(examples):
+        wait_all(out_block[e])
+        wait_all(out_part[e])
+    wait_all(figs)
+    wait_all(finals)
+
+
+def inner_products(dt, raw, raw_gn, length, figures, me, chans):
+    examples = raw.shape[0]
     zero = jnp.zeros((chans, LANES), f32)
 
     def visit(index, carry):
         q, rest = index // 8, index % 8
-        zz, cc = rest // 2, rest % 2
         at = pl.ds(pl.multiple_of(rest * chans, chans), chans)
+        lanes = pl.ds(pl.multiple_of((q % 2) * LANES, LANES), LANES)
         square = carry[0]
         sums = list(carry[1:])
         for tap in range(9):
-            d = dt[cc, q, zz, tap].astype(f32)
+            d = dt[rest % 2, q, rest // 2, tap].astype(f32)
             square = square + d * d
             for e in range(examples):
-                sums[e] = sums[e] + d * raw[e, (q // 2) * 9 + tap, at, pl.ds(pl.multiple_of((q % 2) * LANES, LANES), LANES)]
+                sums[e] = sums[e] + d * raw[e, (q // 2) * 9 + tap, at, lanes]
         return (square, *sums)
 
     totals = lax.fori_loop(0, 32, visit, (zero,) * (examples + 1))
@@ -712,75 +769,81 @@
     totals = lax.fori_loop(0, 8, visit_gn, totals)
     dir_sq = whole_sum(totals[0])
     params = 18 * C * C + 4 * C
+    top = lax.broadcasted_iota(jnp.int32, (8, LANES), 0)
     for e in range(examples):
         size = length[e]
         factor = CLIP / jnp.maximum(size, CLIP)
         influence = factor * whole_sum(totals[1 + e]) * math.sqrt(params) / (CLIP * jnp.sqrt(dir_sq + 1e-06))
-        figures[me, e] = jnp.where(own_rows == 0, size, influence)
-    figs = []
-    for k in range(1, n):
-        figs.append(
-            peer_copy(figures.at[me], figures.at[me], s_fig.at[k - 1], r_fig.at[k - 1], narrow=lax.rem(me + k, n))
-        )
-    for copy in figs:
-        copy.start()
-    for copy in figs + finals + back:
-        copy.wait()
-
-
-def reduce_all(block, part, clip_conv, test_conv, clip_gn, test_gn, raw, raw_gn, length, chans):
-    examples = block.shape[0]
+        figures[me, e] = jnp.where(top == 0, size, influence)
+
+
+def mega(images, cots, timg, tcot, kshard, wl, sg):
+    held, chans = images.shape[0], images.shape[1]
+    examples = held // 8
     out = jax.ShapeDtypeStruct
     anyspace = pl.BlockSpec(memory_space=pl.ANY)
     vmem = pl.BlockSpec(memory_space=pltpu.VMEM)
     dma = pltpu.SemaphoreType.DMA
-    whole = (18, 4, 2, chans, C)
+    exchange = [
+        pltpu.VMEM((18, 4, chans, C), bf16),
+        pltpu.VMEM((4, chans, LANES), bf16),
+        pltpu.VMEM((4, 10, 4, chans, LANES), bf16),
+        pltpu.VMEM((3, 10, 4, chans, LANES), bf16),
+        pltpu.VMEM((10, 4, chans, LANES), bf16),
+        pltpu.VMEM((3, 10, chans, LANES), bf16),
+    ]
+    sems = [dma((2,)), dma((2,)), dma((3,)), dma((3,)), dma((3,)), dma((3,))]
+    scratch = [
+        pltpu.VMEM((examples, C, AUG * PIX), bf16),
+        pltpu.VMEM((examples, C, AUG * PIX), bf16),
+        pltpu.VMEM((C, LANES), bf16),
+        pltpu.VMEM((C, LANES), bf16),
+        pltpu.VMEM((C, KCOLS + LANES), bf16),
+        pltpu.VMEM((examples, C, AUG * PIX), bf16),
+        pltpu.VMEM((examples, C, AUG * PIX), bf16),
+        pltpu.VMEM((examples, 18, C, C), f32),
+        pltpu.VMEM((examples, C, LANES), f32),
+        pltpu.VMEM((examples, 8, LANES), f32),
+        pltpu.VMEM((18, C, C), f32),
+        pltpu.VMEM((C, LANES), f32),
+        pltpu.VMEM((8, LANES), f32),
+        pltpu.VMEM((18, 4, 2, chans, C), bf16),
+        pltpu.VMEM((4, 2, chans, LANES), bf16),
+        pltpu.VMEM((18, 4, 2, chans, C), bf16),
+        pltpu.VMEM((4, 2, chans, LANES), bf16),
+        pltpu.VMEM((2, 4, 4, 10, chans, LANES), bf16),
+    ]
+    kinds = 2 + 2 * examples
+    moves = [
+        dma((kinds, 7)),
+        dma((kinds, 7)),
+        dma((3,)),
+        dma((3,)),
+        dma((3,)),
+        dma((3,)),
+        dma((7,)),
+        dma((7,)),
+        dma((11,)),
+        dma((2 * examples, 7)),
+        dma((2 * examples, 7)),
+        dma((4, 3)),
+        dma((4, 3)),
+        dma((7,)),
+        dma((7,)),
+    ]
     return pl.pallas_call(
-        reduce_kernel,
+        mega_kernel,
         out_shape=(
-            out((8 * examples, chans, AUG * PIX), bf16),
-            out((8 * examples, chans, AUG * PIX), bf16),
+            out((held, chans, AUG * PIX), bf16),
+            out((held, chans, AUG * PIX), bf16),
             out((4, 10, chans, LANES), bf16),
             out((8, examples, 8, LANES), f32),
         ),
-        in_specs=[anyspace, anyspace] + [vmem] * 7,
+        in_specs=[anyspace] * 5 + [vmem] * 2,
         out_specs=(anyspace, anyspace, vmem, vmem),
-        scratch_shapes=[
-            pltpu.VMEM((2, 18, 4, chans, C), bf16),
-            pltpu.VMEM((2, 4, chans, LANES), bf16),
-            pltpu.VMEM((2, 4, 10, 4, chans, LANES), bf16),
-            pltpu.VMEM((3, 2, 10, 4, chans, LANES), bf16),
-            pltpu.VMEM((2, 10, 4, chans, LANES), bf16),
-            pltpu.VMEM((3, 2, 10, chans, LANES), bf16),
-            pltpu.VMEM((2, 4, 4, 10, chans, LANES), bf16),
-            dma((2, 7)),
-            dma((2, 7)),
-            dma((2, 2)),
-            dma((2, 2)),
-            dma((3,)),
-            dma((3,)),
-            dma((3,)),
-            dma((3,)),
-            dma((2, 3)),
-            dma((2, 3)),
-            dma((4,)),
-            dma((4,)),
-            dma((7,)),
-            dma((7,)),
-            dma((2,)),
-        ],
-        compiler_params=pltpu.CompilerParams(collective_id=1, has_side_effects=True, vmem_limit_bytes=58 << 20),
-    )(
-        block,
-        part,
-        clip_conv.reshape(whole),
-        test_conv.reshape(whole),
-        clip_gn.astype(bf16).reshape(4, 2, chans, LANES),
-        test_gn.astype(bf16).reshape(4, 2, chans, LANES),
-        raw,
-        raw_gn,
-        length,
-    )
+        scratch_shapes=WORK_SCRATCH + scratch + exchange + exchange + sems + sems + moves,
+        compiler_params=pltpu.CompilerParams(collective_id=0, has_side_effects=True, vmem_limit_bytes=60 << 20),
+    )(images, cots, timg, tcot, kshard, wl, sg)
 
 
 def pieces(v):
@@ -880,20 +943,19 @@
         (pairs[:, 1:2] == slots[None, :]).astype(f32), 0
     )
     sign_pixels = jnp.repeat(signs, PIX).reshape(8, LANES) * (1.0 / share)
-    wl = lax.dynamic_slice_in_dim(pixels, me * examples, examples, 0)[:, None, :]
-    sg = lax.dynamic_slice_in_dim(sign_pixels, me // share, 1, 0)
     kshard = kernel_rows(conv_weight, gn_params)
     timg, tcot = test_images[0], test_cotangent[0]
     direct = n_wide == 4 and narrow == 8
     if direct:
-        x, cot, xt, ct, ktp = gather(images, cotangent, timg, tcot, kshard, examples)
+        block_out, op, red, figures = mega(
+            images, cotangent, timg, tcot, kshard, pixels[:, None, :], sign_pixels[:, None, :]
+        )
     else:
+        wl = lax.dynamic_slice_in_dim(pixels, me * examples, examples, 0)[:, None, :]
+        sg = lax.dynamic_slice_in_dim(sign_pixels, me // share, 1, 0)
         x, cot, xt, ct, ktp = plain_gather(images, cotangent, timg, tcot, kshard, narrow)
-    block, part, clip_conv, test_conv, clip_gn, test_gn, raw, raw_gn, length = compute(x, cot, xt, ct, ktp, wl, sg)
-    send = reduce_all if direct else plain_reduce
-    block_out, op, red, figures = send(
-        block, part, clip_conv, test_conv, clip_gn, test_gn, raw, raw_gn, length, chans
-    )
+        parts = compute(x, cot, xt, ct, ktp, wl, sg)
+        block_out, op, red, figures = plain_reduce(*parts, chans)
     input_grad = cotangent.astype(f32) * pixels[:, None, :] + op.astype(f32)
     lengths = figures[:, :, 0, 0].reshape(held)
     influence = figures[:, :, 1, 0].reshape(held)

time: 269 us -> 197 us (0.73)
  Pallas kernels: 245 us -> 175 us
    pallas_call x3 -> x1, Pallas kernels: 245 us -> 175 us  [mega(): pl.pallas_call(mega_kernel, out_shape=(out((held, chans, AUG * PIX), bf16...]
    convert_element_type x2 -> x0, other arithmetic: 3.08 us -> none  [the longest x1 1.54 us: reduce_all(): clip_gn.astype(bf16).reshape(4, 2, chans, LANES)]
where the time goes in v2:
time: 197 us; the launch traced here: 196 us
  Pallas kernels  175 us (89%)
  other arithmetic  11.2 us (6%)
  local copies, waits for them, and re-layouts  7.82 us (4%)
  between operations  2.22 us (1%)
    pallas_call x1, Pallas kernels, mega(): pl.pallas_call(mega_kernel, out_shape=(out((held, chans, AUG * PIX), bf16...  175 us

profile of v2, /device:TPU:0, one launch (start us, length us, event | category | flops | bytes accessed | tf_op | source)
XLA Modules:
  0.0 196.2 jit_solution(4415943919025745607)
XLA Ops:
  0.6 0.0 copy-start.6
  0.7 1.2 reduce_sum.36
  1.8 0.0 copy-start.11
  1.9 1.3 multiply_reduce_fusion
  3.1 0.0 copy-start.10
  3.1 1.2 multiply_convert_fusion
  4.4 0.3 copy.49
  4.6 0.3 reshape.71
  5.0 0.0 copy-start.1
  5.0 0.1 pad.2.clone
  5.1 0.0 copy-done.6
  5.1 0.1 maximum_maximum_fusion
  5.2 0.1 copy.52
  5.2 0.1 copy.51
  5.3 0.8 concatenate.7.kshard
  6.1 0.0 copy-done.11
  6.8 0.1 fusion.2
  6.9 0.1 broadcast_in_dim.38
  7.0 0.8 broadcast_in_dim_reshape.4.wl
  7.8 0.0 copy-done.10
  7.8 0.1 convert_reduce_fusion
  7.9 0.1 sub.38
  8.0 0.1 broadcast_in_dim.39
  8.0 0.7 broadcast_in_dim.40.sg
  8.7 175.0 %shard_map.239 = (bf16[16,32,1024]{2,1,0:T(8,128)(2,1)}, bf16[16,32,1024]{2,1,0:T(8,128)(2,1)}, bf16[4,10,32,128]{3,2,1,0:T(8,128)(2,1)}, f32[8,2,8,128]{3,2,1,0:T(8,128)}) custom-call(bf16[16,32,1024]{2,1,0:T(8,128)(2,1)} %images.1, bf16[16,32,1024]{2,1,0:T(8,128)(2,1)} %cots.1, bf16[32,1024]{1,0:T(8,128)(2,1)} %bitcast.36, bf16[32,1024]{1,0:T(8,128)(2,1)} %bitcast.37, ...), custom_call_target="tpu_custom_call" | custom-call | tf_op jit(solution)/shard_map/pallas_call | solution.py:834
  183.7 0.1 mul.94
  183.8 0.0 copy-done.1
  183.8 0.0 copy-start.5
  183.8 3.0 %convert_add_fusion = f32[16,32,1024]{2,1,0:T(8,128)} fusion(bf16[16,32,1024]{2,1,0:T(8,128)(2,1)} %get-tuple-element.16, bf16[16,32,1024]{2,1,0:T(8,128)(2,1)S(1)} %copy-done.1, f32[16,1024]{1,0:T(8,128)S(1)} %mul.94), kind=kLoop, calls=%fused_computation | loop fusion | flops 2097152 | bytes 4259840 | tf_op jit(solution)/shard_map/add | solution.py:959
  186.8 0.0 copy-start
  186.8 0.0 copy-start.3
  186.8 0.0 copy-start.4
  186.8 1.1 slice_reduce_fusion
  188.0 0.6 reshape_squeeze.6
  188.6 0.6 reshape_squeeze.7
  189.8 0.0 copy-done.5
  189.9 0.1 convert_bitcast_fusion
  189.9 0.5 copy.54
  190.4 0.5 reshape.73
  190.9 0.0 copy-done
  190.9 0.0 copy-done.3
  190.9 0.0 copy-done.4
  190.9 0.0 copy-start.7
  190.9 0.0 copy-start.8
  190.9 0.0 copy-start.9
  191.0 0.0 copy-start.2
  191.0 2.8 %fusion.6 = (bf16[2,3,3,256,32]{3,4,2,1,0:T(8,128)(2,1)}, f32[2,3,3,256,32]{3,4,2,1,0:T(8,128)}, f32[2,3,3,256,32]{3,4,2,1,0:T(8,128)}, f32[2,3,3,256,32]{3,4,2,1,0:T(8,128)}) fusion(f32[2,3,3,256,32]{3,4,2,1,0:T(8,128)S(1)} %copy-done, f32[]{:T(128)} %bitcast.10, f32[2,3,3,256,32]{3,4,2,1,0:T(8,128)S(1)} %reshape.73, ...), kind=kLoop, calls=%fused_computation.38 | loop fusion | flops 2654208 | bytes 5013508 | tf_op jit(solution)/shard_map/convert_element_type | solution.py:981
  193.8 0.7 slice_convert_fusion
  194.5 0.1 copy.55
  194.6 0.0 copy-done.7
  194.6 0.0 copy-done.8
  194.6 0.0 copy-done.9
  194.6 0.6 multiply_subtract_fusion.1
  195.2 0.0 copy-done.2
  195.2 1.0 copy.60
  (12 shorter events, 0.1 us)
Async XLA Ops:
  0.6 4.4 %copy-start.6 = (f32[4,32]{1,0:T(4,128)S(1)}, f32[4,32]{1,0:T(4,128)}, u32[]{:S(2)}) copy-start(f32[4,32]{1,0:T(4,128)} %param.24) | copy-start | bytes 1540
  1.8 4.3 %copy-start.11 = (s32[16]{0:T(128)S(1)}, s32[16]{0:T(128)}, u32[]{:S(2)}) copy-start(s32[16]{0:T(128)} %param.22) | copy-start | bytes 196
  3.1 4.6 %copy-start.10 = (s32[8,2]{0,1:T(2,128)S(1)}, s32[8,2]{0,1:T(2,128)}, u32[]{:S(2)}) copy-start(s32[8,2]{0,1:T(2,128)} %param.20) | copy-start | bytes 196
  5.0 178.8 %copy-start.1 = (bf16[16,32,1024]{2,1,0:T(8,128)(2,1)S(1)}, bf16[16,32,1024]{2,1,0:T(8,128)(2,1)}, u32[]{:S(2)}) copy-start(bf16[16,32,1024]{2,1,0:T(8,128)(2,1)} %cots.1) | copy-start | bytes 3145732
  183.8 6.0 %copy-start.5 = (bf16[4,10,32,128]{3,2,1,0:T(8,128)(2,1)S(1)}, bf16[4,10,32,128]{3,2,1,0:T(8,128)(2,1)}, u32[]{:S(2)}) copy-start(bf16[4,10,32,128]{3,2,1,0:T(8,128)(2,1)} %get-tuple-element.18) | copy-start | bytes 983044
  186.8 4.1 %copy-start = (f32[2,3,3,256,32]{3,4,2,1,0:T(8,128)S(1)}, f32[2,3,3,256,32]{3,4,2,1,0:T(8,128)}, u32[]{:S(2)}) copy-start(f32[2,3,3,256,32]{3,4,2,1,0:T(8,128)} %param.23) | copy-start | bytes 1769476
  186.8 4.1 %copy-start.3 = (f32[2,3,3,256,32]{3,4,2,1,0:T(8,128)S(1)}, f32[2,3,3,256,32]{3,4,2,1,0:T(8,128)}, u32[]{:S(2)}) copy-start(f32[2,3,3,256,32]{3,4,2,1,0:T(8,128)} %param.29) | copy-start | bytes 1769476
  186.8 4.1 %copy-start.4 = (f32[2,3,3,256,32]{3,4,2,1,0:T(8,128)S(1)}, f32[2,3,3,256,32]{3,4,2,1,0:T(8,128)}, u32[]{:S(2)}) copy-start(f32[2,3,3,256,32]{3,4,2,1,0:T(8,128)} %param.26) | copy-start | bytes 1769476
  190.9 3.7 %copy-start.7 = (f32[4,32]{1,0:T(4,128)S(1)}, f32[4,32]{1,0:T(4,128)}, u32[]{:S(2)}) copy-start(f32[4,32]{1,0:T(4,128)} %param.30) | copy-start | bytes 1540
  190.9 3.6 %copy-start.8 = (f32[4,32]{1,0:T(4,128)S(1)}, f32[4,32]{1,0:T(4,128)}, u32[]{:S(2)}) copy-start(f32[4,32]{1,0:T(4,128)} %param.28) | copy-start | bytes 1540
  190.9 3.6 %copy-start.9 = (f32[4,32]{1,0:T(4,128)S(1)}, f32[4,32]{1,0:T(4,128)}, u32[]{:S(2)}) copy-start(f32[4,32]{1,0:T(4,128)} %param.27) | copy-start | bytes 1540
  191.0 4.2 %copy-start.2 = (bf16[16,32,1024]{2,1,0:T(8,128)(2,1)S(1)}, bf16[16,32,1024]{2,1,0:T(8,128)(2,1)}, u32[]{:S(2)}) copy-start(bf16[16,32,1024]{2,1,0:T(8,128)(2,1)} %get-tuple-element.50) | copy-start | bytes 3145732

commit v3 on v2

--- a/solution.py
+++ b/solution.py
@@ -161,8 +161,8 @@
     wk.masks = tap_masks()
 
 
-def unpack_params(wk):
-    tail = wk.ktp[:, KCOLS : KCOLS + LANES].astype(f32)
+def unpack_params(wk, tail):
+    tail = tail.astype(f32)
     for k in range(6):
         value = tail[:, k : k + 1] + tail[:, 8 + k : 9 + k] + tail[:, 16 + k : 17 + k]
         value = jnp.broadcast_to(value, (C, LANES))
@@ -172,20 +172,21 @@
             wk.rs[k - 4] = value
 
 
-def turn_kernels(wk):
-    for k in range(18):
-        at = (k // 9) * FAN + (k % 9) * C
-        wk.kb[k // 9, :, (k % 9) * C : (k % 9 + 1) * C] = wk.ktp[:, at : at + C].T
+def turn_kernel(wk, conv):
+    for tap in range(9):
+        wk.kb[conv, :, tap * C : (tap + 1) * C] = wk.kf[conv, :, tap * C : (tap + 1) * C].T
 
 
 def cols(ref, width):
     return ref if width == ref.shape[1] else ref.at[:, :width]
 
 
-def forward(wk, x_load, tiles, block_store):
+def forward(wk, x_load, tiles, block_store, early=None):
     width = tiles * LANES
     norm_forward(wk, x_load, tiles, 0, wk.hat1, wk.rstd1, wk.hid1, wk.col)
-    matmul_cols(wk.mid, wk.ktp[:, :FAN], cols(wk.col, width), width)
+    if early is not None:
+        early()
+    matmul_cols(wk.mid, wk.kf[0], cols(wk.col, width), width)
     norm_forward(
         wk,
         lambda t: wk.mid[:, lane_tile(t)],
@@ -197,7 +198,7 @@
         wk.col if block_store is not None else None,
     )
     if block_store is not None:
-        matmul_cols(wk.mid, wk.ktp[:, FAN : 2 * FAN], cols(wk.col, width), width)
+        matmul_cols(wk.mid, wk.kf[1], cols(wk.col, width), width)
 
         @pl.loop(0, tiles)
         def _(t):
@@ -247,7 +248,7 @@
             second = jnp.zeros((rows, C), f32)
             for tap in range(9):
                 g = grads[conv * 9 + tap, at, :]
-                k = wk.ktp[at, conv * FAN + tap * C : conv * FAN + (tap + 1) * C].astype(f32)
+                k = wk.kf[conv, at, tap * C : (tap + 1) * C].astype(f32)
                 first = first + g
                 second = second + g * k
             first = jnp.sum(first, axis=1, keepdims=True) * (1.0 / FAN)
@@ -256,7 +257,7 @@
             squares = jnp.zeros((rows, C), f32)
             for tap in range(9):
                 g = grads[conv * 9 + tap, at, :]
-                k = wk.ktp[at, conv * FAN + tap * C : conv * FAN + (tap + 1) * C].astype(f32)
+                k = wk.kf[conv, at, tap * C : (tap + 1) * C].astype(f32)
                 value = (g - first - k * second) * rs
                 grads[conv * 9 + tap, at, :] = value
                 squares = squares + value * value
@@ -269,6 +270,7 @@
 
 
 WORK_SCRATCH = [
+    pltpu.VMEM((2, C, FAN), bf16),
     pltpu.VMEM((2, C, FAN), bf16),
     pltpu.VMEM((FAN, AUG * PIX), bf16),
     pltpu.VMEM((C, AUG * PIX), f32),
@@ -286,6 +288,7 @@
     pltpu.VMEM((2, 2, C, LANES), f32),
 ]
 WORK_NAMES = (
+    "kf",
     "kb",
     "col",
     "mid",
@@ -304,9 +307,8 @@
 )
 
 
-def make_work(ktp, refs):
+def make_work(refs):
     wk = Work()
-    wk.ktp = ktp
     for name, ref in zip(WORK_NAMES, refs):
         setattr(wk, name, ref)
     return wk
@@ -316,11 +318,13 @@
     x, cot, xt, ct, ktp, wl, sg, block, part, clipped, test, clipped_gn, test_gn, raw, raw_gn, length, *scratch
 ):
     examples = x.shape[0]
-    wk = make_work(ktp, scratch[:-2])
+    wk = make_work(scratch[:-2])
     tgrad, sq = scratch[-2:]
     fill_work(wk)
-    unpack_params(wk)
-    turn_kernels(wk)
+    unpack_params(wk, ktp[:, KCOLS : KCOLS + LANES])
+    for conv in range(2):
+        wk.kf[conv] = ktp[:, conv * FAN : (conv + 1) * FAN]
+        turn_kernel(wk, conv)
     forward(wk, lambda t: xt[...].astype(f32), 1, None)
     backward_two(wk, lambda t: ct[...].astype(f32), lambda t: sg[...], 1, tgrad)
     backward_one(wk, 1, tgrad, test_gn, None)
@@ -433,6 +437,10 @@
                 )
             )
 
+    def clear(self):
+        for q in range(1, 4):
+            self.half[q, 9] = jnp.zeros_like(self.half[q, 9])
+
     def start_core(self):
         for copy in self.core:
             copy.start()
@@ -450,8 +458,6 @@
                 half[k * 2 + 1, tap] = total[:, :, LANES:].astype(bf16)
 
         half[0, 9] = (self.gn[:, c].astype(f32) + self.cg[...].astype(f32)).astype(bf16)
-        for q in range(1, 4):
-            half[q, 9] = jnp.zeros_like(half[q, 9])
         for copy in self.wide:
             copy.start()
 
@@ -491,7 +497,53 @@
         copy.wait()
 
 
-def mega_kernel(images, cots, timg, tcot, kshard, wl, sg, ob, op, red, figures, *scratch):
+UNITS = 20
+
+
+def own_kernels(weight, gain, shard):
+    chans = weight.shape[1]
+    lane = lax.broadcasted_iota(jnp.int32, (chans, LANES), 1)
+    eye = lax.broadcasted_iota(jnp.int32, (chans, chans), 0) == lax.broadcasted_iota(
+        jnp.int32, (chans, chans), 1
+    )
+    values = [
+        jnp.sum(jnp.where(eye, jnp.broadcast_to(gain[k : k + 1, :], (chans, chans)), 0.0), axis=1, keepdims=True)
+        for k in range(4)
+    ]
+    for conv in range(2):
+        total = jnp.zeros((chans, C), f32)
+        for tap in range(9):
+            total = total + weight[conv * 9 + tap]
+        mean = jnp.sum(total, axis=1, keepdims=True) * (1.0 / FAN)
+        total = jnp.zeros((chans, C), f32)
+        for tap in range(9):
+            centre = weight[conv * 9 + tap] - mean
+            total = total + centre * centre
+        spread = jnp.sum(total, axis=1, keepdims=True) * (1.0 / FAN)
+        scale = lax.rsqrt(FAN * spread + 1e-06)
+        values.append(scale)
+        for tap in range(9):
+            kernel = ((weight[conv * 9 + tap] - mean) * scale).astype(bf16)
+            shard[conv, 2 * tap] = kernel[:, :LANES]
+            shard[conv, 2 * tap + 1] = kernel[:, LANES:]
+    tail = jnp.zeros((chans, LANES), f32)
+    for k, value in enumerate(values):
+        high = value.astype(bf16).astype(f32)
+        mid = (value - high).astype(bf16).astype(f32)
+        low = value - high - mid
+        tail = tail + jnp.where(lane == k, high, 0.0)
+        tail = tail + jnp.where(lane == 8 + k, mid, 0.0)
+        tail = tail + jnp.where(lane == 16 + k, low, 0.0)
+    shard[0, 18] = tail.astype(bf16)
+    zero = jnp.zeros((chans, LANES), bf16)
+    shard[0, 19] = zero
+    shard[1, 18] = zero
+    shard[1, 19] = zero
+
+
+def mega_kernel(
+    images, cots, timg, tcot, weight, gain, pairs, alive, counts, ob, op, red_out, gn_out, norms, infl, *scratch
+):
     n = 8
     me = lax.axis_index("narrow")
     w = lax.axis_index("wide")
@@ -501,31 +553,16 @@
     chans = images.shape[1]
     mine = pl.ds(pl.multiple_of(me * chans, chans), chans)
     work, rest = scratch[: len(WORK_SCRATCH)], scratch[len(WORK_SCRATCH) :]
-    x, cot, xt, ct, ktp, block, part, raw, raw_gn, length, tgrad, tgn, sq = rest[:13]
-    s_conv, s_gn, t_conv, t_gn, dt = rest[13:18]
-    s_refs, t_refs = rest[18:24], rest[24:30]
-    s_sems, t_sems = rest[30:36], rest[36:42]
-    s_in, r_in, s_up, r_up, s_dn, r_dn, s_core, r_core, s_loc = rest[42:51]
-    s_out, r_out, s_fin, r_fin, s_fig, r_fig = rest[51:57]
+    x, cot, xt, ct, shard, ktp, block, part, raw, raw_gn, length, tgrad, tgn, sq = rest[:14]
+    s_conv, s_gn, t_conv, t_gn, dt, red, figures = rest[14:21]
+    s_refs, t_refs = rest[21:27], rest[27:33]
+    s_sems, t_sems = rest[33:39], rest[39:45]
+    s_in, r_in, s_kz, r_kz, s_kw, r_kw, s_kc, r_kc, s_loc = rest[45:54]
+    s_out, r_out, s_fin, r_fin, s_fig, r_fig = rest[54:60]
     greet(
         [{"narrow": lax.rem(me + k, n)} for k in range(1, n)]
         + [{"wide": lax.rem(w + k, 4)} for k in range(1, 4)]
     )
-
-    def rows(zz):
-        return pl.ds(pl.multiple_of((zz * 2 + c) * chans, chans), chans)
-
-    def up(step):
-        src = kshard if step == 0 else ktp.at[rows(z - step)]
-        return peer_copy(src, ktp.at[rows(z - step)], s_up.at[step], r_up.at[step], narrow=me + 2)
-
-    def down(step):
-        src = kshard if step == 0 else ktp.at[rows(z + step)]
-        return peer_copy(src, ktp.at[rows(z + step)], s_dn.at[step], r_dn.at[step], narrow=me - 2)
-
-    def across(slot, zz):
-        src = kshard if slot == 0 else ktp.at[rows(zz)]
-        return peer_copy(src, ktp.at[rows(zz)], s_core.at[slot], r_core.at[slot], narrow=sibling)
 
     def spread(a, src, dst, cut):
         copies = []
@@ -556,81 +593,85 @@
                 copies.append(peer_copy(piece, place, s_out.at[slot, k - 1], r_out.at[slot, k - 1], narrow=to))
         return copies
 
-    own_k = pltpu.make_async_copy(kshard, ktp.at[mine], s_loc.at[10])
     in_test = spread(0, timg, xt.at[mine], test_cut) + spread(1, tcot, ct.at[mine], test_cut)
     in_x = [spread(2 + 2 * e, images, x.at[e, mine], example_cut(e)) for e in range(examples)]
     in_cot = [spread(3 + 2 * e, cots, cot.at[e, mine], example_cut(e)) for e in range(examples)]
     out_block = [give_back(0, e, block, ob) for e in range(examples)]
     out_part = [give_back(1, e, part, op) for e in range(examples)]
-
-    @pl.when(z < 3)
-    def _():
-        up(0).start()
-
-    @pl.when(z > 0)
-    def _():
-        down(0).start()
-
-    across(0, z).start()
-    own_k.start()
+    fifth = pl.ds(w * (UNITS // 4), UNITS // 4)
+    k_line, k_wide, k_core = [], [], []
+    for conv in range(2):
+        k_line.append(
+            [
+                peer_copy(
+                    shard.at[conv, fifth],
+                    ktp.at[conv, fifth, z, c],
+                    s_kz.at[conv, k - 1],
+                    r_kz.at[conv, k - 1],
+                    narrow=lax.rem(z + k, 4) * 2 + c,
+                )
+                for k in range(1, 4)
+            ]
+        )
+        held = ktp.at[conv, fifth, :, c]
+        k_wide.append(
+            [
+                peer_copy(held, held, s_kw.at[conv, k - 1], r_kw.at[conv, k - 1], wide=lax.rem(w + k, 4))
+                for k in range(1, 4)
+            ]
+        )
+        held = ktp.at[conv, :, :, c]
+        k_core.append(peer_copy(held, held, s_kc.at[conv], r_kc.at[conv], narrow=sibling))
+
     start_all(in_test)
-    start_all(in_x[0])
-    wk = make_work(ktp, work)
+    own_kernels(weight, gain, shard)
+    for conv in range(2):
+        start_all(k_line[conv])
+    for e in range(examples):
+        start_all(in_x[e])
+        start_all(in_cot[e])
+    wk = make_work(work)
     fill_work(wk)
-    for step in range(1, 4):
-
-        @pl.when(z - step >= 0)
-        def _():
-            up(step - 1).wait_recv()
-            across(step, z - step).start()
-            if step < 3:
-
-                @pl.when(z < 3)
-                def _():
-                    up(step).start()
-
-        @pl.when(z + step <= 3)
-        def _():
-            down(step - 1).wait_recv()
-            across(3 + step, z + step).start()
-            if step < 3:
-
-                @pl.when(z > 0)
-                def _():
-                    down(step).start()
-
-    for step in range(3):
-
-        @pl.when((z < 3) & (z - step >= 0))
-        def _():
-            up(step).wait_send()
-
-        @pl.when((z > 0) & (z + step <= 3))
-        def _():
-            down(step).wait_send()
-
-    across(0, z).wait()
-    for step in range(1, 4):
-
-        @pl.when(z - step >= 0)
-        def _():
-            across(step, z - step).wait()
-
-        @pl.when(z + step <= 3)
-        def _():
-            across(3 + step, z + step).wait()
-
-    own_k.wait()
-    start_all(in_cot[0])
-    unpack_params(wk)
-    turn_kernels(wk)
-    wait_all(in_test)
-
     place = (w, z, c, me)
     direction = Exchange(place, t_conv, t_gn, t_refs, t_sems)
     clipped = Exchange(place, s_conv, s_gn, s_refs, s_sems)
+    direction.clear()
+    clipped.clear()
+    for conv in range(2):
+        ktp[conv, fifth, z, c] = shard[conv, fifth]
+    lane = lax.broadcasted_iota(jnp.int32, (1, LANES), 1)
+    half = lane // PIX
+    sign = jnp.zeros((1, LANES), f32)
+    for p in range(pairs.shape[0]):
+        sign = sign + jnp.where(lax.rem(pairs[p, 0], AUG) == me * 2 + half, 1.0, 0.0)
+        sign = sign - jnp.where(lax.rem(pairs[p, 1], AUG) == me * 2 + half, 1.0, 0.0)
+
+    def slot_weight(e):
+        count = counts[me * examples + e]
+        live = jnp.where(me * examples + e < alive[0], count, 0)
+        each = 1.0 / jnp.full((1, LANES), count.astype(f32))
+        return lambda t: jnp.where(t * 2 + half < live, each, 0.0)
+
+    for conv in range(2):
+        wait_all(k_line[conv])
+        start_all(k_wide[conv])
+    for conv in range(2):
+        wait_all(k_wide[conv])
+        k_core[conv].start()
+
+    def kernel_arrived(conv):
+        k_core[conv].wait()
+        if conv == 0:
+            unpack_params(wk, ktp[0, 18].reshape(C, LANES))
+        for unit in range(18):
+            wk.kf[conv, :, unit * LANES : (unit + 1) * LANES] = ktp[conv, unit].reshape(C, LANES)
+        turn_kernel(wk, conv)
+
+    kernel_arrived(0)
+    wait_all(in_test)
     forward(wk, lambda t: xt[...].astype(f32), 1, None)
-    backward_two(wk, lambda t: ct[...].astype(f32), lambda t: sg[me], 1, tgrad)
+    kernel_arrived(1)
+    backward_two(wk, lambda t: ct[...].astype(f32), lambda t: sign, 1, tgrad)
     backward_one(wk, 1, tgrad, tgn, None)
     raw_gradient(wk, tgrad, sq)
 
@@ -654,28 +695,24 @@
     core_ag = peer_copy(dt.at[c], dt.at[c], s_fin.at[2, 0], r_fin.at[2, 0], narrow=sibling)
 
     def after_forward(e):
-        if e == 0:
-            direction.start_wide()
-        else:
+        if e == 1:
             wait_all(line_ag)
             start_all(wide_ag)
+            start_all(out_block[1])
 
     def between(e):
         if e == 0:
             direction.start_line()
-        else:
-            wait_all(wide_ag)
-            core_ag.start()
 
     def after_backward(e):
         if e == 0:
             direction.finish(own)
             start_all(line_ag)
+            start_all(out_block[0])
+        start_all(out_part[e])
 
     for e in range(examples):
         wait_all(in_x[e])
-        if e + 1 < examples:
-            start_all(in_x[e + 1])
 
         def block_store(t, value):
             block[e, :, lane_tile(t)] = value.astype(bf16)
@@ -683,22 +720,18 @@
         def part_store(t, value):
             part[e, :, lane_tile(t)] = value.astype(bf16)
 
-        forward(wk, lambda t: x[e, :, lane_tile(t)].astype(f32), 8, block_store)
-        start_all(out_block[e])
+        forward(
+            wk,
+            lambda t: x[e, :, lane_tile(t)].astype(f32),
+            8,
+            block_store,
+            direction.start_wide if e == 0 else None,
+        )
         after_forward(e)
         wait_all(in_cot[e])
-        if e + 1 < examples:
-            start_all(in_cot[e + 1])
-        backward_two(
-            wk,
-            lambda t: cot[e, :, lane_tile(t)].astype(f32),
-            lambda t: wl[me * examples + e, :, lane_tile(t)],
-            8,
-            raw.at[e],
-        )
+        backward_two(wk, lambda t: cot[e, :, lane_tile(t)].astype(f32), slot_weight(e), 8, raw.at[e])
         between(e)
         backward_one(wk, 8, raw.at[e], raw_gn.at[e], part_store)
-        start_all(out_part[e])
         after_backward(e)
         sq[...] = jnp.zeros_like(sq)
         raw_gradient(wk, raw.at[e], sq)
@@ -720,8 +753,10 @@
         s_conv[k] = total.astype(bf16).reshape(4, 2, chans, C)
 
     clipped.start_core()
+    wait_all(wide_ag)
+    core_ag.start()
+    clipped.start_wide()
     core_ag.wait()
-    clipped.start_wide()
     inner_products(dt, raw, raw_gn, length, figures, me, chans)
     figs = []
     for k in range(1, n):
@@ -735,11 +770,23 @@
         to = lax.rem(w + k, 4)
         finals.append(peer_copy(red.at[w], red.at[w], s_fin.at[3, k - 1], r_fin.at[3, k - 1], wide=to))
     start_all(finals)
+    wait_all(figs)
+    slot = lax.broadcasted_iota(jnp.int32, (8, LANES), 1)
+    table = jnp.zeros((8, LANES), f32)
+    for k in range(n):
+        for e in range(examples):
+            table = table + jnp.where(slot == k * examples + e, figures[k, e], 0.0)
+    norms[...] = table[0:1, : n * examples]
+    infl[...] = table[1:2, : n * examples]
     for e in range(examples):
         wait_all(out_block[e])
         wait_all(out_part[e])
-    wait_all(figs)
     wait_all(finals)
+    gn_out[...] = red[0, 9]
+    for conv in range(2):
+        for tap in range(9):
+            red_out[conv * 9 + tap, :, :LANES] = red[conv * 2, tap]
+            red_out[conv * 9 + tap, :, LANES:] = red[conv * 2 + 1, tap]
 
 
 def inner_products(dt, raw, raw_gn, length, figures, me, chans):
@@ -777,12 +824,13 @@
         figures[me, e] = jnp.where(top == 0, size, influence)
 
 
-def mega(images, cots, timg, tcot, kshard, wl, sg):
+def mega(images, cots, timg, tcot, weight, gain, pairs, alive, counts):
     held, chans = images.shape[0], images.shape[1]
     examples = held // 8
     out = jax.ShapeDtypeStruct
     anyspace = pl.BlockSpec(memory_space=pl.ANY)
     vmem = pl.BlockSpec(memory_space=pltpu.VMEM)
+    smem = pl.BlockSpec(memory_space=pltpu.SMEM)
     dma = pltpu.SemaphoreType.DMA
     exchange = [
         pltpu.VMEM((18, 4, chans, C), bf16),
@@ -798,7 +846,8 @@
         pltpu.VMEM((examples, C, AUG * PIX), bf16),
         pltpu.VMEM((C, LANES), bf16),
         pltpu.VMEM((C, LANES), bf16),
-        pltpu.VMEM((C, KCOLS + LANES), bf16),
+        pltpu.VMEM((2, UNITS, chans, LANES), bf16),
+        pltpu.VMEM((2, UNITS, 4, 2, chans, LANES), bf16),
         pltpu.VMEM((examples, C, AUG * PIX), bf16),
         pltpu.VMEM((examples, C, AUG * PIX), bf16),
         pltpu.VMEM((examples, 18, C, C), f32),
@@ -812,17 +861,19 @@
         pltpu.VMEM((18, 4, 2, chans, C), bf16),
         pltpu.VMEM((4, 2, chans, LANES), bf16),
         pltpu.VMEM((2, 4, 4, 10, chans, LANES), bf16),
+        pltpu.VMEM((4, 10, chans, LANES), bf16),
+        pltpu.VMEM((8, examples, 8, LANES), f32),
     ]
     kinds = 2 + 2 * examples
     moves = [
         dma((kinds, 7)),
         dma((kinds, 7)),
-        dma((3,)),
-        dma((3,)),
-        dma((3,)),
-        dma((3,)),
-        dma((7,)),
-        dma((7,)),
+        dma((2, 3)),
+        dma((2, 3)),
+        dma((2, 3)),
+        dma((2, 3)),
+        dma((2,)),
+        dma((2,)),
         dma((11,)),
         dma((2 * examples, 7)),
         dma((2 * examples, 7)),
@@ -836,14 +887,16 @@
         out_shape=(
             out((held, chans, AUG * PIX), bf16),
             out((held, chans, AUG * PIX), bf16),
-            out((4, 10, chans, LANES), bf16),
-            out((8, examples, 8, LANES), f32),
+            out((18, chans, C), bf16),
+            out((chans, LANES), bf16),
+            out((1, held), f32),
+            out((1, held), f32),
         ),
-        in_specs=[anyspace] * 5 + [vmem] * 2,
-        out_specs=(anyspace, anyspace, vmem, vmem),
+        in_specs=[anyspace] * 4 + [vmem] * 2 + [smem] * 3,
+        out_specs=(anyspace, anyspace) + (vmem,) * 4,
         scratch_shapes=WORK_SCRATCH + scratch + exchange + exchange + sems + sems + moves,
         compiler_params=pltpu.CompilerParams(collective_id=0, has_side_effects=True, vmem_limit_bytes=60 << 20),
-    )(images, cots, timg, tcot, kshard, wl, sg)
+    )(images, cots, timg, tcot, weight, gain, pairs, alive, counts)
 
 
 def pieces(v):
@@ -894,8 +947,6 @@
     rows = lax.psum(clip_conv, ("wide", "narrow"))
     rows = lax.dynamic_slice_in_dim(rows, own, chans, 1)
     gn_rows = lax.dynamic_slice_in_dim(lax.psum(clip_gn.astype(bf16), ("wide", "narrow")), own, chans, 0)
-    red = rows.reshape(2, 9, chans, 2, LANES).transpose(0, 3, 1, 2, 4).reshape(4, 9, chans, LANES)
-    red = jnp.concatenate([red, jnp.broadcast_to(gn_rows, (4, 1, chans, LANES))], 1)
     d = lax.psum(test_conv, ("wide", "narrow")).astype(f32)
     d_gn = lax.psum(test_gn.astype(bf16), ("wide", "narrow")).astype(f32)
     dir_sq = jnp.sum(d * d) + jnp.sum(d_gn * d_gn)
@@ -904,7 +955,7 @@
     factor = CLIP / jnp.maximum(size, CLIP)
     influence = factor * inner * math.sqrt(18 * C * C + 4 * C) / (CLIP * jnp.sqrt(dir_sq + 1e-06))
     figures = lax.all_gather(jnp.stack([size, influence], 1), "narrow", axis=0)
-    return ob, op, red, figures[:, :, :, None]
+    return ob, op, rows, gn_rows, figures[:, :, 0], figures[:, :, 1]
 
 
 def local(
@@ -943,25 +994,24 @@
         (pairs[:, 1:2] == slots[None, :]).astype(f32), 0
     )
     sign_pixels = jnp.repeat(signs, PIX).reshape(8, LANES) * (1.0 / share)
-    kshard = kernel_rows(conv_weight, gn_params)
     timg, tcot = test_images[0], test_cotangent[0]
-    direct = n_wide == 4 and narrow == 8
-    if direct:
-        block_out, op, red, figures = mega(
-            images, cotangent, timg, tcot, kshard, pixels[:, None, :], sign_pixels[:, None, :]
+    if n_wide == 4 and narrow == 8:
+        weight = conv_weight.transpose(0, 1, 2, 4, 3).reshape(18, chans, C)
+        outs = mega(
+            images, cotangent, timg, tcot, weight, gn_params, pair_index, example_count, aug_count
         )
     else:
+        kshard = kernel_rows(conv_weight, gn_params)
         wl = lax.dynamic_slice_in_dim(pixels, me * examples, examples, 0)[:, None, :]
         sg = lax.dynamic_slice_in_dim(sign_pixels, me // share, 1, 0)
         x, cot, xt, ct, ktp = plain_gather(images, cotangent, timg, tcot, kshard, narrow)
         parts = compute(x, cot, xt, ct, ktp, wl, sg)
-        block_out, op, red, figures = plain_reduce(*parts, chans)
+        outs = plain_reduce(*parts, chans)
+    block_out, op, red, red_gn, lengths, influence = outs
     input_grad = cotangent.astype(f32) * pixels[:, None, :] + op.astype(f32)
-    lengths = figures[:, :, 0, 0].reshape(held)
-    influence = figures[:, :, 1, 0].reshape(held)
-    sum_conv = red[:, :9].reshape(2, 2, 9, chans, LANES).transpose(0, 2, 1, 4, 3)
-    sum_conv = sum_conv.reshape(2, 3, 3, C, chans).astype(f32)
-    sum_norm = red[0, 9, :, :4].T.astype(f32)
+    lengths, influence = lengths.reshape(held), influence.reshape(held)
+    sum_conv = red.reshape(2, 3, 3, chans, C).transpose(0, 1, 2, 4, 3).astype(f32)
+    sum_norm = red_gn[:, :4].T.astype(f32)
     total = held * n_wide
     noisy_conv = (sum_conv + math.sqrt(total) * noise_conv) / total
     noisy_norm = (sum_norm + math.sqrt(total) * noise_gn) / total

time: 197 us -> 159 us (0.81)
  Pallas kernels: 175 us -> 140 us
    pallas_call x1, Pallas kernels: 175 us -> 140 us  [mega(): pl.pallas_call(mega_kernel, out_shape=(out((held, chans, AUG * PIX), bf16...]
    unnamed x25 -> x26, local copies, waits for them, and re-layouts: 1.03 us -> 6.1 us
    mul x0 -> x4, other arithmetic: none -> 2.74 us  [the longest x1 0.69 us: adamw(): first_new = 0.5 * first + 0.5 * grad]
    reduce_sum x3 -> x0, other arithmetic: 2.56 us -> none  [the longest x1 1.28 us: kernel_rows(): spread = jnp.mean(centre * centre, axis=(1, 2, 3), keepdims=True)]
where the time goes in v3:
time: 159 us; the launch traced here: 158 us
  Pallas kernels  140 us (88%)
  other arithmetic  9.64 us (6%)
  local copies, waits for them, and re-layouts  6.63 us (4%)
  between operations  2.16 us (1%)
    pallas_call x1, Pallas kernels, mega(): pl.pallas_call(mega_kernel, out_shape=(out((held, chans, AUG * PIX), bf16...  140 us
    unnamed x26, local copies, waits for them, and re-layouts  6.1 us

profile of v3, /device:TPU:0, one launch (start us, length us, event | category | flops | bytes accessed | tf_op | source)
XLA Modules:
  0.0 158.3 jit_solution(9672308579915289225)
XLA Ops:
  0.6 0.0 copy-start
  2.1 0.7 convert_divide_fusion
  2.7 0.7 broadcast_multiply_fusion.3
  3.4 0.7 broadcast_multiply_fusion.2
  4.1 0.7 broadcast_multiply_fusion.1
  4.8 0.7 broadcast_multiply_fusion
  5.5 1.3 copy.40.pairs
  6.8 0.7 fusion.2
  7.6 0.1 copy.44
  7.6 0.1 copy.41
  7.7 0.1 copy.43
  7.8 0.1 copy.42
  7.9 0.8 copy.45
  8.7 0.1 broadcast_in_dim.21
  8.8 0.1 mul.76
  8.9 139.9 %shard_map.239 = (bf16[16,32,1024]{2,1,0:T(8,128)(2,1)}, bf16[16,32,1024]{2,1,0:T(8,128)(2,1)}, bf16[18,32,256]{2,1,0:T(8,128)(2,1)}, bf16[32,128]{1,0:T(8,128)(2,1)}, f32[1,16]{1,0:T(1,128)}, /*index=5*/f32[1,16]{1,0:T(1,128)}) custom-call(bf16[16,32,1024]{2,1,0:T(8,128)(2,1)} %images.1, bf16[16,32,1024]{2,1,0:T(8,128)(2,1)} %cots.1, ...), custom_call_target="tpu_custom_call" | custom-call | tf_op jit(solution)/shard_map/pallas_call | solution.py:885
  148.7 0.7 multiply_subtract_fusion.1
  149.5 0.7 copy.46
  150.1 0.7 copy.48
  150.8 0.7 copy.47
  151.4 0.0 copy-done
  151.4 0.0 copy-start.1
  151.4 0.0 copy-start.3
  151.4 0.0 copy-start.4
  151.4 0.0 copy-start.5
  151.5 0.0 copy-start.6
  151.5 3.1 %convert_add_fusion = f32[16,32,1024]{2,1,0:T(8,128)} fusion(bf16[16,32,1024]{2,1,0:T(8,128)(2,1)} %get-tuple-element.18, bf16[16,32,1024]{2,1,0:T(8,128)(2,1)S(1)} %copy-done, f32[16,1024]{1,0:T(8,128)S(1)} %mul.76), kind=kLoop, calls=%fused_computation | loop fusion | flops 2097152 | bytes 4259840 | tf_op jit(solution)/shard_map/add | solution.py:1011
  154.6 0.0 copy-done.1
  154.6 0.0 copy-done.3
  154.6 0.0 copy-done.4
  154.6 0.0 copy-done.5
  154.6 0.0 copy-done.6
  154.6 0.0 copy-start.2
  154.6 1.7 %fusion.3 = (bf16[2,3,3,256,32]{3,4,2,1,0:T(8,128)(2,1)}, f32[2,3,3,256,32]{3,4,2,1,0:T(8,128)}, f32[2,3,3,256,32]{3,4,2,1,0:T(8,128)}, f32[2,3,3,256,32]{3,4,2,1,0:T(8,128)}) fusion(f32[2,3,3,256,32]{3,4,2,1,0:T(8,128)S(1)} %copy-done.1, f32[]{:T(128)} %bitcast.9, f32[2,3,3,256,32]{3,4,2,1,0:T(8,128)S(1)} %copy-done.3, ...), kind=kLoop, calls=%fused_computation.19 | loop fusion | flops 2801664 | bytes 4718596 | tf_op jit(solution)/shard_map/convert_element_type | solution.py:1031
  156.3 0.0 copy-start.8
  156.3 0.0 copy-start.7
  156.3 0.0 copy-done.2
  156.3 1.0 copy.54
  157.3 0.0 copy-done.8
  157.3 0.5 copy.55
  157.8 0.0 copy-done.7
  157.8 0.5 copy.56
  (1 shorter events, 0.0 us)
Async XLA Ops:
  0.6 150.8 %copy-start = (bf16[16,32,1024]{2,1,0:T(8,128)(2,1)S(1)}, bf16[16,32,1024]{2,1,0:T(8,128)(2,1)}, u32[]{:S(2)}) copy-start(bf16[16,32,1024]{2,1,0:T(8,128)(2,1)} %cots.1) | copy-start | bytes 3145732
  151.4 3.1 %copy-start.1 = (f32[2,3,3,256,32]{3,4,2,1,0:T(8,128)S(1)}, f32[2,3,3,256,32]{3,4,2,1,0:T(8,128)}, u32[]{:S(2)}) copy-start(f32[2,3,3,256,32]{3,4,2,1,0:T(8,128)} %param.23) | copy-start | bytes 1769476
  151.4 3.1 %copy-start.3 = (f32[2,3,3,256,32]{3,4,2,1,0:T(8,128)S(1)}, f32[2,3,3,256,32]{3,4,2,1,0:T(8,128)}, u32[]{:S(2)}) copy-start(f32[2,3,3,256,32]{3,4,2,1,0:T(8,128)} %param.29) | copy-start | bytes 1769476
  151.4 3.1 %copy-start.4 = (f32[2,3,3,256,32]{3,4,2,1,0:T(8,128)S(1)}, f32[2,3,3,256,32]{3,4,2,1,0:T(8,128)}, u32[]{:S(2)}) copy-start(f32[2,3,3,256,32]{3,4,2,1,0:T(8,128)} %param.26) | copy-start | bytes 1769476
  151.4 3.1 %copy-start.5 = (f32[2,3,3,256,32]{3,4,2,1,0:T(8,128)S(1)}, f32[2,3,3,256,32]{3,4,2,1,0:T(8,128)}, u32[]{:S(2)}) copy-start(f32[2,3,3,256,32]{3,4,2,1,0:T(8,128)} %param.25) | copy-start | bytes 1769476
  151.5 3.1 %copy-start.6 = (bf16[18,32,256]{2,1,0:T(8,128)(2,1)S(1)}, bf16[18,32,256]{2,1,0:T(8,128)(2,1)}, u32[]{:S(2)}) copy-start(bf16[18,32,256]{2,1,0:T(8,128)(2,1)} %get-tuple-element.21) | copy-start | bytes 884740
  154.6 1.7 %copy-start.2 = (bf16[16,32,1024]{2,1,0:T(8,128)(2,1)S(1)}, bf16[16,32,1024]{2,1,0:T(8,128)(2,1)}, u32[]{:S(2)}) copy-start(bf16[16,32,1024]{2,1,0:T(8,128)(2,1)} %get-tuple-element.63) | copy-start | bytes 3145732
  156.3 1.0 copy-start.8
  156.3 1.5 copy-start.7

commit v4 on v3

--- a/solution.py
+++ b/solution.py
@@ -642,9 +642,9 @@
     lane = lax.broadcasted_iota(jnp.int32, (1, LANES), 1)
     half = lane // PIX
     sign = jnp.zeros((1, LANES), f32)
-    for p in range(pairs.shape[0]):
-        sign = sign + jnp.where(lax.rem(pairs[p, 0], AUG) == me * 2 + half, 1.0, 0.0)
-        sign = sign - jnp.where(lax.rem(pairs[p, 1], AUG) == me * 2 + half, 1.0, 0.0)
+    for p in range(pairs.shape[1]):
+        sign = sign + jnp.where(lax.rem(pairs[0, p], AUG) == me * 2 + half, 1.0, 0.0)
+        sign = sign - jnp.where(lax.rem(pairs[1, p], AUG) == me * 2 + half, 1.0, 0.0)
 
     def slot_weight(e):
         count = counts[me * examples + e]
@@ -655,11 +655,10 @@
     for conv in range(2):
         wait_all(k_line[conv])
         start_all(k_wide[conv])
-    for conv in range(2):
+
+    def kernel_arrived(conv):
         wait_all(k_wide[conv])
         k_core[conv].start()
-
-    def kernel_arrived(conv):
         k_core[conv].wait()
         if conv == 0:
             unpack_params(wk, ktp[0, 18].reshape(C, LANES))
@@ -899,6 +898,106 @@
     )(images, cots, timg, tcot, weight, gain, pairs, alive, counts)
 
 
+def update(weight, first, second, grad, correction, rate, decay):
+    first_new = 0.5 * first + 0.5 * grad
+    second_new = 0.5 * second + 0.5 * grad * grad
+    step = first_new / correction / (jnp.sqrt(second_new / correction) + 1e-08)
+    return weight - rate * (step + decay * weight), first_new, second_new
+
+
+def tail_kernel(
+    total, alive, counts, steps, ob, op, cots, red, red_gn, weight, m1, m2, noise, gw, g1, g2, gnoise, norms, infl,
+    block_out, grad_out, new, low, first, second, gnew, gfirst, gsecond, norms_out, infl_out
+):
+    step = pl.program_id(0)
+    held = ob.shape[0]
+    block_out[...] = ob[...]
+    image = lax.broadcasted_iota(jnp.int32, (1, AUG * PIX), 1) // PIX
+    for j in range(held):
+        e = step * held + j
+        count = counts[e]
+        live = jnp.where(e < alive[0], count, 0)
+        each = 1.0 / jnp.full((1, AUG * PIX), count.astype(f32))
+        row = jnp.where(image < live, each, 0.0)
+        grad_out[j] = cots[j].astype(f32) * row + op[j].astype(f32)
+    correction = 1.0 - jnp.exp2(jnp.full((1, 1), -steps[0].astype(f32)))
+    grad = (red[...].astype(f32) + math.sqrt(total) * noise[...]) * (1.0 / total)
+    value, one, two = update(weight[...], m1[...], m2[...], grad, correction, 1.0 / math.sqrt(FAN), 0.1)
+    new[...] = value
+    low[...] = value.astype(bf16)
+    first[...] = one
+    second[...] = two
+
+    @pl.when(step == 0)
+    def _():
+        chans = red_gn.shape[0]
+        eye = lax.broadcasted_iota(jnp.int32, (chans, chans), 0) == lax.broadcasted_iota(
+            jnp.int32, (chans, chans), 1
+        )
+        for k in range(4):
+            column = red_gn[:, k : k + 1].astype(f32)
+            row = jnp.sum(jnp.where(eye, jnp.broadcast_to(column, (chans, chans)), 0.0), axis=0, keepdims=True)
+            at = slice(k, k + 1)
+            grad = (row + math.sqrt(total) * gnoise[at, :]) * (1.0 / total)
+            value, one, two = update(gw[at, :], g1[at, :], g2[at, :], grad, correction, 0.1, 0.0)
+            gnew[at, :] = value
+            gfirst[at, :] = one
+            gsecond[at, :] = two
+        norms_out[...] = norms[...]
+        infl_out[...] = infl[...]
+
+
+def finish(total, alive, counts, steps, ob, op, cots, red, red_gn, conv, gn, norms, infl):
+    held, chans = ob.shape[0], ob.shape[1]
+    grid = 4
+    rows = 18 * chans
+    smem = pl.BlockSpec(memory_space=pltpu.SMEM)
+    images = pl.BlockSpec((held // grid, chans, AUG * PIX), lambda i: (i, 0, 0))
+    part = pl.BlockSpec((rows // grid, C), lambda i: (i, 0))
+
+    def whole(v):
+        return pl.BlockSpec(v.shape, lambda i: (0,) * len(v.shape))
+
+    def out(v, kind=None):
+        return jax.ShapeDtypeStruct(v.shape, kind or v.dtype)
+
+    flat = [v.transpose(0, 1, 2, 4, 3).reshape(rows, C) for v in conv]
+    outs = pl.pallas_call(
+        functools.partial(tail_kernel, total),
+        grid=(grid,),
+        out_shape=[out(ob), out(ob, f32)]
+        + [out(flat[0]), out(flat[0], bf16), out(flat[0]), out(flat[0])]
+        + [out(gn[0])] * 3
+        + [out(norms), out(infl)],
+        in_specs=[smem] * 3
+        + [images] * 3
+        + [part, whole(red_gn)]
+        + [part] * 4
+        + [whole(gn[0])] * 4
+        + [whole(norms), whole(infl)],
+        out_specs=[images] * 2 + [part] * 4 + [whole(gn[0])] * 3 + [whole(norms), whole(infl)],
+        compiler_params=pltpu.CompilerParams(vmem_limit_bytes=62 << 20),
+    )(alive, counts, steps, ob, op, cots, red.reshape(rows, C), red_gn, *flat, *gn, norms, infl)
+
+    def back(v):
+        return v.reshape(2, 3, 3, chans, C).transpose(0, 1, 2, 4, 3)
+
+    block_out, grad_out, new, low, first, second, gnew, gfirst, gsecond, norms, infl = outs
+    return (
+        block_out,
+        grad_out,
+        norms.reshape(held),
+        infl.reshape(held),
+        back(new),
+        back(low),
+        back(first),
+        back(second),
+        gnew,
+        gfirst,
+        gsecond,
+    )
+
+
 def pieces(v):
     high = lax.reduce_precision(v, 8, 7)
     rest = v - high
@@ -917,13 +1016,6 @@
     small = jnp.concatenate([gn_params.T, scale.reshape(2, chans).T, jnp.zeros((chans, 2), f32)], 1)
     tail = jnp.concatenate(list(pieces(small)) + [jnp.zeros((chans, LANES - 24), bf16)], 1)
     return jnp.concatenate([rows, tail], 1)
-
-
-def adamw(weight, first, second, grad, correction, rate, decay):
-    first_new = 0.5 * first + 0.5 * grad
-    second_new = 0.5 * second + 0.5 * grad * grad
-    update = first_new / correction / (jnp.sqrt(second_new / correction) + 1e-08)
-    return (weight - rate * (update + decay * weight), first_new, second_new)
 
 
 def plain_gather(images, cots, timg, tcot, kshard, narrow):
@@ -981,26 +1073,26 @@
     examples = held // narrow
     share = narrow // 8
     me = lax.axis_index("narrow")
-    slots = jnp.arange(AUG, dtype=jnp.int32)
-    live = jnp.arange(held, dtype=jnp.int32) < example_count[0]
-    weights = jnp.where(
-        live[:, None] & (slots[None, :] < aug_count[:, None]),
-        1.0 / aug_count.astype(f32)[:, None],
-        f32(0.0),
-    )
-    pixels = jnp.repeat(weights, PIX, axis=1)
-    pairs = pair_index % AUG
-    signs = jnp.sum((pairs[:, 0:1] == slots[None, :]).astype(f32), 0) - jnp.sum(
-        (pairs[:, 1:2] == slots[None, :]).astype(f32), 0
-    )
-    sign_pixels = jnp.repeat(signs, PIX).reshape(8, LANES) * (1.0 / share)
     timg, tcot = test_images[0], test_cotangent[0]
     if n_wide == 4 and narrow == 8:
         weight = conv_weight.transpose(0, 1, 2, 4, 3).reshape(18, chans, C)
         outs = mega(
-            images, cotangent, timg, tcot, weight, gn_params, pair_index, example_count, aug_count
+            images, cotangent, timg, tcot, weight, gn_params, pair_index.T, example_count, aug_count
         )
     else:
+        slots = jnp.arange(AUG, dtype=jnp.int32)
+        live = jnp.arange(held, dtype=jnp.int32) < example_count[0]
+        weights = jnp.where(
+            live[:, None] & (slots[None, :] < aug_count[:, None]),
+            1.0 / aug_count.astype(f32)[:, None],
+            f32(0.0),
+        )
+        pixels = jnp.repeat(weights, PIX, axis=1)
+        pairs = pair_index % AUG
+        signs = jnp.sum((pairs[:, 0:1] == slots[None, :]).astype(f32), 0) - jnp.sum(
+            (pairs[:, 1:2] == slots[None, :]).astype(f32), 0
+        )
+        sign_pixels = jnp.repeat(signs, PIX).reshape(8, LANES) * (1.0 / share)
         kshard = kernel_rows(conv_weight, gn_params)
         wl = lax.dynamic_slice_in_dim(pixels, me * examples, examples, 0)[:, None, :]
         sg = lax.dynamic_slice_in_dim(sign_pixels, me // share, 1, 0)
@@ -1008,32 +1100,20 @@
         parts = compute(x, cot, xt, ct, ktp, wl, sg)
         outs = plain_reduce(*parts, chans)
     block_out, op, red, red_gn, lengths, influence = outs
-    input_grad = cotangent.astype(f32) * pixels[:, None, :] + op.astype(f32)
-    lengths, influence = lengths.reshape(held), influence.reshape(held)
-    sum_conv = red.reshape(2, 3, 3, chans, C).transpose(0, 1, 2, 4, 3).astype(f32)
-    sum_norm = red_gn[:, :4].T.astype(f32)
-    total = held * n_wide
-    noisy_conv = (sum_conv + math.sqrt(total) * noise_conv) / total
-    noisy_norm = (sum_norm + math.sqrt(total) * noise_gn) / total
-    correction = 1.0 - jnp.power(f32(0.5), step_count[0].astype(f32))
-    conv_new, conv_first, conv_second = adamw(
-        conv_weight, conv_moment1, conv_moment2, noisy_conv, correction, 1.0 / math.sqrt(9 * C), 0.1
-    )
-    gn_new, gn_first, gn_second = adamw(
-        gn_params, gn_moment1, gn_moment2, noisy_norm, correction, 0.1, 0.0
-    )
-    return (
+    return finish(
+        held * n_wide,
+        example_count,
+        aug_count,
+        step_count,
         block_out,
-        input_grad,
-        lengths,
-        influence,
-        conv_new,
-        conv_new.astype(bf16),
-        conv_first,
-        conv_second,
-        gn_new,
-        gn_first,
-        gn_second,
+        op,
+        cotangent,
+        red,
+        red_gn,
+        (conv_weight, conv_moment1, conv_moment2, noise_conv),
+        (gn_params, gn_moment1, gn_moment2, noise_gn),
+        lengths.reshape(1, held),
+        influence.reshape(1, held),
     )
 
 

time: 159 us -> 149 us (0.937)
  other arithmetic: 9.64 us -> 0 us
  local copies, waits for them, and re-layouts: 6.63 us -> 0 us
  Pallas kernels: 140 us -> 146 us
    unnamed x26 -> x0, local copies, waits for them, and re-layouts: 6.1 us -> none
    pallas_call x0 -> x1, Pallas kernels: none -> 5.85 us  [finish(): pl.pallas_call(functools.partial(tail_kernel, total), grid=(grid,), out_s...]
    add x1 -> x0, other arithmetic: 3.11 us -> none  [local(): input_grad = cotangent.astype(f32) * pixels[:, None, :] + op.astype(f32)]
    mul x4 -> x0, other arithmetic: 2.74 us -> none  [the longest x1 0.69 us: adamw(): first_new = 0.5 * first + 0.5 * grad]
    convert_element_type x1 -> x0, other arithmetic: 1.68 us -> none  [local(): conv_new.astype(bf16)]
where the time goes in v4:
time: 149 us; the launch traced here: 148 us
  Pallas kernels  146 us (98%)
  between operations  2.13 us (1%)
    pallas_call x1, Pallas kernels, mega(): pl.pallas_call(mega_kernel, out_shape=(out((held, chans, AUG * PIX), bf16...  141 us
    pallas_call x1, Pallas kernels, finish(): pl.pallas_call(functools.partial(tail_kernel, total), grid=(grid,), out_s...  5.85 us

profile of v4, /device:TPU:0, one launch (start us, length us, event | category | flops | bytes accessed | tf_op | source)
XLA Modules:
  0.0 148.5 jit_solution(4287960152720659788)
XLA Ops:
  1.9 140.5 %shard_map.239 = (bf16[16,32,1024]{2,1,0:T(8,128)(2,1)}, bf16[16,32,1024]{2,1,0:T(8,128)(2,1)}, bf16[18,32,256]{2,1,0:T(8,128)(2,1)}, bf16[32,128]{1,0:T(8,128)(2,1)}, f32[1,16]{1,0:T(1,128)}, /*index=5*/f32[1,16]{1,0:T(1,128)}) custom-call(bf16[16,32,1024]{2,1,0:T(8,128)(2,1)} %images.1, bf16[16,32,1024]{2,1,0:T(8,128)(2,1)} %cots.3, ...), custom_call_target="tpu_custom_call" | custom-call | tf_op jit(solution)/shard_map/pallas_call | solution.py:884
  142.5 5.9 %shard_map.240 = (bf16[16,32,1024]{2,1,0:T(8,128)(2,1)}, f32[16,32,1024]{2,1,0:T(8,128)}, f32[576,256]{1,0:T(8,128)}, bf16[576,256]{1,0:T(8,128)(2,1)}, f32[576,...) custom-call(s32[1]{0:T(128)S(6)} %copy.27.alive, ...), custom_call_target="tpu_custom_call" | custom-call | tf_op jit(solution)/shard_map/pallas_call | solution.py:965

commit v5 on v4

--- a/solution.py
+++ b/solution.py
@@ -35,13 +35,11 @@
 
 
 def image_sum(rows, ones):
-    return lax.dot_general(
-        rows,
-        ones,
-        (((1,), (0,)), ((), ())),
-        precision=lax.Precision.HIGHEST,
-        preferred_element_type=f32,
-    )
+    high = rows.astype(bf16)
+    rest = rows - high.astype(f32)
+    mid = rest.astype(bf16)
+    low = (rest - mid.astype(f32)).astype(bf16)
+    return product(jnp.concatenate([high, mid, low], axis=1), ones)
 
 
 def sigmoid(z):
@@ -86,14 +84,14 @@
 def norm_forward(wk, load, tiles, which, hat, rstd, hidden, col):
     stat = wk.stat
 
-    @pl.loop(0, tiles)
+    @pl.loop(0, tiles, unroll=tiles)
     def _(t):
         stat[pl.ds(pl.multiple_of(t * GROUPS, GROUPS), GROUPS), :] = group_sum(load(t))
 
     rows = tiles * GROUPS
     stat[:rows, :] = image_sum(stat[:rows, :], wk.ones[...]) * (1.0 / (PIX * C // GROUPS))
 
-    @pl.loop(0, tiles)
+    @pl.loop(0, tiles, unroll=tiles)
     def _(t):
         at = pl.ds(pl.multiple_of(t * GROUPS, GROUPS), GROUPS)
         centre = load(t) - spread_group(stat[at, :])
@@ -103,7 +101,7 @@
     spread = image_sum(stat[:rows, :], wk.ones[...]) * (1.0 / (PIX * C // GROUPS))
     rstd[:rows, :] = lax.rsqrt(spread + 1e-05)
 
-    @pl.loop(0, tiles)
+    @pl.loop(0, tiles, unroll=tiles)
     def _(t):
         at = pl.ds(pl.multiple_of(t * GROUPS, GROUPS), GROUPS)
         normed = hat[:, lane_tile(t)] * spread_group(rstd[at, :])
@@ -120,7 +118,7 @@
     acc[0] = jnp.zeros((C, LANES), f32)
     acc[1] = jnp.zeros((C, LANES), f32)
 
-    @pl.loop(0, tiles)
+    @pl.loop(0, tiles, unroll=tiles)
     def _(t):
         at = pl.ds(pl.multiple_of(t * GROUPS, GROUPS), GROUPS)
         normed = hat[:, lane_tile(t)]
@@ -140,7 +138,7 @@
         stat[:rows, :] = image_sum(stat[:rows, :], wk.ones[...]) * scale
         stat2[:rows, :] = image_sum(stat2[:rows, :], wk.ones[...]) * scale
 
-        @pl.loop(0, tiles)
+        @pl.loop(0, tiles, unroll=tiles)
         def _(t):
             at = pl.ds(pl.multiple_of(t * GROUPS, GROUPS), GROUPS)
             value = grad[:, lane_tile(t)] - spread_group(stat[at, :])
@@ -155,9 +153,9 @@
 
 
 def fill_work(wk):
-    half_a = lax.broadcasted_iota(jnp.int32, (LANES, LANES), 0) // PIX
-    half_b = lax.broadcasted_iota(jnp.int32, (LANES, LANES), 1) // PIX
-    wk.ones[...] = jnp.where(half_a == half_b, 1.0, 0.0).astype(f32)
+    half_a = (lax.broadcasted_iota(jnp.int32, (3 * LANES, LANES), 0) // PIX) % 2
+    half_b = lax.broadcasted_iota(jnp.int32, (3 * LANES, LANES), 1) // PIX
+    wk.ones[...] = jnp.where(half_a == half_b, 1.0, 0.0).astype(f32).astype(bf16)
     wk.masks = tap_masks()
 
 
@@ -200,7 +198,7 @@
     if block_store is not None:
         matmul_cols(wk.mid, wk.kf[1], cols(wk.col, width), width)
 
-        @pl.loop(0, tiles)
+        @pl.loop(0, tiles, unroll=tiles)
         def _(t):
             block_store(t, x_load(t) + wk.mid[:, lane_tile(t)])
 
@@ -208,7 +206,7 @@
 def backward_two(wk, cot_load, weight_load, tiles, grads):
     width = tiles * LANES
 
-    @pl.loop(0, tiles)
+    @pl.loop(0, tiles, unroll=tiles)
     def _(t):
         store_taps((cot_load(t) * weight_load(t)).astype(bf16), wk.col, t, wk.masks, True)
 
@@ -282,7 +280,7 @@
     pltpu.VMEM((LANES, LANES), f32),
     pltpu.VMEM((LANES, LANES), f32),
     pltpu.VMEM((LANES, LANES), f32),
-    pltpu.VMEM((LANES, LANES), f32),
+    pltpu.VMEM((3 * LANES, LANES), bf16),
     pltpu.VMEM((4, C, LANES), f32),
     pltpu.VMEM((2, C, LANES), f32),
     pltpu.VMEM((2, 2, C, LANES), f32),
@@ -411,11 +409,27 @@
     pl.semaphore_wait(barrier, len(peers))
 
 
+def near_of(z, c):
+    return (z + 1 - 2 * (z % 2)) * 2 + c
+
+
+def far_of(z, c):
+    return lax.rem(z + 2, 4) * 2 + c
+
+
+GRID = 2
+A = 4
+B = 8
+D = 5
+E = 6
+F = 2
+
+
 class Exchange:
     def __init__(self, place, conv, gn, refs, sems):
         self.w, self.z, self.c, self.me = place
         self.conv, self.gn = conv, gn
-        self.cb, self.cg, self.half, self.wb, self.quarter, self.zb = refs
+        self.cb, self.cg, self.half, self.wb, self.quarter, self.nb, self.mid, self.fb = refs
         s_core, r_core, s_wide, r_wide, s_z, r_z = sems
         w, z, c = self.w, self.z, self.c
         sibling = self.me + 1 - 2 * c
@@ -423,31 +437,27 @@
             peer_copy(conv.at[:, :, 1 - c], self.cb, s_core.at[0], r_core.at[0], narrow=sibling),
             peer_copy(gn.at[:, 1 - c], self.cg, s_core.at[1], r_core.at[1], narrow=sibling),
         ]
-        self.wide, self.line = [], []
+        self.wide = []
         for k in range(1, 4):
             to = lax.rem(w + k, 4)
             self.wide.append(
                 peer_copy(self.half.at[to], self.wb.at[k - 1], s_wide.at[k - 1], r_wide.at[k - 1], wide=to)
             )
-        for k in range(1, 4):
-            to = lax.rem(z + k, 4)
-            self.line.append(
-                peer_copy(
-                    self.quarter.at[:, to], self.zb.at[k - 1], s_z.at[k - 1], r_z.at[k - 1], narrow=to * 2 + c
-                )
-            )
+        self.p, self.h = z % 2, z // 2
+        self.near = peer_copy(
+            self.quarter.at[:, :, 1 - self.p], self.nb, s_z.at[0], r_z.at[0], narrow=near_of(z, c)
+        )
+        self.far = peer_copy(self.mid.at[:, 1 - self.h], self.fb, s_z.at[1], r_z.at[1], narrow=far_of(z, c))
 
     def clear(self):
         for q in range(1, 4):
             self.half[q, 9] = jnp.zeros_like(self.half[q, 9])
 
     def start_core(self):
-        for copy in self.core:
-            copy.start()
+        start_all(self.core)
 
     def start_wide(self):
-        for copy in self.core:
-            copy.wait()
+        wait_all(self.core)
         half, c = self.half, self.c
         for k in range(2):
 
@@ -458,33 +468,37 @@
                 half[k * 2 + 1, tap] = total[:, :, LANES:].astype(bf16)
 
         half[0, 9] = (self.gn[:, c].astype(f32) + self.cg[...].astype(f32)).astype(bf16)
-        for copy in self.wide:
-            copy.start()
-
-    def start_line(self):
-        for copy in self.wide:
-            copy.wait()
+        start_all(self.wide)
+
+    def start_near(self):
+        wait_all(self.wide)
 
         @pl.loop(0, 10)
         def _(tap):
-            total = self.half[self.w, tap].astype(f32)
-            for k in range(3):
-                total = total + self.wb[k, tap].astype(f32)
-            self.quarter[tap] = total.astype(bf16)
-
-        for copy in self.line:
-            copy.start()
-
-    def finish(self, out):
-        for copy in self.line:
-            copy.wait()
+            for zz in range(4):
+                total = self.half[self.w, tap, zz].astype(f32)
+                for k in range(3):
+                    total = total + self.wb[k, tap, zz].astype(f32)
+                self.quarter[tap, zz // 2, zz % 2] = total.astype(bf16)
+
+        start_all([self.near])
+
+    def start_far(self):
+        wait_all([self.near])
 
         @pl.loop(0, 10)
         def _(tap):
-            total = self.quarter[tap, self.z].astype(f32)
-            for k in range(3):
-                total = total + self.zb[k, tap].astype(f32)
-            out[tap] = total.astype(bf16)
+            total = self.quarter[tap, :, self.p].astype(f32) + self.nb[tap].astype(f32)
+            self.mid[tap] = total.astype(bf16)
+
+        start_all([self.far])
+
+    def finish(self, out):
+        wait_all([self.far])
+
+        @pl.loop(0, 10)
+        def _(tap):
+            out[tap] = (self.mid[tap, self.h].astype(f32) + self.fb[tap].astype(f32)).astype(bf16)
 
 
 def start_all(copies):
@@ -500,7 +514,7 @@
 UNITS = 20
 
 
-def own_kernels(weight, gain, shard):
+def own_kernels(weight, gain, shard, sent):
     chans = weight.shape[1]
     lane = lax.broadcasted_iota(jnp.int32, (chans, LANES), 1)
     eye = lax.broadcasted_iota(jnp.int32, (chans, chans), 0) == lax.broadcasted_iota(
@@ -510,6 +524,7 @@
         jnp.sum(jnp.where(eye, jnp.broadcast_to(gain[k : k + 1, :], (chans, chans)), 0.0), axis=1, keepdims=True)
         for k in range(4)
     ]
+    means = []
     for conv in range(2):
         total = jnp.zeros((chans, C), f32)
         for tap in range(9):
@@ -520,12 +535,8 @@
             centre = weight[conv * 9 + tap] - mean
             total = total + centre * centre
         spread = jnp.sum(total, axis=1, keepdims=True) * (1.0 / FAN)
-        scale = lax.rsqrt(FAN * spread + 1e-06)
-        values.append(scale)
-        for tap in range(9):
-            kernel = ((weight[conv * 9 + tap] - mean) * scale).astype(bf16)
-            shard[conv, 2 * tap] = kernel[:, :LANES]
-            shard[conv, 2 * tap + 1] = kernel[:, LANES:]
+        means.append(mean)
+        values.append(lax.rsqrt(FAN * spread + 1e-06))
     tail = jnp.zeros((chans, LANES), f32)
     for k, value in enumerate(values):
         high = value.astype(bf16).astype(f32)
@@ -534,11 +545,15 @@
         tail = tail + jnp.where(lane == k, high, 0.0)
         tail = tail + jnp.where(lane == 8 + k, mid, 0.0)
         tail = tail + jnp.where(lane == 16 + k, low, 0.0)
-    shard[0, 18] = tail.astype(bf16)
     zero = jnp.zeros((chans, LANES), bf16)
-    shard[0, 19] = zero
-    shard[1, 18] = zero
-    shard[1, 19] = zero
+    for conv in range(2):
+        for tap in range(9):
+            kernel = ((weight[conv * 9 + tap] - means[conv]) * values[4 + conv]).astype(bf16)
+            shard[conv, 2 * tap] = kernel[:, :LANES]
+            shard[conv, 2 * tap + 1] = kernel[:, LANES:]
+        shard[conv, 18] = tail.astype(bf16) if conv == 0 else zero
+        shard[conv, 19] = zero
+        sent(conv)
 
 
 def mega_kernel(
@@ -555,10 +570,10 @@
     work, rest = scratch[: len(WORK_SCRATCH)], scratch[len(WORK_SCRATCH) :]
     x, cot, xt, ct, shard, ktp, block, part, raw, raw_gn, length, tgrad, tgn, sq = rest[:14]
     s_conv, s_gn, t_conv, t_gn, dt, red, figures = rest[14:21]
-    s_refs, t_refs = rest[21:27], rest[27:33]
-    s_sems, t_sems = rest[33:39], rest[39:45]
-    s_in, r_in, s_kz, r_kz, s_kw, r_kw, s_kc, r_kc, s_loc = rest[45:54]
-    s_out, r_out, s_fin, r_fin, s_fig, r_fig = rest[54:60]
+    s_refs, t_refs = rest[21:29], rest[29:37]
+    s_sems, t_sems = rest[37:43], rest[43:49]
+    s_in, r_in, s_kz, r_kz, s_kw, r_kw, s_kc, r_kc, s_loc = rest[49:58]
+    s_out, r_out, s_fin, r_fin, s_fig, r_fig = rest[58:64]
     greet(
         [{"narrow": lax.rem(me + k, n)} for k in range(1, n)]
         + [{"wide": lax.rem(w + k, 4)} for k in range(1, 4)]
@@ -599,34 +614,39 @@
     out_block = [give_back(0, e, block, ob) for e in range(examples)]
     out_part = [give_back(1, e, part, op) for e in range(examples)]
     fifth = pl.ds(w * (UNITS // 4), UNITS // 4)
-    k_line, k_wide, k_core = [], [], []
+    h, p = z // 2, z % 2
+    k_far, k_near, k_wide, k_core = [], [], [], []
     for conv in range(2):
-        k_line.append(
+        k_far.append(
             [
                 peer_copy(
                     shard.at[conv, fifth],
-                    ktp.at[conv, fifth, z, c],
-                    s_kz.at[conv, k - 1],
-                    r_kz.at[conv, k - 1],
-                    narrow=lax.rem(z + k, 4) * 2 + c,
+                    ktp.at[conv, fifth, h, p, c],
+                    s_kz.at[conv, 0],
+                    r_kz.at[conv, 0],
+                    narrow=far_of(z, c),
                 )
-                for k in range(1, 4)
             ]
         )
-        held = ktp.at[conv, fifth, :, c]
+        held = ktp.at[conv, fifth, :, p, c]
+        k_near.append([peer_copy(held, held, s_kz.at[conv, 1], r_kz.at[conv, 1], narrow=near_of(z, c))])
+        held = ktp.at[conv, fifth, :, :, c]
         k_wide.append(
             [
                 peer_copy(held, held, s_kw.at[conv, k - 1], r_kw.at[conv, k - 1], wide=lax.rem(w + k, 4))
                 for k in range(1, 4)
             ]
         )
-        held = ktp.at[conv, :, :, c]
-        k_core.append(peer_copy(held, held, s_kc.at[conv], r_kc.at[conv], narrow=sibling))
-
+        held = ktp.at[conv, :, :, :, c]
+        k_core.append([peer_copy(held, held, s_kc.at[conv], r_kc.at[conv], narrow=sibling)])
+
+    own_kernels(weight, gain, shard, lambda conv: start_all(k_far[conv]))
     start_all(in_test)
-    own_kernels(weight, gain, shard)
     for conv in range(2):
-        start_all(k_line[conv])
+        ktp[conv, fifth, h, p, c] = shard[conv, fifth]
+    for conv in range(2):
+        wait_all(k_far[conv])
+        start_all(k_near[conv])
     for e in range(examples):
         start_all(in_x[e])
         start_all(in_cot[e])
@@ -637,8 +657,6 @@
     clipped = Exchange(place, s_conv, s_gn, s_refs, s_sems)
     direction.clear()
     clipped.clear()
-    for conv in range(2):
-        ktp[conv, fifth, z, c] = shard[conv, fifth]
     lane = lax.broadcasted_iota(jnp.int32, (1, LANES), 1)
     half = lane // PIX
     sign = jnp.zeros((1, LANES), f32)
@@ -653,13 +671,13 @@
         return lambda t: jnp.where(t * 2 + half < live, each, 0.0)
 
     for conv in range(2):
-        wait_all(k_line[conv])
+        wait_all(k_near[conv])
         start_all(k_wide[conv])
 
     def kernel_arrived(conv):
         wait_all(k_wide[conv])
-        k_core[conv].start()
-        k_core[conv].wait()
+        start_all(k_core[conv])
+        wait_all(k_core[conv])
         if conv == 0:
             unpack_params(wk, ktp[0, 18].reshape(C, LANES))
         for unit in range(18):
@@ -681,34 +699,35 @@
     t_gn[...] = tgn[...].astype(bf16).reshape(4, 2, chans, LANES)
     direction.start_core()
 
-    own = dt.at[c, w, z]
-    line_ag, wide_ag = [], []
-    for k in range(1, 4):
-        to = lax.rem(z + k, 4)
-        line_ag.append(peer_copy(own, own, s_fin.at[0, k - 1], r_fin.at[0, k - 1], narrow=to * 2 + c))
+    own = dt.at[c, w, z // 2, z % 2]
+    both = dt.at[c, w, :, z % 2]
+    far_ag = [peer_copy(own, own, s_fin.at[0, 0], r_fin.at[0, 0], narrow=far_of(z, c))]
+    near_ag = [peer_copy(both, both, s_fin.at[0, 1], r_fin.at[0, 1], narrow=near_of(z, c))]
+    wide_ag = []
     for k in range(1, 4):
         to = lax.rem(w + k, 4)
         wide_ag.append(
             peer_copy(dt.at[c, w], dt.at[c, w], s_fin.at[1, k - 1], r_fin.at[1, k - 1], wide=to)
         )
-    core_ag = peer_copy(dt.at[c], dt.at[c], s_fin.at[2, 0], r_fin.at[2, 0], narrow=sibling)
-
-    def after_forward(e):
+    core_ag = [peer_copy(dt.at[c], dt.at[c], s_fin.at[2, 0], r_fin.at[2, 0], narrow=sibling)]
+
+    def early_forward(e):
+        if e == 0:
+            direction.start_wide()
+
+    def between(e):
         if e == 1:
-            wait_all(line_ag)
-            start_all(wide_ag)
-            start_all(out_block[1])
-
-    def between(e):
+            direction.start_far()
+            start_all(out_block[0][A:])
+
+    def after_raw(e):
         if e == 0:
-            direction.start_line()
-
-    def after_backward(e):
-        if e == 0:
+            direction.start_near()
+            start_all(out_block[0][:A])
+        else:
             direction.finish(own)
-            start_all(line_ag)
-            start_all(out_block[0])
-        start_all(out_part[e])
+            start_all(far_ag)
+            start_all(out_part[0][:D])
 
     for e in range(examples):
         wait_all(in_x[e])
@@ -724,19 +743,18 @@
             lambda t: x[e, :, lane_tile(t)].astype(f32),
             8,
             block_store,
-            direction.start_wide if e == 0 else None,
+            functools.partial(early_forward, e),
         )
-        after_forward(e)
         wait_all(in_cot[e])
         backward_two(wk, lambda t: cot[e, :, lane_tile(t)].astype(f32), slot_weight(e), 8, raw.at[e])
         between(e)
         backward_one(wk, 8, raw.at[e], raw_gn.at[e], part_store)
-        after_backward(e)
         sq[...] = jnp.zeros_like(sq)
         raw_gradient(wk, raw.at[e], sq)
         gn = raw_gn[e]
         square = whole_sum(sq[...]) + whole_sum(gn * gn)
         length[e] = jnp.broadcast_to(jnp.sqrt(square), (8, LANES))
+        after_raw(e)
 
     factors = [CLIP / jnp.maximum(length[e][0:1, 0:1], CLIP) for e in range(examples)]
     total = factors[0] * raw_gn[0]
@@ -752,23 +770,33 @@
         s_conv[k] = total.astype(bf16).reshape(4, 2, chans, C)
 
     clipped.start_core()
+    clipped.start_wide()
+    wait_all(far_ag)
+    start_all(near_ag)
+    start_all(out_part[0][D:])
+    start_all(out_block[1][:E])
+    wait_all(near_ag)
+    start_all(wide_ag)
+    clipped.start_near()
+    start_all(out_block[1][E:])
+    start_all(out_part[1][:F])
+    clipped.start_far()
+    start_all(out_part[1][F:])
+    clipped.finish(red.at[w])
+    finals = []
+    for k in range(1, 4):
+        to = lax.rem(w + k, 4)
+        finals.append(peer_copy(red.at[w], red.at[w], s_fin.at[3, k - 1], r_fin.at[3, k - 1], wide=to))
+    start_all(finals)
     wait_all(wide_ag)
-    core_ag.start()
-    clipped.start_wide()
-    core_ag.wait()
+    start_all(core_ag)
+    wait_all(core_ag)
     inner_products(dt, raw, raw_gn, length, figures, me, chans)
     figs = []
     for k in range(1, n):
         to = lax.rem(me + k, n)
         figs.append(peer_copy(figures.at[me], figures.at[me], s_fig.at[k - 1], r_fig.at[k - 1], narrow=to))
     start_all(figs)
-    clipped.start_line()
-    clipped.finish(red.at[w])
-    finals = []
-    for k in range(1, 4):
-        to = lax.rem(w + k, 4)
-        finals.append(peer_copy(red.at[w], red.at[w], s_fin.at[3, k - 1], r_fin.at[3, k - 1], wide=to))
-    start_all(finals)
     wait_all(figs)
     slot = lax.broadcasted_iota(jnp.int32, (8, LANES), 1)
     table = jnp.zeros((8, LANES), f32)
@@ -799,7 +827,7 @@
         square = carry[0]
         sums = list(carry[1:])
         for tap in range(9):
-            d = dt[rest % 2, q, rest // 2, tap].astype(f32)
+            d = dt[rest % 2, q, rest // 4, (rest // 2) % 2, tap].astype(f32)
             square = square + d * d
             for e in range(examples):
                 sums[e] = sums[e] + d * raw[e, (q // 2) * 9 + tap, at, lanes]
@@ -809,7 +837,7 @@
 
     def visit_gn(rest, carry):
         at = pl.ds(pl.multiple_of(rest * chans, chans), chans)
-        d = dt[rest % 2, 0, rest // 2, 9].astype(f32)
+        d = dt[rest % 2, 0, rest // 4, (rest // 2) % 2, 9].astype(f32)
         return (carry[0] + d * d,) + tuple(carry[1 + e] + d * raw_gn[e, at, :] for e in range(examples))
 
     totals = lax.fori_loop(0, 8, visit_gn, totals)
@@ -836,17 +864,19 @@
         pltpu.VMEM((4, chans, LANES), bf16),
         pltpu.VMEM((4, 10, 4, chans, LANES), bf16),
         pltpu.VMEM((3, 10, 4, chans, LANES), bf16),
-        pltpu.VMEM((10, 4, chans, LANES), bf16),
-        pltpu.VMEM((3, 10, chans, LANES), bf16),
+        pltpu.VMEM((10, 2, 2, chans, LANES), bf16),
+        pltpu.VMEM((10, 2, chans, LANES), bf16),
+        pltpu.VMEM((10, 2, chans, LANES), bf16),
+        pltpu.VMEM((10, chans, LANES), bf16),
     ]
-    sems = [dma((2,)), dma((2,)), dma((3,)), dma((3,)), dma((3,)), dma((3,))]
+    sems = [dma((2,)), dma((2,)), dma((3,)), dma((3,)), dma((2,)), dma((2,))]
     scratch = [
         pltpu.VMEM((examples, C, AUG * PIX), bf16),
         pltpu.VMEM((examples, C, AUG * PIX), bf16),
         pltpu.VMEM((C, LANES), bf16),
         pltpu.VMEM((C, LANES), bf16),
         pltpu.VMEM((2, UNITS, chans, LANES), bf16),
-        pltpu.VMEM((2, UNITS, 4, 2, chans, LANES), bf16),
+        pltpu.VMEM((2, UNITS, 2, 2, 2, chans, LANES), bf16),
         pltpu.VMEM((examples, C, AUG * PIX), bf16),
         pltpu.VMEM((examples, C, AUG * PIX), bf16),
         pltpu.VMEM((examples, 18, C, C), f32),
@@ -859,7 +889,7 @@
         pltpu.VMEM((4, 2, chans, LANES), bf16),
         pltpu.VMEM((18, 4, 2, chans, C), bf16),
         pltpu.VMEM((4, 2, chans, LANES), bf16),
-        pltpu.VMEM((2, 4, 4, 10, chans, LANES), bf16),
+        pltpu.VMEM((2, 4, 2, 2, 10, chans, LANES), bf16),
         pltpu.VMEM((4, 10, chans, LANES), bf16),
         pltpu.VMEM((8, examples, 8, LANES), f32),
     ]
@@ -949,7 +979,7 @@
 
 def finish(total, alive, counts, steps, ob, op, cots, red, red_gn, conv, gn, norms, infl):
     held, chans = ob.shape[0], ob.shape[1]
-    grid = 4
+    grid = GRID
     rows = 18 * chans
     smem = pl.BlockSpec(memory_space=pltpu.SMEM)
     images = pl.BlockSpec((held // grid, chans, AUG * PIX), lambda i: (i, 0, 0))

time: 149 us -> 135 us (0.906)
  Pallas kernels: 146 us -> 133 us
    pallas_call x1, Pallas kernels: 141 us -> 128 us  [mega(): pl.pallas_call(mega_kernel, out_shape=(out((held, chans, AUG * PIX), bf16...]
where the time goes in v5:
time: 135 us
  Pallas kernels  133 us (99%)
  between operations  2.13 us (2%)
    pallas_call x1, Pallas kernels, mega(): pl.pallas_call(mega_kernel, out_shape=(out((held, chans, AUG * PIX), bf16...  128 us
    pallas_call x1, Pallas kernels, finish(): pl.pallas_call(functools.partial(tail_kernel, total), grid=(grid,), out_s...  4.87 us

profile of v5, /device:TPU:0, one launch (start us, length us, event | category | flops | bytes accessed | tf_op | source)
XLA Modules:
  0.0 135.0 jit_solution(5770165125902022384)
XLA Ops:
  1.9 128.0 %shard_map.239 = (bf16[16,32,1024]{2,1,0:T(8,128)(2,1)}, bf16[16,32,1024]{2,1,0:T(8,128)(2,1)}, bf16[18,32,256]{2,1,0:T(8,128)(2,1)}, bf16[32,128]{1,0:T(8,128)(2,1)}, f32[1,16]{1,0:T(1,128)}, /*index=5*/f32[1,16]{1,0:T(1,128)}) custom-call(bf16[16,32,1024]{2,1,0:T(8,128)(2,1)} %images.1, bf16[16,32,1024]{2,1,0:T(8,128)(2,1)} %cots.3, ...), custom_call_target="tpu_custom_call" | custom-call | tf_op jit(solution)/shard_map/pallas_call | solution.py:914
  129.9 4.9 %shard_map.240 = (bf16[16,32,1024]{2,1,0:T(8,128)(2,1)}, f32[16,32,1024]{2,1,0:T(8,128)}, f32[576,256]{1,0:T(8,128)}, bf16[576,256]{1,0:T(8,128)(2,1)}, f32[576,...) custom-call(s32[1]{0:T(128)S(6)} %copy.27.alive, ...), custom_call_target="tpu_custom_call" | custom-call | tf_op jit(solution)/shard_map/pallas_call | solution.py:995

commit v6 on v5

--- a/solution.py
+++ b/solution.py
@@ -422,7 +422,8 @@
 B = 8
 D = 5
 E = 6
-F = 2
+F = 1
+G = 8
 
 
 class Exchange:
@@ -781,7 +782,7 @@
     start_all(out_block[1][E:])
     start_all(out_part[1][:F])
     clipped.start_far()
-    start_all(out_part[1][F:])
+    start_all(out_part[1][F:G])
     clipped.finish(red.at[w])
     finals = []
     for k in range(1, 4):
@@ -797,6 +798,7 @@
         to = lax.rem(me + k, n)
         figs.append(peer_copy(figures.at[me], figures.at[me], s_fig.at[k - 1], r_fig.at[k - 1], narrow=to))
     start_all(figs)
+    start_all(out_part[1][G:])
     wait_all(figs)
     slot = lax.broadcasted_iota(jnp.int32, (8, LANES), 1)
     table = jnp.zeros((8, LANES), f32)
@@ -833,7 +835,7 @@
                 sums[e] = sums[e] + d * raw[e, (q // 2) * 9 + tap, at, lanes]
         return (square, *sums)
 
-    totals = lax.fori_loop(0, 32, visit, (zero,) * (examples + 1))
+    totals = lax.fori_loop(0, 32, visit, (zero,) * (examples + 1), unroll=4)
 
     def visit_gn(rest, carry):
         at = pl.ds(pl.multiple_of(rest * chans, chans), chans)

time: 135 us -> 134 us (level)
  no operation moved by 1% of the time
where the time goes in v6:
time: 134 us
  Pallas kernels  132 us (99%)
  between operations  2.13 us (2%)
    pallas_call x1, Pallas kernels, mega(): pl.pallas_call(mega_kernel, out_shape=(out((held, chans, AUG * PIX), bf16...  127 us
    pallas_call x1, Pallas kernels, finish(): pl.pallas_call(functools.partial(tail_kernel, total), grid=(grid,), out_s...  4.87 us

profile of v6, /device:TPU:0, one launch (start us, length us, event | category | flops | bytes accessed | tf_op | source)
XLA Modules:
  0.0 133.9 jit_solution(9377833764035498653)
XLA Ops:
  1.9 126.9 %shard_map.239 = (bf16[16,32,1024]{2,1,0:T(8,128)(2,1)}, bf16[16,32,1024]{2,1,0:T(8,128)(2,1)}, bf16[18,32,256]{2,1,0:T(8,128)(2,1)}, bf16[32,128]{1,0:T(8,128)(2,1)}, f32[1,16]{1,0:T(1,128)}, /*index=5*/f32[1,16]{1,0:T(1,128)}) custom-call(bf16[16,32,1024]{2,1,0:T(8,128)(2,1)} %images.1, bf16[16,32,1024]{2,1,0:T(8,128)(2,1)} %cots.3, ...), custom_call_target="tpu_custom_call" | custom-call | tf_op jit(solution)/shard_map/pallas_call | solution.py:916
  128.8 4.9 %shard_map.240 = (bf16[16,32,1024]{2,1,0:T(8,128)(2,1)}, f32[16,32,1024]{2,1,0:T(8,128)}, f32[576,256]{1,0:T(8,128)}, bf16[576,256]{1,0:T(8,128)(2,1)}, f32[576,...) custom-call(s32[1]{0:T(128)S(6)} %copy.27.alive, ...), custom_call_target="tpu_custom_call" | custom-call | tf_op jit(solution)/shard_map/pallas_call | solution.py:997

commit v7 on v6

--- a/solution.py
+++ b/solution.py
@@ -238,7 +238,7 @@
 def raw_gradient(wk, grads, sq):
     rows = 32
 
-    @pl.loop(0, C // rows)
+    @pl.loop(0, C // rows, unroll=2)
     def _(j):
         at = pl.ds(pl.multiple_of(j * rows, rows), rows)
         for conv in range(2):

time: 134 us -> 134 us (level)
  no operation moved by 1% of the time
where the time goes in v7:
time: 134 us
  Pallas kernels  132 us (99%)
  between operations  2.15 us (2%)
    pallas_call x1, Pallas kernels, mega(): pl.pallas_call(mega_kernel, out_shape=(out((held, chans, AUG * PIX), bf16...  127 us
    pallas_call x1, Pallas kernels, finish(): pl.pallas_call(functools.partial(tail_kernel, total), grid=(grid,), out_s...  4.87 us

profile of v7, /device:TPU:0, one launch (start us, length us, event | category | flops | bytes accessed | tf_op | source)
XLA Modules:
  0.0 133.7 jit_solution(14875867391305794890)
XLA Ops:
  1.9 126.7 %shard_map.239 = (bf16[16,32,1024]{2,1,0:T(8,128)(2,1)}, bf16[16,32,1024]{2,1,0:T(8,128)(2,1)}, bf16[18,32,256]{2,1,0:T(8,128)(2,1)}, bf16[32,128]{1,0:T(8,128)(2,1)}, f32[1,16]{1,0:T(1,128)}, /*index=5*/f32[1,16]{1,0:T(1,128)}) custom-call(bf16[16,32,1024]{2,1,0:T(8,128)(2,1)} %images.1, bf16[16,32,1024]{2,1,0:T(8,128)(2,1)} %cots.3, ...), custom_call_target="tpu_custom_call" | custom-call | tf_op jit(solution)/shard_map/pallas_call | solution.py:916
  128.6 4.9 %shard_map.240 = (bf16[16,32,1024]{2,1,0:T(8,128)(2,1)}, f32[16,32,1024]{2,1,0:T(8,128)}, f32[576,256]{1,0:T(8,128)}, bf16[576,256]{1,0:T(8,128)(2,1)}, f32[576,...) custom-call(s32[1]{0:T(128)S(6)} %copy.27.alive, ...), custom_call_target="tpu_custom_call" | custom-call | tf_op jit(solution)/shard_map/pallas_call | solution.py:997
